TPU v7x, 32 devices: a whole 2x2x4 slice. The times are simulated.
32 devices in a mesh: wide: 8 (over z, y), narrow: 4 (over x, core).
Axes of the slice: x: 2, y: 2, z: 4, core: 2. Of those that a mesh axis runs over, the one named last changes fastest.
Arguments:
- tokens: bfloat16 [8, 1024, 2048], P('wide', 'narrow'), may hold values from -6 to 6
- cotangent: bfloat16 [8, 1024, 2048], P('wide', 'narrow'), may hold values from -6 to 6
- lengths: int32 [8], P('wide'), may hold values from 256 to 1024, as said below
- norm_gains: float32 [4352], replicated, may hold values from 0.6 to 1.6
- gains_first: float32 [4352], replicated
- gains_second: float32 [4352], replicated, as said below
- query_weight: float32 [2048, 2048], P('wide', 'narrow'), may hold values from -0.125 to 0.125
- query_first: float32 [2048, 2048], P('wide', 'narrow')
- query_second: float32 [2048, 2048], P('wide', 'narrow'), as said below
- keyval_weight: float32 [2, 2048, 1024], P(None, 'wide', 'narrow'), may hold values from -0.125 to 0.125
- keyval_first: float32 [2, 2048, 1024], P(None, 'wide', 'narrow')
- keyval_second: float32 [2, 2048, 1024], P(None, 'wide', 'narrow'), as said below
- output_weight: float32 [2048, 2048], P('narrow', 'wide'), may hold values from -0.5 to 0.5
- output_first: float32 [2048, 2048], P('narrow', 'wide')
- output_second: float32 [2048, 2048], P('narrow', 'wide'), as said below
- gateup_weight: float32 [2, 2048, 6144], P(None, 'wide', 'narrow'), may hold values from -0.125 to 0.125
- gateup_first: float32 [2, 2048, 6144], P(None, 'wide', 'narrow')
- gateup_second: float32 [2, 2048, 6144], P(None, 'wide', 'narrow'), as said below
- down_weight: float32 [6144, 2048], P('narrow', 'wide'), may hold values from -0.078125 to 0.078125
- down_first: float32 [6144, 2048], P('narrow', 'wide')
- down_second: float32 [6144, 2048], P('narrow', 'wide'), as said below
Outputs:
- result: bfloat16 [8, 1024, 2048], P('wide', 'narrow')
- input_grad: bfloat16 [8, 1024, 2048], P('wide', 'narrow')
- rms_values: float32 [3, 8, 1024], P(None, 'wide', 'narrow')
- new_gains: float32 [4352], replicated
- new_gains_first: float32 [4352], replicated
- new_gains_second: float32 [4352], replicated
- new_query: float32 [2048, 2048], P('wide', 'narrow')
- new_query_first: float32 [2048, 2048], P('wide', 'narrow')
- new_query_second: float32 [2048, 2048], P('wide', 'narrow')
- new_keyval: float32 [2, 2048, 1024], P(None, 'wide', 'narrow')
- new_keyval_first: float32 [2, 2048, 1024], P(None, 'wide', 'narrow')
- new_keyval_second: float32 [2, 2048, 1024], P(None, 'wide', 'narrow')
- new_output: float32 [2048, 2048], P('narrow', 'wide')
- new_output_first: float32 [2048, 2048], P('narrow', 'wide')
- new_output_second: float32 [2048, 2048], P('narrow', 'wide')
- new_gateup: float32 [2, 2048, 6144], P(None, 'wide', 'narrow')
- new_gateup_first: float32 [2, 2048, 6144], P(None, 'wide', 'narrow')
- new_gateup_second: float32 [2, 2048, 6144], P(None, 'wide', 'narrow')
- new_down: float32 [6144, 2048], P('narrow', 'wide')
- new_down_first: float32 [6144, 2048], P('narrow', 'wide')
- new_down_second: float32 [6144, 2048], P('narrow', 'wide')
- lamb_stats: float32 [2, 11], replicated
- trust_ratios: float32 [11], replicated
Inputs may be any that keep to these rules, and one draw needn't show every extreme that they name: `lengths`: some sequence has all 1024 positions valid and some exactly 256. `gains_second`: positive. `query_second`: positive. `keyval_second`: positive. `output_second`: positive. `gateup_second`: positive. `down_second`: positive.
All inputs are finite; a program needn't handle non-finite values.
Results may differ from a plain program's by a relative error of at most 0.024.
Values may be sent and summed in bfloat16 or wider, within the bound.
No kernel may reach another device: no remote copies, remote signals or barrier semaphores. Data moves between devices by JAX's collectives and lax.ppermute only.
A program may use at most 192 MiB of HBM per device.

v0:
```python
import jax
import jax.numpy as jnp
from jax import lax
from jax.sharding import PartitionSpec as P

D = 2048
H = 16
KV = 8
HD = 128
STEP = 10


EPS = 1e-06
THETA = 1000000.0
BETA_ONE = 0.9
BETA_TWO = 0.999
ADAM_EPS = 1e-06
DECAY = 0.01
LEARN = 0.5


def overall(items):
    return lax.psum((items[0], items[1]), ("wide", "narrow"))


def rope_tables(length):
    places = jnp.arange(length, dtype=jnp.float32)
    frequency = THETA ** (-jnp.arange(HD // 2, dtype=jnp.float32) * 2.0 / HD)
    angles = places[:, None] * frequency[None, :]
    return (jnp.cos(angles)[:, None, :], jnp.sin(angles)[:, None, :])


def rotate(values, cos_table, sin_table):
    halfway = HD // 2
    former = values[..., :halfway]
    latter = values[..., halfway:]
    return jnp.concatenate(
        [former * cos_table - latter * sin_table, latter * cos_table + former * sin_table], -1
    )


def unrotate(gradient, cos_table, sin_table):
    halfway = HD // 2
    former = gradient[..., :halfway]
    latter = gradient[..., halfway:]
    return jnp.concatenate(
        [former * cos_table + latter * sin_table, latter * cos_table - former * sin_table], -1
    )


def head_norm(raw_values, head_count):
    shaped = raw_values.reshape(raw_values.shape[:-1] + (head_count, HD))
    inverse = lax.rsqrt(jnp.mean(shaped * shaped, -1, keepdims=True) + EPS)
    return (shaped * inverse, inverse)


def head_norm_back(scaled_grad, unit_values, inverse, gain_vector):
    gain_grad = jnp.sum(scaled_grad * unit_values, axis=(0, 1, 2))
    unit_grad = scaled_grad * gain_vector
    raw_grad = inverse * (
        unit_grad - unit_values * jnp.mean(unit_grad * unit_values, -1, keepdims=True)
    )
    return (raw_grad, gain_grad)


def norm_back(normed_grad, hat_values, inverse, gain_vector):
    gain_grad = jnp.sum(normed_grad * hat_values, axis=(0, 1))
    scaled = normed_grad * gain_vector
    return (
        inverse * (scaled - hat_values * jnp.mean(scaled * hat_values, -1, keepdims=True)),
        gain_grad,
    )


def attend_forward(queries, keys, values, valid_len):
    length = queries.shape[0]
    block_rows = min(512, length)
    block_count = length // block_rows
    score_scale = HD ** (-0.5)
    key_places = jnp.arange(length, dtype=jnp.int32)

    def one_block(start):
        query_block = lax.dynamic_slice_in_dim(queries, start, block_rows, 0)
        scores = (
            jnp.einsum("qgrd,kgd->grqk", query_block, keys, preferred_element_type=jnp.float32)
            * score_scale
        )
        query_places = start + jnp.arange(block_rows, dtype=jnp.int32)
        allowed = (key_places[None, :] <= query_places[:, None]) & (key_places[None, :] < valid_len)
        scores = jnp.where(allowed, scores, -1e30)
        row_max = jnp.max(scores, -1, keepdims=True)
        weights = jnp.exp(scores - row_max)
        row_sum = jnp.sum(weights, -1, keepdims=True)
        probability = (weights / row_sum).astype(jnp.bfloat16)
        context = jnp.einsum(
            "grqk,kgd->qgrd", probability, values, preferred_element_type=jnp.float32
        )
        return (context.astype(jnp.bfloat16), row_max + jnp.log(row_sum))

    starts = jnp.arange(block_count, dtype=jnp.int32) * block_rows
    context, log_norm = lax.map(one_block, starts)
    return (context.reshape(length, -1), log_norm)


def attend_backward(queries, keys, values, valid_len, log_norm, context_grad):
    length = queries.shape[0]
    block_rows = min(512, length)
    block_count = length // block_rows
    score_scale = HD ** (-0.5)
    key_places = jnp.arange(length, dtype=jnp.int32)
    starts = jnp.arange(block_count, dtype=jnp.int32) * block_rows

    def one_block(carried, inputs):
        key_grad, value_grad = carried
        start, norm_block = inputs
        query_block = lax.dynamic_slice_in_dim(queries, start, block_rows, 0)
        grad_block = lax.dynamic_slice_in_dim(context_grad, start, block_rows, 0)
        scores = (
            jnp.einsum("qgrd,kgd->grqk", query_block, keys, preferred_element_type=jnp.float32)
            * score_scale
        )
        query_places = start + jnp.arange(block_rows, dtype=jnp.int32)
        allowed = (key_places[None, :] <= query_places[:, None]) & (key_places[None, :] < valid_len)
        probability = jnp.where(allowed, jnp.exp(scores - norm_block), 0.0)
        value_grad = value_grad + jnp.einsum(
            "grqk,qgrd->kgd",
            probability.astype(jnp.bfloat16),
            grad_block,
            preferred_element_type=jnp.float32,
        )
        prob_grad = jnp.einsum(
            "qgrd,kgd->grqk", grad_block, values, preferred_element_type=jnp.float32
        )
        row_inner = jnp.sum(probability * prob_grad, -1, keepdims=True)
        score_grad = (probability * (prob_grad - row_inner)).astype(jnp.bfloat16)
        query_grad = (
            jnp.einsum("grqk,kgd->qgrd", score_grad, keys, preferred_element_type=jnp.float32)
            * score_scale
        )
        key_grad = (
            key_grad
            + jnp.einsum(
                "grqk,qgrd->kgd", score_grad, query_block, preferred_element_type=jnp.float32
            )
            * score_scale
        )
        return ((key_grad, value_grad), query_grad)

    zero_grad = jnp.zeros(keys.shape, jnp.float32)
    (key_grad, value_grad), query_grad = lax.scan(
        one_block, (zero_grad, zero_grad), (starts, log_norm)
    )
    return (query_grad.reshape(queries.shape), key_grad, value_grad)


def adam_step(gradient, moment_one, moment_two, master):
    new_one = BETA_ONE * moment_one + (1.0 - BETA_ONE) * gradient
    new_two = BETA_TWO * moment_two + (1.0 - BETA_TWO) * gradient * gradient
    update = (
        new_one / (1.0 - BETA_ONE**STEP) / (jnp.sqrt(new_two / (1.0 - BETA_TWO**STEP)) + ADAM_EPS)
        + DECAY * master
    )
    return (new_one, new_two, update)


def square(values):
    return jnp.sum(values * values)


def root_mean(values):
    return jnp.sqrt(jnp.mean(values * values, -1))


def shards(
    tokens,
    cotangent,
    lengths,
    norm_gains,
    gains_first,
    gains_second,
    query_weight,
    query_first,
    query_second,
    keyval_weight,
    keyval_first,
    keyval_second,
    output_weight,
    output_first,
    output_second,
    gateup_weight,
    gateup_first,
    gateup_second,
    down_weight,
    down_first,
    down_second,
):
    batch_size, shard_len = (tokens.shape[0], tokens.shape[1])
    narrow_size = lax.axis_size("narrow")
    seq_len = shard_len * narrow_size
    local_heads = H // narrow_size
    local_groups = KV // narrow_size
    repeat = H // KV
    gain_one = norm_gains[:D]
    gain_two = norm_gains[D : 2 * D]
    gain_query = norm_gains[2 * D : 2 * D + HD]
    gain_key = norm_gains[2 * D + HD :]
    cos_table, sin_table = rope_tables(seq_len)
    full_query, full_keyval, full_output, full_gateup, full_down = (
        lax.all_gather(query_weight.astype(jnp.bfloat16), "wide", axis=0, tiled=True),
        lax.all_gather(keyval_weight.astype(jnp.bfloat16), "wide", axis=1, tiled=True),
        lax.all_gather(output_weight.astype(jnp.bfloat16), "wide", axis=1, tiled=True),
        lax.all_gather(gateup_weight.astype(jnp.bfloat16), "wide", axis=1, tiled=True),
        lax.all_gather(down_weight.astype(jnp.bfloat16), "wide", axis=1, tiled=True),
    )
    residual = tokens.astype(jnp.float32)
    inv_one = lax.rsqrt(jnp.mean(residual * residual, -1, keepdims=True) + EPS)
    hat_one = residual * inv_one
    whole_one = lax.all_gather(
        (hat_one * gain_one).astype(jnp.bfloat16), "narrow", axis=1, tiled=True
    )
    query_raw = jnp.einsum("bsd,dc->bsc", whole_one, full_query, preferred_element_type=jnp.float32)
    keyval_raw = jnp.einsum(
        "bsd,tdc->tbsc", whole_one, full_keyval, preferred_element_type=jnp.float32
    )
    query_unit, query_inv = head_norm(query_raw, local_heads)
    key_unit, key_inv = head_norm(keyval_raw[0], local_groups)
    query_rot = rotate(query_unit * gain_query, cos_table, sin_table).astype(jnp.bfloat16)
    key_rot = rotate(key_unit * gain_key, cos_table, sin_table).astype(jnp.bfloat16)
    value_low = keyval_raw[1].astype(jnp.bfloat16).reshape(batch_size, seq_len, local_groups, HD)
    query_heads = query_rot.reshape(batch_size, seq_len, local_groups, repeat, HD)
    context, log_norm = lax.map(
        lambda inputs: attend_forward(inputs[0], inputs[1], inputs[2], inputs[3]),
        (query_heads, key_rot, value_low, lengths),
    )
    attn_part = lax.psum_scatter(
        jnp.einsum("bsc,cd->bsd", context, full_output, preferred_element_type=jnp.float32).astype(
            jnp.bfloat16
        ),
        "narrow",
        scatter_dimension=1,
        tiled=True,
    ).astype(jnp.float32)
    middle = residual + attn_part
    inv_two = lax.rsqrt(jnp.mean(middle * middle, -1, keepdims=True) + EPS)
    hat_two = middle * inv_two
    whole_two = lax.all_gather(
        (hat_two * gain_two).astype(jnp.bfloat16), "narrow", axis=1, tiled=True
    )
    gateup = jnp.einsum("bsd,tdf->tbsf", whole_two, full_gateup, preferred_element_type=jnp.float32)
    gate_val = gateup[0]
    up_val = gateup[1]
    sigmoid = jax.nn.sigmoid(gate_val)
    swish = gate_val * sigmoid
    hidden = (swish * up_val).astype(jnp.bfloat16)
    mlp_part = lax.psum_scatter(
        jnp.einsum("bsf,fd->bsd", hidden, full_down, preferred_element_type=jnp.float32).astype(
            jnp.bfloat16
        ),
        "narrow",
        scatter_dimension=1,
        tiled=True,
    ).astype(jnp.float32)
    final = middle + mlp_part
    result = final.astype(jnp.bfloat16)
    rms_values = jnp.stack([root_mean(attn_part), root_mean(mlp_part), root_mean(final)])
    places = lax.axis_index("narrow") * shard_len + jnp.arange(shard_len, dtype=jnp.int32)
    valid = (places[None, :] < lengths[:, None]).astype(jnp.float32)
    grad_out = cotangent.astype(jnp.float32) * valid[:, :, None]
    whole_grad = lax.all_gather(grad_out.astype(jnp.bfloat16), "narrow", axis=1, tiled=True)
    down_grad = jnp.einsum("bsf,bsd->fd", hidden, whole_grad, preferred_element_type=jnp.float32)
    hidden_grad = jnp.einsum(
        "bsd,fd->bsf", whole_grad, full_down, preferred_element_type=jnp.float32
    )
    slope = sigmoid * (1.0 + gate_val * (1.0 - sigmoid))
    pair_grad = jnp.stack([hidden_grad * up_val * slope, hidden_grad * swish]).astype(jnp.bfloat16)
    gateup_grad = jnp.einsum(
        "bsd,tbsf->tdf", whole_two, pair_grad, preferred_element_type=jnp.float32
    )
    normed_two = lax.psum_scatter(
        jnp.einsum(
            "tbsf,tdf->bsd", pair_grad, full_gateup, preferred_element_type=jnp.float32
        ).astype(jnp.bfloat16),
        "narrow",
        scatter_dimension=1,
        tiled=True,
    ).astype(jnp.float32)
    middle_norm, gain_two_grad = norm_back(normed_two, hat_two, inv_two, gain_two)
    middle_grad = grad_out + middle_norm
    whole_mid = lax.all_gather(middle_grad.astype(jnp.bfloat16), "narrow", axis=1, tiled=True)
    output_grad = jnp.einsum("bsc,bsd->cd", context, whole_mid, preferred_element_type=jnp.float32)
    context_grad = jnp.einsum(
        "bsd,cd->bsc", whole_mid, full_output, preferred_element_type=jnp.float32
    ).astype(jnp.bfloat16)
    context_grad = context_grad.reshape(batch_size, seq_len, local_groups, repeat, HD)
    query_grad, key_grad, value_grad = lax.map(
        lambda inputs: attend_backward(
            inputs[0], inputs[1], inputs[2], inputs[3], inputs[4], inputs[5]
        ),
        (query_heads, key_rot, value_low, lengths, log_norm, context_grad),
    )
    query_scaled = unrotate(
        query_grad.reshape(batch_size, seq_len, local_heads, HD), cos_table, sin_table
    )
    key_scaled = unrotate(key_grad, cos_table, sin_table)
    query_back, gain_query_grad = head_norm_back(query_scaled, query_unit, query_inv, gain_query)
    key_back, gain_key_grad = head_norm_back(key_scaled, key_unit, key_inv, gain_key)
    query_low = query_back.reshape(batch_size, seq_len, local_heads * HD).astype(jnp.bfloat16)
    keyval_low = jnp.stack(
        [
            key_back.reshape(batch_size, seq_len, local_groups * HD),
            value_grad.reshape(batch_size, seq_len, local_groups * HD),
        ]
    ).astype(jnp.bfloat16)
    query_wgrad = jnp.einsum(
        "bsd,bsc->dc", whole_one, query_low, preferred_element_type=jnp.float32
    )
    keyval_wgrad = jnp.einsum(
        "bsd,tbsc->tdc", whole_one, keyval_low, preferred_element_type=jnp.float32
    )
    normed_one = lax.psum_scatter(
        (
            jnp.einsum("bsc,dc->bsd", query_low, full_query, preferred_element_type=jnp.float32)
            + jnp.einsum(
                "tbsc,tdc->bsd", keyval_low, full_keyval, preferred_element_type=jnp.float32
            )
        ).astype(jnp.bfloat16),
        "narrow",
        scatter_dimension=1,
        tiled=True,
    ).astype(jnp.float32)
    input_norm, gain_one_grad = norm_back(normed_one, hat_one, inv_one, gain_one)
    input_grad = (middle_grad + input_norm).astype(jnp.bfloat16)
    gain_part = jnp.concatenate([gain_one_grad, gain_two_grad, gain_query_grad, gain_key_grad])
    query_sum, keyval_sum, output_sum, gateup_sum, down_sum = (
        lax.psum_scatter(
            query_wgrad.astype(jnp.bfloat16), "wide", scatter_dimension=0, tiled=True
        ).astype(jnp.float32),
        lax.psum_scatter(
            keyval_wgrad.astype(jnp.bfloat16), "wide", scatter_dimension=1, tiled=True
        ).astype(jnp.float32),
        lax.psum_scatter(
            output_grad.astype(jnp.bfloat16), "wide", scatter_dimension=1, tiled=True
        ).astype(jnp.float32),
        lax.psum_scatter(
            gateup_grad.astype(jnp.bfloat16), "wide", scatter_dimension=1, tiled=True
        ).astype(jnp.float32),
        lax.psum_scatter(
            down_grad.astype(jnp.bfloat16), "wide", scatter_dimension=1, tiled=True
        ).astype(jnp.float32),
    )
    new_query_first, new_query_second, query_update = adam_step(
        query_sum, query_first, query_second, query_weight
    )
    new_keyval_first, new_keyval_second, keyval_update = adam_step(
        keyval_sum, keyval_first, keyval_second, keyval_weight
    )
    new_output_first, new_output_second, output_update = adam_step(
        output_sum, output_first, output_second, output_weight
    )
    new_gateup_first, new_gateup_second, gateup_update = adam_step(
        gateup_sum, gateup_first, gateup_second, gateup_weight
    )
    new_down_first, new_down_second, down_update = adam_step(
        down_sum, down_first, down_second, down_weight
    )
    squares = jnp.stack(
        [
            square(query_weight),
            square(keyval_weight[0]),
            square(keyval_weight[1]),
            square(output_weight),
            square(gateup_weight[0]),
            square(gateup_weight[1]),
            square(down_weight),
            square(query_update),
            square(keyval_update[0]),
            square(keyval_update[1]),
            square(output_update),
            square(gateup_update[0]),
            square(gateup_update[1]),
            square(down_update),
        ]
    )
    gain_total, square_total = overall((gain_part, squares))
    matrix_norms = jnp.sqrt(square_total)
    matrix_weight = matrix_norms[:7]
    matrix_update = matrix_norms[7:]
    new_gains_first, new_gains_second, gains_update = adam_step(
        gain_total, gains_first, gains_second, norm_gains
    )
    segments = ((0, D), (2 * D, 2 * D + HD), (2 * D + HD, 2 * D + 2 * HD), (D, 2 * D))
    gain_weight = [jnp.sqrt(square(norm_gains[lower:upper])) for lower, upper in segments]
    gain_update = [jnp.sqrt(square(gains_update[lower:upper])) for lower, upper in segments]
    weight_norms = jnp.stack(
        [
            gain_weight[0],
            matrix_weight[0],
            matrix_weight[1],
            matrix_weight[2],
            gain_weight[1],
            gain_weight[2],
            matrix_weight[3],
            gain_weight[3],
            matrix_weight[4],
            matrix_weight[5],
            matrix_weight[6],
        ]
    )
    update_norms = jnp.stack(
        [
            gain_update[0],
            matrix_update[0],
            matrix_update[1],
            matrix_update[2],
            gain_update[1],
            gain_update[2],
            matrix_update[3],
            gain_update[3],
            matrix_update[4],
            matrix_update[5],
            matrix_update[6],
        ]
    )
    trust = weight_norms / update_norms
    gain_trust = jnp.concatenate(
        [
            jnp.full((D,), 1.0, jnp.float32) * trust[0],
            jnp.full((D,), 1.0, jnp.float32) * trust[7],
            jnp.full((HD,), 1.0, jnp.float32) * trust[4],
            jnp.full((HD,), 1.0, jnp.float32) * trust[5],
        ]
    )
    new_gains = norm_gains - LEARN * gain_trust * gains_update
    new_query = query_weight - LEARN * trust[1] * query_update
    new_keyval = (
        keyval_weight - LEARN * jnp.stack([trust[2], trust[3]])[:, None, None] * keyval_update
    )
    new_output = output_weight - LEARN * trust[6] * output_update
    new_gateup = (
        gateup_weight - LEARN * jnp.stack([trust[8], trust[9]])[:, None, None] * gateup_update
    )
    new_down = down_weight - LEARN * trust[10] * down_update
    lamb_stats = jnp.stack([weight_norms, update_norms])
    return (
        result,
        input_grad,
        rms_values,
        new_gains,
        new_gains_first,
        new_gains_second,
        new_query,
        new_query_first,
        new_query_second,
        new_keyval,
        new_keyval_first,
        new_keyval_second,
        new_output,
        new_output_first,
        new_output_second,
        new_gateup,
        new_gateup_first,
        new_gateup_second,
        new_down,
        new_down_first,
        new_down_second,
        lamb_stats,
        trust,
    )


def solution(mesh):
    in_specs = (
        P("wide", "narrow", None),
        P("wide", "narrow", None),
        P("wide"),
        P(),
        P(),
        P(),
        P("wide", "narrow"),
        P("wide", "narrow"),
        P("wide", "narrow"),
        P(None, "wide", "narrow"),
        P(None, "wide", "narrow"),
        P(None, "wide", "narrow"),
        P("narrow", "wide"),
        P("narrow", "wide"),
        P("narrow", "wide"),
        P(None, "wide", "narrow"),
        P(None, "wide", "narrow"),
        P(None, "wide", "narrow"),
        P("narrow", "wide"),
        P("narrow", "wide"),
        P("narrow", "wide"),
    )
    out_specs = (
        P("wide", "narrow", None),
        P("wide", "narrow", None),
        P(None, "wide", "narrow"),
        P(),
        P(),
        P(),
        P("wide", "narrow"),
        P("wide", "narrow"),
        P("wide", "narrow"),
        P(None, "wide", "narrow"),
        P(None, "wide", "narrow"),
        P(None, "wide", "narrow"),
        P("narrow", "wide"),
        P("narrow", "wide"),
        P("narrow", "wide"),
        P(None, "wide", "narrow"),
        P(None, "wide", "narrow"),
        P(None, "wide", "narrow"),
        P("narrow", "wide"),
        P("narrow", "wide"),
        P("narrow", "wide"),
        P(),
        P(),
    )
    return jax.shard_map(shards, mesh=mesh, in_specs=in_specs, out_specs=out_specs, check_vma=False)
```

profile of v0, /device:TPU:0, one launch (start us, length us, event | category | flops | bytes accessed | tf_op | source)
XLA Modules:
  0.0 1548.0 jit_solution(10490052216814497383)
XLA Ops:
  18.5 44.3 %all-gather.12.cloned.1.call-done = bf16[2048,512]{1,0:T(8,128)(2,1)} async-done(((bf16[256,512]{1,0:T(8,128)(2,1)}), bf16[2048,512]{1,0:T(8,128)(2,1)}) %all-gather.12.cloned.1.call-update) | async-done | bytes 2097168 | tf_op jit(solution)/shard_map/all_gather | solution.py:209
  62.8 35.1 %all-gather.10.cloned.1.call-done = bf16[1,1024,2048]{2,1,0:T(8,128)(2,1)} async-done(((bf16[1,256,2048]{2,1,0:T(8,128)(2,1)}), bf16[1,1024,2048]{2,1,0:T(8,128)(2,1)}) %all-gather.10.cloned.1.call-update) | async-done | bytes 4194320 | tf_op jit(solution)/shard_map/all_gather | solution.py:218
  109.4 42.2 %all-gather.14.cloned.1.call-done = bf16[2,2048,256]{1,2,0:T(8,128)(2,1)} async-done(((bf16[2,256,256]{1,2,0:T(8,128)(2,1)}), bf16[2,2048,256]{1,2,0:T(8,128)(2,1)}) %all-gather.14.cloned.1.call-update) | async-done | bytes 2097168 | tf_op jit(solution)/shard_map/all_gather | solution.py:210
  167.7 27.1 %while.50 = (s32[]{:T(128)}, bf16[2,512,2,2,128]{4,3,2,1,0:T(2,128)(2,1)}, f32[2,2,2,512,1]{3,2,1,4,0:T(2,128)S(1)}, s32[2]{0:T(128)S(1)}, s32[]{:T(128)}, /*ind...) while((s32[]{:T(128)}, ...), condition=%wide.region_6.7_spmd.clone.clone, body=%wide.region_3.6_spmd.clone.clone.sunk | while | flops 1100217856 | bytes 40966412 | solution.py:101
  209.7 42.8 %reduce-scatter.10.cloned.1.call-done = bf16[1,256,2048]{2,1,0:T(8,128)(2,1)} async-done(((bf16[1,1024,2048]{2,1,0:T(8,128)(2,1)}), bf16[1,256,2048]{2,1,0:T(8,128)(2,1)}) %reduce-scatter.10.cloned.1.call-update) | async-done | bytes 1048592 | tf_op jit(solution)/shard_map/reduce_scatter | solution.py:235
  262.2 28.1 %all-gather.18.cloned.1.call-done = bf16[1,1024,2048]{2,1,0:T(8,128)(2,1)} async-done(((bf16[1,256,2048]{2,1,0:T(8,128)(2,1)}), bf16[1,1024,2048]{2,1,0:T(8,128)(2,1)}) %all-gather.18.cloned.1.call-update) | async-done | bytes 4194320 | tf_op jit(solution)/shard_map/all_gather | solution.py:246
  290.4 179.5 %all-gather.20.cloned.1.call-done = bf16[2,2048,1536]{2,1,0:T(8,128)(2,1)} async-done(((bf16[2,256,1536]{2,1,0:T(8,128)(2,1)}), bf16[2,2048,1536]{2,1,0:T(8,128)(2,1)}) %all-gather.20.cloned.1.call-update) | async-done | bytes 12582928 | tf_op jit(solution)/shard_map/all_gather | solution.py:212
  469.8 19.2 %convolution_bitcast_fusion.1 = f32[2,1,1024,1536]{3,2,0,1:T(8,128)} fusion(bf16[2,2048,1536]{2,1,0:T(8,128)(2,1)} %all-gather.20.cloned.1.call-done, bf16[1,1024,2048]{2,1,0:T(8,128)(2,1)} %all-gather.18.cloned.1.call-done), kind=kOutput, calls=%fused_computation.69 | convolution fusion | flops 12884901888 | bytes 29360128 | tf_op jit(solution)/shard_map/bsd,tdf->tbsf/dot_general | solution.py:249
  489.0 15.8 %all-gather.24.cloned.1.call-done = bf16[1,1024,2048]{2,1,0:T(8,128)(2,1)} async-done(((bf16[1,256,2048]{2,1,0:T(8,128)(2,1)}), bf16[1,1024,2048]{2,1,0:T(8,128)(2,1)}) %all-gather.24.cloned.1.call-update) | async-done | bytes 4194320 | tf_op jit(solution)/shard_map/all_gather | solution.py:269
  517.7 118.5 %reduce-scatter.26.cloned.1.call-done = bf16[1536,256]{1,0:T(8,128)(2,1)} async-done(((bf16[1536,2048]{1,0:T(8,128)(2,1)}), bf16[1536,256]{1,0:T(8,128)(2,1)}) %reduce-scatter.26.cloned.1.call-update) | async-done | bytes 786448 | tf_op jit(solution)/shard_map/reduce_scatter | solution.py:347
  642.8 99.2 %all-gather.22.cloned.1.call-done = bf16[1536,2048]{1,0:T(8,128)(2,1)} async-done(((bf16[1536,256]{1,0:T(8,128)(2,1)}), bf16[1536,2048]{1,0:T(8,128)(2,1)}) %all-gather.22.cloned.1.call-update) | async-done | bytes 6291472 | tf_op jit(solution)/shard_map/all_gather | solution.py:213
  742.0 14.9 fusion.90
  759.6 17.7 %fusion.80 = bf16[1,1024,2048]{2,1,0:T(8,128)(2,1)} fusion(bf16[2,2048,1536]{2,1,0:T(8,128)(2,1)} %all-gather.20.cloned.1.call-done, bf16[1,1024,1536]{2,1,0:T(8,128)(2,1)S(1)} %get-tuple-element.520, bf16[1,1024,1536]{2,1,0:T(8,128)(2,1)S(1)} %get-tuple-element.519), kind=kOutput, calls=%fused_computation.108 | convolution fusion | flops 12890144768 | bytes 23068672 | tf_op jit(solution)/shard_map/tbsf,tdf->bsd/dot_general | solution.py:280
  777.3 14.6 convert_bitcast_fusion.1
  792.2 27.9 %reduce-scatter.14.cloned.1.call-done = bf16[1,256,2048]{2,1,0:T(8,128)(2,1)} async-done(((bf16[1,1024,2048]{2,1,0:T(8,128)(2,1)}), bf16[1,256,2048]{2,1,0:T(8,128)(2,1)}) %reduce-scatter.14.cloned.1.call-update) | async-done | bytes 1048592 | tf_op jit(solution)/shard_map/reduce_scatter | solution.py:279
  820.2 46.9 %reduce-scatter.12.cloned.1.call-done = bf16[1,256,2048]{2,1,0:T(8,128)(2,1)} async-done(((bf16[1,1024,2048]{2,1,0:T(8,128)(2,1)}), bf16[1,256,2048]{2,1,0:T(8,128)(2,1)}) %reduce-scatter.12.cloned.1.call-update) | async-done | bytes 1048592 | tf_op jit(solution)/shard_map/reduce_scatter | solution.py:255
  873.8 34.5 %all-gather.26.cloned.1.call-done = bf16[1,1024,2048]{2,1,0:T(8,128)(2,1)} async-done(((bf16[1,256,2048]{2,1,0:T(8,128)(2,1)}), bf16[1,1024,2048]{2,1,0:T(8,128)(2,1)}) %all-gather.26.cloned.1.call-update) | async-done | bytes 4194320 | tf_op jit(solution)/shard_map/all_gather | solution.py:289
  914.6 50.2 %while.51 = (s32[]{:T(128)}, f32[1024,2,128]{0,2,1:T(8,128)S(1)}, f32[1024,2,128]{0,2,1:T(8,128)}, f32[2,512,2,2,128]{4,1,0,3,2:T(8,128)}, s32[2]{0:T(128)S(1)},...) while((s32[]{:T(128)}, f32[1024,2,128]{0,2,1:T(8,128)S(1)}, ...), condition=%wide.region_14.15_spmd.clone.clone, body=%wide.region_12.14_spmd.clone.clone.sunk | while | flops 2718432768 | bytes 180943296 | solution.py:150
  1009.9 19.3 %convert_bitcast_fusion = bf16[2,2048,1536]{1,2,0:T(8,128)(2,1)} fusion(bf16[1,1024,2048]{2,1,0:T(8,128)(2,1)} %all-gather.18.cloned.1.call-done, bf16[1,1024,1536]{2,1,0:T(8,128)(2,1)} %copy-done.91, bf16[1,1024,1536]{2,1,0:T(8,128)(2,1)} %copy-done.90), kind=kOutput, calls=%fused_computation.64 | convolution fusion | flops 12894339072 | bytes 23068672 | tf_op jit(solution)/shard_map/bsd,tbsf->tdf/dot_general | solution.py:276
  1053.9 60.2 %reduce-scatter.18.cloned.1.call-done = bf16[256,512]{1,0:T(8,128)(2,1)} async-done(((bf16[2048,512]{1,0:T(8,128)(2,1)}), bf16[256,512]{1,0:T(8,128)(2,1)}) %reduce-scatter.18.cloned.1.call-update) | async-done | bytes 262160 | tf_op jit(solution)/shard_map/reduce_scatter | solution.py:335
  1117.1 67.9 %reduce-scatter.22.cloned.1.call-done = bf16[512,256]{1,0:T(8,128)(2,1)} async-done(((bf16[512,2048]{1,0:T(8,128)(2,1)}), bf16[512,256]{1,0:T(8,128)(2,1)}) %reduce-scatter.22.cloned.1.call-update) | async-done | bytes 262160 | tf_op jit(solution)/shard_map/reduce_scatter | solution.py:341
  1188.4 42.6 %reduce-scatter.16.cloned.1.call-done = bf16[1,256,2048]{2,1,0:T(8,128)(2,1)} async-done(((bf16[1,1024,2048]{2,1,0:T(8,128)(2,1)}), bf16[1,256,2048]{2,1,0:T(8,128)(2,1)}) %reduce-scatter.16.cloned.1.call-update) | async-done | bytes 1048592 | tf_op jit(solution)/shard_map/reduce_scatter | solution.py:320
  1237.4 205.0 %reduce-scatter.24.cloned.1.call-done = bf16[2,256,1536]{1,2,0:T(8,128)(2,1)} async-done(((bf16[2,2048,1536]{1,2,0:T(8,128)(2,1)}), bf16[2,256,1536]{1,2,0:T(8,128)(2,1)}) %reduce-scatter.24.cloned.1.call-update) | async-done | bytes 1572880 | tf_op jit(solution)/shard_map/reduce_scatter | solution.py:344
  1463.1 39.9 %all-reduce = (f32[4352]{0:T(1024)S(1)}, f32[14]{0:T(128)S(1)}) all-reduce(f32[4352]{0:T(1024)S(1)} %pad_maximum_fusion.12, f32[14]{0:T(128)S(1)} %stack.136), channel_id=1, replica_groups=mesh['wide'=8,'narrow'=4] {'wide','narrow'}, use_global_device_ids=true, to_apply=%region_52.53 | all-reduce | flops 4366 | bytes 34928 | tf_op jit(solution)/shard_map/psum | solution.py:23
  (402 shorter events, 299.8 us)
Async XLA Ops:
  7.2 55.6 %all-gather.12.cloned.1.call-start = ((), (), s32[]{:S(2)}) async-start(), calls=%async_computation.10 | async-start | bytes 2359296 | tf_op jit(solution)/shard_map/all_gather | solution.py:209
  9.2 88.8 %all-gather.10.cloned.1.call-start = ((), (), s32[]{:S(2)}) async-start(), calls=%async_computation.9 | async-start | bytes 5242880 | tf_op jit(solution)/shard_map/all_gather | solution.py:218
  11.4 860.3 %copy-start.60 = (f32[2048]{0:T(1024)}, f32[2048]{0:T(1024)S(1)}, u32[]{:S(2)}) copy-start(f32[2048]{0:T(1024)S(1)} %get-tuple-element.539) | copy-start | bytes 24580
  12.7 138.9 %all-gather.14.cloned.1.call-start = ((), (), s32[]{:S(2)}) async-start(), calls=%async_computation.11 | async-start | bytes 2359296 | tf_op jit(solution)/shard_map/all_gather | solution.py:210
  13.9 189.5 %all-gather.16.cloned.1.call-start = ((), (), s32[]{:S(2)}) async-start(), calls=%async_computation.12 | async-start | bytes 2359296 | tf_op jit(solution)/shard_map/all_gather | solution.py:211
  14.7 237.8 %reduce-scatter.10.cloned.1.call-start = ((), (), s32[]{:S(2)}) async-start(), calls=%async_computation.13 | async-start | bytes 5242880 | tf_op jit(solution)/shard_map/reduce_scatter | solution.py:235
  15.4 147.4 %copy-start.82 = (f32[128]{0:T(128)}, f32[128]{0:T(128)S(1)}, u32[]{:S(2)}) copy-start(f32[128]{0:T(128)S(1)} %get-tuple-element.537) | copy-start | bytes 1540
  17.4 143.2 %copy-start.20 = (f32[1024,64]{1,0:T(8,128)}, f32[1024,64]{1,0:T(8,128)S(1)}, u32[]{:S(2)}) copy-start(f32[1024,64]{1,0:T(8,128)S(1)} %get-tuple-element.557) | copy-start | bytes 786436
  17.6 145.4 %copy-start.37 = (f32[1024,64]{0,1:T(8,128)}, f32[1024,64]{0,1:T(8,128)S(1)}, u32[]{:S(2)}) copy-start(f32[1024,64]{0,1:T(8,128)S(1)} %copy.107) | copy-start | bytes 786436
  209.6 80.8 %all-gather.18.cloned.1.call-start = ((), (), s32[]{:S(2)}) async-start(), calls=%async_computation.14 | async-start | bytes 5242880 | tf_op jit(solution)/shard_map/all_gather | solution.py:246
  254.2 617.5 %copy-start.70 = (f32[256]{0:T(256)}, f32[256]{0:T(256)S(1)}, u32[]{:S(2)}) copy-start(f32[256]{0:T(256)S(1)} %add_rsqrt_fusion.2) | copy-start | bytes 3076
  255.7 214.1 %all-gather.20.cloned.1.call-start = ((), (), s32[]{:S(2)}) async-start(), calls=%async_computation.15 | async-start | bytes 14155776 | tf_op jit(solution)/shard_map/all_gather | solution.py:212
  259.0 245.7 %all-gather.24.cloned.1.call-start = ((), (), s32[]{:S(2)}) async-start(), calls=%async_computation.18 | async-start | bytes 5242880 | tf_op jit(solution)/shard_map/all_gather | solution.py:269
  259.7 612.0 %copy-start.76 = (f32[256]{0:T(256)}, f32[256]{0:T(256)S(1)}, u32[]{:S(2)}) copy-start(f32[256]{0:T(256)S(1)} %compare_convert_fusion) | copy-start | bytes 3076
  262.2 374.1 %reduce-scatter.26.cloned.1.call-start = ((), (), s32[]{:S(2)}) async-start(), calls=%async_computation.26 | async-start | bytes 7077888 | tf_op jit(solution)/shard_map/reduce_scatter | solution.py:347
  517.7 224.3 %all-gather.22.cloned.1.call-start = ((), (), s32[]{:S(2)}) async-start(), calls=%async_computation.16 | async-start | bytes 7077888 | tf_op jit(solution)/shard_map/all_gather | solution.py:213
  642.8 177.4 %reduce-scatter.14.cloned.1.call-start = ((), (), s32[]{:S(2)}) async-start(), calls=%async_computation.19 | async-start | bytes 5242880 | tf_op jit(solution)/shard_map/reduce_scatter | solution.py:279
  777.3 89.7 %reduce-scatter.12.cloned.1.call-start = ((), (), s32[]{:S(2)}) async-start(), calls=%async_computation.17 | async-start | bytes 5242880 | tf_op jit(solution)/shard_map/reduce_scatter | solution.py:255
  792.0 116.3 %all-gather.26.cloned.1.call-start = ((), (), s32[]{:S(2)}) async-start(), calls=%async_computation.20 | async-start | bytes 5242880 | tf_op jit(solution)/shard_map/all_gather | solution.py:289
  873.7 174.0 %reduce-scatter.20.cloned.1.call-start = ((), (), s32[]{:S(2)}) async-start(), calls=%async_computation.23 | async-start | bytes 2359296 | tf_op jit(solution)/shard_map/reduce_scatter | solution.py:338
  975.3 138.8 %reduce-scatter.18.cloned.1.call-start = ((), (), s32[]{:S(2)}) async-start(), calls=%async_computation.22 | async-start | bytes 2359296 | tf_op jit(solution)/shard_map/reduce_scatter | solution.py:335
  992.6 192.3 %reduce-scatter.22.cloned.1.call-start = ((), (), s32[]{:S(2)}) async-start(), calls=%async_computation.24 | async-start | bytes 2359296 | tf_op jit(solution)/shard_map/reduce_scatter | solution.py:341
  999.9 231.2 %reduce-scatter.16.cloned.1.call-start = ((), (), s32[]{:S(2)}) async-start(), calls=%async_computation.21 | async-start | bytes 5242880 | tf_op jit(solution)/shard_map/reduce_scatter | solution.py:320
  1009.8 432.5 %reduce-scatter.24.cloned.1.call-start = ((), (), s32[]{:S(2)}) async-start(), calls=%async_computation.25 | async-start | bytes 14155776 | tf_op jit(solution)/shard_map/reduce_scatter | solution.py:344
  (96 other events, 2097.8 us)
Sparse Core Ops, SparseCore 0:
  10.7 51.9 all-gather.11
  64.9 32.9 all-gather.9
  100.5 51.0 all-gather.13
  154.1 49.2 all-gather.15
  209.7 42.6 reduce-scatter.9
  255.8 34.4 all-gather.17
  293.4 176.4 all-gather.19
  472.1 32.6 all-gather.23
  517.8 118.3 reduce-scatter.25
  642.9 99.0 all-gather.21
  777.4 42.6 reduce-scatter.13
  822.5 44.4 reduce-scatter.11
  873.8 34.4 all-gather.25
  975.4 68.1 reduce-scatter.19
  1047.3 66.6 reduce-scatter.17
  1117.8 67.1 reduce-scatter.21
  1187.5 43.5 reduce-scatter.15
  1234.5 207.7 reduce-scatter.23
where the time goes:
time: 1550 us
  waiting for transfers between devices  1100 us (71%)
  matrix products  184 us (12%)
  other arithmetic  115 us (7%)
  local copies, waits for them, and re-layouts  78.8 us (5%)
  blocking collectives  39.9 us (3%)
  between operations  23.7 us (2%)
    reduce_scatter x1, waiting for transfers between devices, shards(): lax.psum_scatter(gateup_grad.astype(jnp.bfloat16), 'wide', scatter_dimens...  205 us
    all_gather x1, waiting for transfers between devices, shards(): lax.all_gather(gateup_weight.astype(jnp.bfloat16), 'wide', axis=1, tiled=...  179 us
    reduce_scatter x1, waiting for transfers between devices, shards(): lax.psum_scatter(down_grad.astype(jnp.bfloat16), 'wide', scatter_dimensio...  119 us
    all_gather x1, waiting for transfers between devices, shards(): lax.all_gather(down_weight.astype(jnp.bfloat16), 'wide', axis=1, tiled=True)  99.2 us
    reduce_scatter x1, waiting for transfers between devices, shards(): lax.psum_scatter(output_grad.astype(jnp.bfloat16), 'wide', scatter_dimens...  67.9 us
    reduce_scatter x1, waiting for transfers between devices, shards(): lax.psum_scatter(query_wgrad.astype(jnp.bfloat16), 'wide', scatter_dimens...  60.2 us
    reduce_scatter x1, waiting for transfers between devices, shards(): lax.psum_scatter(jnp.einsum('bsf,fd->bsd', hidden, full_down, preferred_e...  46.9 us
    all_gather x1, waiting for transfers between devices, shards(): lax.all_gather(query_weight.astype(jnp.bfloat16), 'wide', axis=0, tiled=T...  44.3 us
  transfers between devices with their start and end apart: 18, of which 17 were waited for; matrix products, arithmetic and copies ran while one was open for 12% of the time, Pallas kernels for 0%

commit v1 on v0

v1 whole, which is shorter than its diff:
```python
import functools

import jax
import jax.numpy as jnp
from jax import lax
from jax.experimental import pallas as pl
from jax.experimental.pallas import tpu as pltpu
from jax.sharding import PartitionSpec as P

D = 2048
H = 16
KV = 8
HD = 128
STEP = 10


EPS = 1e-06
THETA = 1000000.0
BETA_ONE = 0.9
BETA_TWO = 0.999
ADAM_EPS = 1e-06
DECAY = 0.01
LEARN = 0.5

SCALE = HD ** (-0.5)

CHIP = ("narrow", 2)
CORE = ("narrow", 1)
PAIR = ("inner", 1)


def swap(values, link):
    axis, bit = link
    return lax.ppermute(values, axis, [(i, i ^ bit) for i in range(lax.axis_size(axis))])


def gather_rows(own):
    half = own.shape[0] // 2
    chip = swap(own, CHIP)
    pair = swap(own, PAIR)
    cross = [swap(chip[:half], PAIR), swap(pair[half:], CHIP)]
    near = [own, chip, pair, *cross]
    return jnp.concatenate(near + [swap(block, CORE) for block in near], 0)


def scatter_rows(near, far_low):
    rows = near.shape[0] // 4
    half = rows // 2
    part = (near + swap(far_low, CORE).astype(jnp.float32)).astype(jnp.bfloat16)
    own, chip, pair, cross = (part[i * rows : (i + 1) * rows] for i in range(4))
    from_pair = swap(cross[:half], PAIR)
    from_chip = swap(cross[half:], CHIP)
    chip_late = swap(chip[half:], CHIP)
    pair_early = swap(pair[:half], PAIR)
    wide = jnp.float32
    chip_early = swap((chip[:half].astype(wide) + from_pair.astype(wide)).astype(jnp.bfloat16), CHIP)
    pair_late = swap((pair[half:].astype(wide) + from_chip.astype(wide)).astype(jnp.bfloat16), PAIR)
    return own.astype(wide) + jnp.concatenate(
        [
            chip_early.astype(wide) + pair_early.astype(wide),
            chip_late.astype(wide) + pair_late.astype(wide),
        ],
        0,
    )


def product_rows(form, left, right):
    rows = left.shape[0] // 2
    far = jnp.einsum(form, left[rows:], right, preferred_element_type=jnp.float32)
    near = jnp.einsum(form, left[:rows], right, preferred_element_type=jnp.float32)
    return scatter_rows(near, far.astype(jnp.bfloat16))


def halves(values, axis):
    place = lax.axis_index("inner")
    size = values.shape[axis] // 2
    mine = lax.dynamic_slice_in_dim(values, place * size, size, axis)
    theirs = lax.dynamic_slice_in_dim(values, (1 - place) * size, size, axis)
    return (mine, theirs)


def in_order(mine, theirs, axis):
    first = lax.axis_index("inner") == 0
    return jnp.concatenate([jnp.where(first, mine, theirs), jnp.where(first, theirs, mine)], axis)


def trade(values, cut, join):
    mine, theirs = halves(values, cut)
    return in_order(mine, swap(theirs, PAIR), join)


def rope_tables(length):
    places = jnp.arange(length, dtype=jnp.float32)
    frequency = THETA ** (-jnp.arange(HD // 2, dtype=jnp.float32) * 2.0 / HD)
    angles = places[:, None] * frequency[None, :]
    cos_table = jnp.cos(angles)
    sin_table = jnp.sin(angles)
    return (
        jnp.concatenate([cos_table, cos_table], 1),
        jnp.concatenate([-sin_table, sin_table], 1),
    )


def unit_of(raw):
    inverse = lax.rsqrt(jnp.mean(raw * raw, -1, keepdims=True) + EPS)
    return (raw * inverse, inverse)


def turn(values, cos_table, sin_table):
    return values * cos_table + pltpu.roll(values, HD // 2, 1) * sin_table


def place_of(meta, block):
    relative = jnp.bitwise_xor(meta[0], block)
    return (jnp.bitwise_and(relative, 1), lax.shift_right_logical(relative, 1))


def load_heads(meta, raw, gains, cos_ref, sin_ref, queries, keys, values, rows, blocks, heads):
    gain_query = gains[0:1, :]
    gain_key = gains[1:2, :]
    for block in range(blocks):
        core, chip = place_of(meta, block)
        span = slice(block * rows, (block + 1) * rows)
        tile = raw[core, chip]
        cos_table = cos_ref[span, :]
        sin_table = sin_ref[span, :]
        for head in range(heads):
            unit, _ = unit_of(tile[:, head * HD : (head + 1) * HD])
            queries[head, span, :] = turn(unit * gain_query, cos_table, sin_table).astype(jnp.bfloat16)
        unit, _ = unit_of(tile[:, heads * HD : (heads + 1) * HD])
        keys[span, :] = turn(unit * gain_key, cos_table, sin_table).astype(jnp.bfloat16)
        values[span, :] = tile[:, (heads + 1) * HD :].astype(jnp.bfloat16)


def weights_of(query, keys, start, valid_len):
    scores = lax.dot_general(query, keys, (((1,), (1,)), ((), ())), preferred_element_type=jnp.float32)
    row = start + lax.broadcasted_iota(jnp.int32, scores.shape, 0)
    column = lax.broadcasted_iota(jnp.int32, scores.shape, 1)
    allowed = (column <= row) & (column < valid_len)
    weights = jnp.where(allowed, jnp.exp(scores * SCALE), 0.0)
    return (weights, 1.0 / jnp.sum(weights, -1, keepdims=True))


def forward_kernel(rows, blocks, heads, meta, raw, gains, cos_ref, sin_ref, context, queries, keys, values):
    load_heads(meta, raw, gains, cos_ref, sin_ref, queries, keys, values, rows, blocks, heads)
    valid_len = meta[1 + pl.program_id(0)]
    for block in range(blocks):
        core, chip = place_of(meta, block)
        seen = (block + 1) * rows
        for head in range(heads):
            query = queries[head, block * rows : seen, :]
            weights, inverse = weights_of(query, keys[:seen, :], block * rows, valid_len)
            part = jnp.dot(
                weights.astype(jnp.bfloat16), values[:seen, :], preferred_element_type=jnp.float32
            )
            context[core, chip, :, head * HD : (head + 1) * HD] = (part * inverse).astype(jnp.bfloat16)


def backward_kernel(
    rows, blocks, heads, meta, raw, context_grad, gains, cos_ref, sin_ref,
    raw_grad, gain_grad, queries, keys, values, key_grad, value_grad, query_grad,
):
    load_heads(meta, raw, gains, cos_ref, sin_ref, queries, keys, values, rows, blocks, heads)
    valid_len = meta[1 + pl.program_id(0)]
    key_grad[...] = jnp.zeros_like(key_grad)
    value_grad[...] = jnp.zeros_like(value_grad)
    first = (((0,), (0,)), ((), ()))
    last = (((1,), (1,)), ((), ()))
    for block in range(blocks):
        core, chip = place_of(meta, block)
        seen = (block + 1) * rows
        for head in range(heads):
            query = queries[head, block * rows : seen, :]
            grad = context_grad[core, chip, :, head * HD : (head + 1) * HD]
            weights, inverse = weights_of(query, keys[:seen, :], block * rows, valid_len)
            probability = weights * inverse
            value_grad[:seen, :] += lax.dot_general(
                probability.astype(jnp.bfloat16), grad, first, preferred_element_type=jnp.float32
            )
            prob_grad = lax.dot_general(grad, values[:seen, :], last, preferred_element_type=jnp.float32)
            inner = jnp.sum(probability * prob_grad, -1, keepdims=True)
            score_grad = (probability * (prob_grad - inner)).astype(jnp.bfloat16)
            query_grad[head, block * rows : seen, :] = SCALE * jnp.dot(
                score_grad, keys[:seen, :], preferred_element_type=jnp.float32
            )
            key_grad[:seen, :] += SCALE * lax.dot_general(
                score_grad, query, first, preferred_element_type=jnp.float32
            )
    query_total = jnp.zeros((1, HD), jnp.float32)
    key_total = jnp.zeros((1, HD), jnp.float32)
    for block in range(blocks):
        core, chip = place_of(meta, block)
        span = slice(block * rows, (block + 1) * rows)
        cos_table = cos_ref[span, :]
        sin_table = sin_ref[span, :]

        def back(raw_values, turned, gain):
            unit, inverse = unit_of(raw_values)
            scaled = turn(turned, cos_table, -sin_table)
            total = jnp.sum(scaled * unit, 0, keepdims=True)
            scaled = scaled * gain
            result = inverse * (scaled - unit * jnp.mean(scaled * unit, -1, keepdims=True))
            return (result.astype(jnp.bfloat16), total)

        for head in range(heads):
            columns = slice(head * HD, (head + 1) * HD)
            result, total = back(raw[core, chip, :, columns], query_grad[head, span, :], gains[0:1, :])
            raw_grad[core, chip, :, columns] = result
            query_total += total
        columns = slice(heads * HD, (heads + 1) * HD)
        result, total = back(raw[core, chip, :, columns], key_grad[span, :], gains[1:2, :])
        raw_grad[core, chip, :, columns] = result
        key_total += total
        raw_grad[core, chip, :, (heads + 1) * HD :] = value_grad[span, :].astype(jnp.bfloat16)
    gain_grad[0:1, :] = query_total
    gain_grad[1:2, :] = key_total


def row_blocks(rows, columns):
    return pl.BlockSpec((2, None, 2, rows, columns), lambda s, meta: (0, s, 0, 0, 0))


def whole(shape):
    return pl.BlockSpec(shape, lambda s, meta: (0,) * len(shape))


def split_rows(values, rows):
    return values.reshape(2, 2, 2, rows, values.shape[-1])


def attend_forward(meta, raw, gains, cos_table, sin_table):
    length = cos_table.shape[0]
    rows = raw.shape[0] // 8
    blocks = length // rows
    heads = raw.shape[1] // HD - 2
    pairs = 2 * heads * length * length
    result = pl.pallas_call(
        functools.partial(forward_kernel, rows, blocks, heads),
        out_shape=jax.ShapeDtypeStruct((2, 2, 2, rows, heads * HD), jnp.bfloat16),
        grid_spec=pltpu.PrefetchScalarGridSpec(
            num_scalar_prefetch=1,
            grid=(2,),
            in_specs=[
                row_blocks(rows, raw.shape[1]),
                whole((2, HD)),
                whole((length, HD)),
                whole((length, HD)),
            ],
            out_specs=row_blocks(rows, heads * HD),
            scratch_shapes=[
                pltpu.VMEM((heads, length, HD), jnp.bfloat16),
                pltpu.VMEM((length, HD), jnp.bfloat16),
                pltpu.VMEM((length, HD), jnp.bfloat16),
            ],
        ),
        compiler_params=pltpu.CompilerParams(vmem_limit_bytes=40 << 20),
        cost_estimate=pl.CostEstimate(
            flops=4 * pairs * HD, transcendentals=pairs, bytes_accessed=raw.size * 6
        ),
        name="attend_forward",
    )(meta, split_rows(raw, rows), gains, cos_table, sin_table)
    return result.reshape(8 * rows, heads * HD)


def attend_backward(meta, raw, context_grad, gains, cos_table, sin_table):
    length = cos_table.shape[0]
    rows = raw.shape[0] // 8
    blocks = length // rows
    width = raw.shape[1]
    heads = width // HD - 2
    pairs = 2 * heads * length * length
    raw_grad, gain_grad = pl.pallas_call(
        functools.partial(backward_kernel, rows, blocks, heads),
        out_shape=(
            jax.ShapeDtypeStruct((2, 2, 2, rows, width), jnp.bfloat16),
            jax.ShapeDtypeStruct((2, 2, HD), jnp.float32),
        ),
        grid_spec=pltpu.PrefetchScalarGridSpec(
            num_scalar_prefetch=1,
            grid=(2,),
            in_specs=[
                row_blocks(rows, width),
                row_blocks(rows, heads * HD),
                whole((2, HD)),
                whole((length, HD)),
                whole((length, HD)),
            ],
            out_specs=(
                row_blocks(rows, width),
                pl.BlockSpec((None, 2, HD), lambda s, meta: (s, 0, 0)),
            ),
            scratch_shapes=[
                pltpu.VMEM((heads, length, HD), jnp.bfloat16),
                pltpu.VMEM((length, HD), jnp.bfloat16),
                pltpu.VMEM((length, HD), jnp.bfloat16),
                pltpu.VMEM((length, HD), jnp.float32),
                pltpu.VMEM((length, HD), jnp.float32),
                pltpu.VMEM((heads, length, HD), jnp.float32),
            ],
        ),
        compiler_params=pltpu.CompilerParams(vmem_limit_bytes=48 << 20),
        cost_estimate=pl.CostEstimate(
            flops=10 * pairs * HD, transcendentals=pairs, bytes_accessed=raw.size * 8
        ),
        name="attend_backward",
    )(meta, split_rows(raw, rows), split_rows(context_grad, rows), gains, cos_table, sin_table)
    return (raw_grad.reshape(8 * rows, width), jnp.sum(gain_grad, 0))


def norm_back(normed_grad, hat_values, inverse, gain_vector):
    gain_grad = jnp.sum(normed_grad * hat_values, axis=0)
    scaled = normed_grad * gain_vector
    return (
        inverse * (scaled - hat_values * jnp.mean(scaled * hat_values, -1, keepdims=True)),
        gain_grad,
    )


def adam_step(gradient, moment_one, moment_two, master):
    new_one = BETA_ONE * moment_one + (1.0 - BETA_ONE) * gradient
    new_two = BETA_TWO * moment_two + (1.0 - BETA_TWO) * gradient * gradient
    update = (
        new_one / (1.0 - BETA_ONE**STEP) / (jnp.sqrt(new_two / (1.0 - BETA_TWO**STEP)) + ADAM_EPS)
        + DECAY * master
    )
    return (new_one, new_two, update)


def square(values):
    return jnp.sum(values * values)


def root_mean(values):
    return jnp.sqrt(jnp.mean(values * values, -1))


def gather_outer(values):
    return lax.all_gather(values, "outer", axis=0, tiled=True)


def scatter_outer(values):
    return lax.psum_scatter(values, "outer", scatter_dimension=0, tiled=True)


def shards(
    tokens,
    cotangent,
    lengths,
    norm_gains,
    gains_first,
    gains_second,
    query_weight,
    query_first,
    query_second,
    keyval_weight,
    keyval_first,
    keyval_second,
    output_weight,
    output_first,
    output_second,
    gateup_weight,
    gateup_first,
    gateup_second,
    down_weight,
    down_first,
    down_second,
):
    low = jnp.bfloat16
    shard_len = tokens.shape[1]
    narrow_size = lax.axis_size("narrow")
    outer_size = lax.axis_size("outer")
    seq_len = shard_len * narrow_size
    gain_one = norm_gains[:D]
    gain_two = norm_gains[D : 2 * D]
    head_gains = norm_gains[2 * D :].reshape(2, HD)
    cos_table, sin_table = rope_tables(seq_len)

    attn_pair = jnp.concatenate(
        [
            trade(part.astype(low), 1, 0)
            for part in (query_weight, keyval_weight[0], keyval_weight[1])
        ],
        1,
    )
    output_pair = trade(output_weight.astype(low), 0, 1)
    gateup_pair = jnp.concatenate(
        [trade(gateup_weight[0].astype(low), 1, 0), trade(gateup_weight[1].astype(low), 1, 0)], 1
    )
    down_pair = trade(down_weight.astype(low), 0, 1)
    full_attn = gather_outer(attn_pair)
    full_output = gather_outer(output_pair[None])
    full_gateup = gather_outer(gateup_pair)
    full_down = gather_outer(down_pair[None])
    piece = output_pair.shape[1]
    hidden_size = down_pair.shape[0]

    residual = tokens[0].astype(jnp.float32)
    inv_one = lax.rsqrt(jnp.mean(residual * residual, -1, keepdims=True) + EPS)
    hat_one = residual * inv_one
    whole_one = gather_rows((hat_one * gain_one).astype(low))
    raw = jnp.einsum("rd,dc->rc", whole_one, full_attn, preferred_element_type=jnp.float32)
    meta = jnp.concatenate(
        [lax.axis_index("narrow").astype(jnp.int32)[None], lengths, swap(lengths, PAIR)]
    )
    context = attend_forward(meta, raw, head_gains, cos_table, sin_table)

    def out_product(left, right):
        rows = left.shape[0]
        result = jnp.einsum("rc,zcd->rzd", left, right, preferred_element_type=jnp.float32)
        return result.reshape(rows, D)

    def rows_out(left, right):
        rows = left.shape[0] // 2
        far = out_product(left[rows:], right).astype(low)
        return scatter_rows(out_product(left[:rows], right), far)

    attn_part = rows_out(context, full_output)
    middle = residual + attn_part
    inv_two = lax.rsqrt(jnp.mean(middle * middle, -1, keepdims=True) + EPS)
    hat_two = middle * inv_two
    whole_two = gather_rows((hat_two * gain_two).astype(low))
    gateup = jnp.einsum("rd,df->rf", whole_two, full_gateup, preferred_element_type=jnp.float32)
    gate_val = gateup[:, :hidden_size]
    up_val = gateup[:, hidden_size:]
    sigmoid = jax.nn.sigmoid(gate_val)
    swish = gate_val * sigmoid
    hidden = (swish * up_val).astype(low)

    places = lax.axis_index("narrow") * shard_len + jnp.arange(shard_len, dtype=jnp.int32)
    valid = (places < lengths[0]).astype(jnp.float32)
    grad_out = cotangent[0].astype(jnp.float32) * valid[:, None]
    whole_grad = gather_rows(grad_out.astype(low))
    pieces_grad = whole_grad.reshape(whole_grad.shape[0], outer_size, piece)
    down_grad = jnp.einsum("rf,rzd->zfd", hidden, pieces_grad, preferred_element_type=jnp.float32)
    hidden_grad = jnp.einsum("rzd,zfd->rf", pieces_grad, full_down, preferred_element_type=jnp.float32)
    slope = sigmoid * (1.0 + gate_val * (1.0 - sigmoid))
    pair_grad = jnp.concatenate([hidden_grad * up_val * slope, hidden_grad * swish], 1).astype(low)
    gateup_grad = jnp.einsum("rd,rf->df", whole_two, pair_grad, preferred_element_type=jnp.float32)
    normed_two = product_rows("rf,df->rd", pair_grad, full_gateup)
    middle_norm, gain_two_grad = norm_back(normed_two, hat_two, inv_two, gain_two)
    middle_grad = grad_out + middle_norm
    whole_mid = gather_rows(middle_grad.astype(low))
    pieces_mid = whole_mid.reshape(whole_mid.shape[0], outer_size, piece)
    output_grad = jnp.einsum("rc,rzd->zcd", context, pieces_mid, preferred_element_type=jnp.float32)
    context_grad = jnp.einsum(
        "rzd,zcd->rc", pieces_mid, full_output, preferred_element_type=jnp.float32
    ).astype(low)
    attn_low, head_gain_grad = attend_backward(meta, raw, context_grad, head_gains, cos_table, sin_table)
    attn_grad = jnp.einsum("rd,rc->dc", whole_one, attn_low, preferred_element_type=jnp.float32)
    normed_one = product_rows("rc,dc->rd", attn_low, full_attn)
    input_norm, gain_one_grad = norm_back(normed_one, hat_one, inv_one, gain_one)
    input_grad = (middle_grad + input_norm).astype(low)

    mlp_part = rows_out(hidden, full_down)
    final = middle + mlp_part
    result = final.astype(low)
    rms_values = jnp.stack([root_mean(attn_part), root_mean(mlp_part), root_mean(final)])[:, None, :]

    down_sum = trade(scatter_outer(down_grad.astype(low))[0], 1, 0).astype(jnp.float32)
    gateup_own = scatter_outer(gateup_grad.astype(low))
    gateup_sum = jnp.stack(
        [trade(gateup_own[:, :hidden_size], 0, 1), trade(gateup_own[:, hidden_size:], 0, 1)]
    ).astype(jnp.float32)
    output_sum = trade(scatter_outer(output_grad.astype(low))[0], 1, 0).astype(jnp.float32)
    attn_own = scatter_outer(attn_grad.astype(low))
    query_half = query_weight.shape[1] // 2
    key_half = keyval_weight.shape[2] // 2
    query_sum = trade(attn_own[:, :query_half], 0, 1).astype(jnp.float32)
    keyval_sum = jnp.stack(
        [
            trade(attn_own[:, query_half : query_half + key_half], 0, 1),
            trade(attn_own[:, query_half + key_half :], 0, 1),
        ]
    ).astype(jnp.float32)

    gain_part = jnp.concatenate([gain_one_grad, gain_two_grad, head_gain_grad.reshape(-1)])
    new_query_first, new_query_second, query_update = adam_step(
        query_sum, query_first, query_second, query_weight
    )
    new_keyval_first, new_keyval_second, keyval_update = adam_step(
        keyval_sum, keyval_first, keyval_second, keyval_weight
    )
    new_output_first, new_output_second, output_update = adam_step(
        output_sum, output_first, output_second, output_weight
    )
    new_gateup_first, new_gateup_second, gateup_update = adam_step(
        gateup_sum, gateup_first, gateup_second, gateup_weight
    )
    new_down_first, new_down_second, down_update = adam_step(
        down_sum, down_first, down_second, down_weight
    )
    squares = jnp.stack(
        [
            square(query_weight),
            square(keyval_weight[0]),
            square(keyval_weight[1]),
            square(output_weight),
            square(gateup_weight[0]),
            square(gateup_weight[1]),
            square(down_weight),
            square(query_update),
            square(keyval_update[0]),
            square(keyval_update[1]),
            square(output_update),
            square(gateup_update[0]),
            square(gateup_update[1]),
            square(down_update),
        ]
    )
    gain_total, square_total = lax.psum((gain_part, squares), ("outer", "inner", "narrow"))
    matrix_norms = jnp.sqrt(square_total)
    matrix_weight = matrix_norms[:7]
    matrix_update = matrix_norms[7:]
    new_gains_first, new_gains_second, gains_update = adam_step(
        gain_total, gains_first, gains_second, norm_gains
    )
    segments = ((0, D), (2 * D, 2 * D + HD), (2 * D + HD, 2 * D + 2 * HD), (D, 2 * D))
    gain_weight = [jnp.sqrt(square(norm_gains[lower:upper])) for lower, upper in segments]
    gain_update = [jnp.sqrt(square(gains_update[lower:upper])) for lower, upper in segments]

    def ordered(gain, matrix):
        return jnp.stack(
            [gain[0], matrix[0], matrix[1], matrix[2], gain[1], gain[2], matrix[3], gain[3]]
            + [matrix[4], matrix[5], matrix[6]]
        )

    weight_norms = ordered(gain_weight, matrix_weight)
    update_norms = ordered(gain_update, matrix_update)
    trust = weight_norms / update_norms
    gain_trust = jnp.concatenate(
        [
            jnp.full((D,), 1.0, jnp.float32) * trust[0],
            jnp.full((D,), 1.0, jnp.float32) * trust[7],
            jnp.full((HD,), 1.0, jnp.float32) * trust[4],
            jnp.full((HD,), 1.0, jnp.float32) * trust[5],
        ]
    )
    new_gains = norm_gains - LEARN * gain_trust * gains_update
    new_query = query_weight - LEARN * trust[1] * query_update
    new_keyval = (
        keyval_weight - LEARN * jnp.stack([trust[2], trust[3]])[:, None, None] * keyval_update
    )
    new_output = output_weight - LEARN * trust[6] * output_update
    new_gateup = (
        gateup_weight - LEARN * jnp.stack([trust[8], trust[9]])[:, None, None] * gateup_update
    )
    new_down = down_weight - LEARN * trust[10] * down_update
    lamb_stats = jnp.stack([weight_norms, update_norms])
    return (
        result[None],
        input_grad[None],
        rms_values,
        new_gains,
        new_gains_first,
        new_gains_second,
        new_query,
        new_query_first,
        new_query_second,
        new_keyval,
        new_keyval_first,
        new_keyval_second,
        new_output,
        new_output_first,
        new_output_second,
        new_gateup,
        new_gateup_first,
        new_gateup_second,
        new_down,
        new_down_first,
        new_down_second,
        lamb_stats,
        trust,
    )


def solution(mesh):
    wide_size, narrow_size = mesh.devices.shape
    cube = jax.sharding.Mesh(
        mesh.devices.reshape(wide_size // 2, 2, narrow_size), ("outer", "inner", "narrow")
    )
    wide = ("outer", "inner")
    rows = P(wide, "narrow", None)
    matrix = P(wide, "narrow")
    stacked = P(None, wide, "narrow")
    turned = P("narrow", wide)
    in_specs = (rows, rows, P(wide), P(), P(), P())
    in_specs += (matrix,) * 3 + (stacked,) * 3 + (turned,) * 3 + (stacked,) * 3 + (turned,) * 3
    out_specs = (rows, rows, stacked, P(), P(), P())
    out_specs += (matrix,) * 3 + (stacked,) * 3 + (turned,) * 3 + (stacked,) * 3 + (turned,) * 3
    out_specs += (P(), P())
    return jax.shard_map(shards, mesh=cube, in_specs=in_specs, out_specs=out_specs, check_vma=False)
```

time: 1550 us -> 806 us (0.52)
  waiting for transfers between devices: 1100 us -> 261 us
  local copies, waits for them, and re-layouts: 78.8 us -> 147 us
  starting transfers between devices: 1.1 us -> 62.8 us
  matrix products: 184 us -> 141 us
  Pallas kernels: 0 us -> 32.7 us
  other arithmetic: 115 us -> 87.3 us
    reduce_scatter x9 -> x4, waiting for transfers between devices: 612 us -> 67.4 us  [scatter_outer(): return lax.psum_scatter(values, 'outer', scatter_dimension=0, tiled=True)]
    all_gather x9 -> x4, waiting for transfers between devices: 485 us -> 0.01 us  [gather_outer(): return lax.all_gather(values, 'outer', axis=0, tiled=True)]
    ppermute x0 -> x79, waiting for transfers between devices: none -> 194 us  [swap(): lax.ppermute(values, axis, [(i, i ^ bit) for i in range(lax.axis_size(axi...]
    ppermute x0 -> x79, starting transfers between devices: none -> 62.2 us  [swap(): lax.ppermute(values, axis, [(i, i ^ bit) for i in range(lax.axis_size(axi...]
    dot_general x29 -> x16, matrix products: 184 us -> 141 us  [the longest x1 19.6 us: shards(): jnp.einsum('rd,rf->df', whole_two, pair_grad, preferred_element_type=jnp....]
    pallas_call x0 -> x2, Pallas kernels: none -> 32.7 us  [the longest x1 24.1 us: attend_backward(): pl.pallas_call(functools.partial(backward_kernel, rows, blocks, heads), o...]
    reshape x1 -> x3, local copies, waits for them, and re-layouts: 3.06 us -> 34.3 us  [the longest x1 12.9 us: shards(): pieces_grad = whole_grad.reshape(whole_grad.shape[0], outer_size, piece)]
    slice x4 -> x22, local copies, waits for them, and re-layouts: 1.6 us -> 19 us  [the longest x8 6.86 us: gather_rows(): cross = [swap(chip[:half], PAIR), swap(pair[half:], CHIP)]]
  transfers between devices with their start and end apart: 18 -> 87, of which waited for: 17 -> 29; matrix products, arithmetic and copies ran while one was open for 12% -> 38% of each run, Pallas kernels for 0% -> 4%
where the time goes in v1:
time: 806 us; the launch traced here: 798 us
  waiting for transfers between devices  261 us (32%)
  local copies, waits for them, and re-layouts  147 us (18%)
  matrix products  141 us (17%)
  other arithmetic  87.3 us (11%)
  starting transfers between devices  62.8 us (8%)
  blocking collectives  41 us (5%)
  Pallas kernels  32.7 us (4%)
  between operations  24.9 us (3%)
    ppermute x79, waiting for transfers between devices, swap(): lax.ppermute(values, axis, [(i, i ^ bit) for i in range(lax.axis_size(axi...  194 us
    reduce_scatter x4, waiting for transfers between devices, scatter_outer(): return lax.psum_scatter(values, 'outer', scatter_dimension=0, tiled=True)  67.4 us
    ppermute x79, starting transfers between devices, swap(): lax.ppermute(values, axis, [(i, i ^ bit) for i in range(lax.axis_size(axi...  62.2 us
    unnamed x202, local copies, waits for them, and re-layouts  56.5 us
    psum x1, blocking collectives, shards(): lax.psum((gain_part, squares), ('outer', 'inner', 'narrow'))  41 us
    pallas_call x1, Pallas kernels, attend_backward(): pl.pallas_call(functools.partial(backward_kernel, rows, blocks, heads), o...  24.1 us
    dot_general x1, matrix products, shards(): jnp.einsum('rd,rf->df', whole_two, pair_grad, preferred_element_type=jnp....  19.6 us
    dot_general x1, matrix products, shards(): jnp.einsum('rd,df->rf', whole_two, full_gateup, preferred_element_type=jn...  19 us
  transfers between devices with their start and end apart: 87, of which 29 were waited for; matrix products, arithmetic and copies ran while one was open for 38% of the time, Pallas kernels for 4%

profile of v1, /device:TPU:0, one launch (start us, length us, event | category | flops | bytes accessed | tf_op | source)
XLA Modules:
  0.0 798.3 jit_solution(12095472153105207150)
XLA Ops:
  42.1 15.1 %collective-permute-done = s32[1]{0:T(128)} collective-permute-done((s32[1]{0:T(128)}, s32[1]{0:T(128)}, u32[]{:S(2)}, u32[]{:S(2)}) %collective-permute-start) | collective-permute-done | bytes 36 | tf_op jit(solution)/shard_map/ppermute | solution.py:34
  99.5 8.1 %fusion.88 = f32[2048,512]{1,0:T(8,128)S(1)} fusion(bf16[2048,2048]{1,0:T(8,128)(2,1)} %constant_dynamic-update-slice_fusion, bf16[2048,512]{1,0:T(8,128)(2,1)} %all-gather.7.cloned.1.call-done), kind=kOutput, calls=%fused_computation.290 | convolution fusion | flops 4294967296 | bytes 14680064 | tf_op jit(solution)/shard_map/rd,dc->rc/dot_general | solution.py:401
  107.7 8.6 %attend_forward.1 = bf16[2,2,2,256,256]{4,3,2,1,0:T(8,128)(2,1)S(1)} custom-call(s32[3]{0:T(128)S(1)} %pad_add_fusion.meta, f32[2,2,2,256,512]{4,3,2,1,0:T(8,128)S(1)} %bitcast.171, f32[2,128]{1,0:T(2,128)S(1)} %slice_bitcast_fusion.4.gains, f32[1024,128]{1,0:T(8,128)S(1)} %pad_maximum_fusion.5.cos_ref, f32[1024,128]{1,0:T(8,128)S(1)} %pad_maximum_fusion.6.sin_ref), custom_call_target="tpu_custom_call" | custom-call | flops 2147483648 | bytes 6291456 | tf_op jit(solution)/shard_map/attend_forward/pallas_call | solution.py:237
  138.7 11.2 %collective-permute-done.40 = bf16[256,2048]{1,0:T(8,128)(2,1)} collective-permute-done((bf16[256,2048]{1,0:T(8,128)(2,1)}, bf16[256,2048]{1,0:T(8,128)(2,1)}, u32[]{:S(2)}, u32[]{:S(2)}) %collective-permute-start.40) | collective-permute-done | bytes 1048608 | tf_op jit(solution)/shard_map/ppermute | solution.py:34
  186.9 8.3 %collective-permute-done.20 = bf16[128,2048]{1,0:T(8,128)(2,1)S(1)} collective-permute-done((bf16[128,2048]{1,0:T(8,128)(2,1)S(1)}, bf16[128,2048]{1,0:T(8,128)(2,1)S(1)}, u32[]{:S(2)}, u32[]{:S(2)}) %collective-permute-start.20) | collective-permute-done | bytes 524320 | tf_op jit(solution)/shard_map/ppermute | solution.py:34
  195.4 10.5 %collective-permute-done.17 = bf16[128,2048]{1,0:T(8,128)(2,1)S(1)} collective-permute-done((bf16[128,2048]{1,0:T(8,128)(2,1)S(1)}, bf16[128,2048]{1,0:T(8,128)(2,1)S(1)}, u32[]{:S(2)}, u32[]{:S(2)}) %collective-permute-start.17) | collective-permute-done | bytes 524320 | tf_op jit(solution)/shard_map/ppermute | solution.py:34
  217.4 18.5 %collective-permute-done.22 = bf16[256,2048]{1,0:T(8,128)(2,1)S(1)} collective-permute-done((bf16[256,2048]{1,0:T(8,128)(2,1)}, bf16[256,2048]{1,0:T(8,128)(2,1)S(1)}, u32[]{:S(2)}, u32[]{:S(2)}) %collective-permute-start.22) | collective-permute-done | bytes 1048608 | tf_op jit(solution)/shard_map/ppermute | solution.py:34
  240.6 12.9 %copy.82 = bf16[2048,2048]{0,1:T(8,128)(2,1)} copy(bf16[2048,2048]{1,0:T(8,128)(2,1)} %constant_dynamic-update-slice_fusion.20) | data formatting | bytes 16777216 | tf_op jit(solution)/shard_map/reshape | solution.py:433
  269.2 19.0 %fusion.89 = f32[2048,1536]{0,1:T(8,128)} fusion(bf16[2048,2048]{1,0:T(8,128)(2,1)} %constant_dynamic-update-slice_fusion.10, bf16[2048,1536]{1,0:T(8,128)(2,1)} %all-gather.9.cloned.1.call-done), kind=kOutput, calls=%fused_computation.291 | convolution fusion | flops 12884901888 | bytes 27262976 | tf_op jit(solution)/shard_map/rd,df->rf/dot_general | solution.py:422
  288.2 16.6 %fusion.2 = (bf16[2048,768]{0,1:T(8,128)(2,1)}, bf16[2048,768]{0,1:T(8,128)(2,1)}, bf16[2048,768]{0,1:T(8,128)(2,1)S(1)}) fusion(f32[2048,1536]{0,1:T(8,128)} %fusion.89, bf16[4,768,512]{2,1,0:T(8,128)(2,1)} %bitcast.198, bf16[2048,4,512]{0,2,1:T(8,128)(2,1)} %bitcast.176), kind=kOutput, calls=%fused_computation.14 | convolution fusion | flops 6466043904 | bytes 33554432 | tf_op jit(solution)/shard_map/rzd,zfd->rf/dot_general | solution.py:435
  316.4 11.5 %convolution_convert_fusion.1 = bf16[1024,2048]{1,0:T(8,128)(2,1)} fusion(bf16[2048,1536]{1,0:T(8,128)(2,1)} %all-gather.9.cloned.1.call-done, bf16[2048,768]{0,1:T(8,128)(2,1)} %get-tuple-element.86, bf16[2048,768]{0,1:T(8,128)(2,1)} %get-tuple-element.85), kind=kOutput, calls=%fused_computation.20 | convolution fusion | flops 6450839552 | bytes 16777216 | tf_op jit(solution)/shard_map/rf,df->rd/dot_general | solution.py:69
  334.0 9.1 %copy.78 = f32[1024,2048]{1,0:T(8,128)} copy(f32[1024,2048]{0,1:T(8,128)} %bitcast.182) | data formatting | bytes 16777216 | tf_op jit(solution)/shard_map/reshape | solution.py:410
  354.4 10.6 %add_convert_fusion.1 = bf16[1024,2048]{1,0:T(8,128)(2,1)S(1)} fusion(bf16[1024,2048]{1,0:T(8,128)(2,1)} %collective-permute-done.49, bf16[2048,1536]{1,0:T(8,128)(2,1)} %all-gather.9.cloned.1.call-done, bf16[2048,768]{0,1:T(8,128)(2,1)} %get-tuple-element.86, bf16[2048,768]{0,1:T(8,128)(2,1)} %get-tuple-element.85), kind=kOutput, calls=%fused_computation.1 | convolution fusion | flops 6455033856 | bytes 20971520 | tf_op jit(solution)/shard_map/rf,df->rd/dot_general | solution.py:70
  372.0 8.6 %convert_bitcast_fusion = bf16[4,768,512]{1,2,0:T(8,128)(2,1)} fusion(bf16[2048,4,512]{0,2,1:T(8,128)(2,1)S(1)} %bitcast.179, bf16[2048,768]{0,1:T(8,128)(2,1)S(1)} %copy-done.82), kind=kOutput, calls=%fused_computation.38 | convolution fusion | flops 6444023808 | bytes 14680064 | tf_op jit(solution)/shard_map/rf,rzd->zfd/dot_general | solution.py:434
  412.2 12.6 %collective-permute-done.55 = bf16[128,2048]{1,0:T(8,128)(2,1)S(1)} collective-permute-done((bf16[128,2048]{1,0:T(8,128)(2,1)S(1)}, bf16[128,2048]{1,0:T(8,128)(2,1)S(1)}, u32[]{:S(2)}, u32[]{:S(2)}) %collective-permute-start.55) | collective-permute-done | bytes 524320 | tf_op jit(solution)/shard_map/ppermute | solution.py:34
  434.1 21.1 %collective-permute-done.57 = bf16[256,2048]{1,0:T(8,128)(2,1)S(1)} collective-permute-done((bf16[256,2048]{1,0:T(8,128)(2,1)S(1)}, bf16[256,2048]{1,0:T(8,128)(2,1)S(1)}, u32[]{:S(2)}, u32[]{:S(2)}) %collective-permute-start.57) | collective-permute-done | bytes 1048608 | tf_op jit(solution)/shard_map/ppermute | solution.py:34
  475.6 12.4 %copy.83 = bf16[2048,2048]{0,1:T(8,128)(2,1)} copy(bf16[2048,2048]{1,0:T(8,128)(2,1)} %constant_dynamic-update-slice_fusion.30) | data formatting | bytes 16777216 | tf_op jit(solution)/shard_map/reshape | solution.py:443
  499.7 24.1 %attend_backward.1 = (bf16[2,2,2,256,512]{4,3,2,1,0:T(8,128)(2,1)S(1)}, f32[2,2,128]{2,1,0:T(2,128)S(1)}) custom-call(s32[3]{0:T(128)S(1)} %copy-done.9, f32[2,2,2,256,512]{4,3,2,1,0:T(8,128)} %bitcast.172, bf16[2,2,2,256,256]{4,3,2,1,0:T(8,128)(2,1)S(1)} %bitcast.173, f32[2,128]{1,0:T(2,128)S(1)} %copy-done.7, f32[1024,128]{1,0:T(8,128)S(1)} %copy-done.5, ...), custom_call_target="tpu_custom_call" | custom-call | flops 5368709120 | bytes 8388608 | tf_op jit(solution)/shard_map/attend_backward/pallas_call | solution.py:272
  523.8 9.5 %convolution_convert_fusion.4 = bf16[2048,512]{1,0:T(8,128)(2,1)} fusion(bf16[2048,2048]{1,0:T(8,128)(2,1)} %constant_dynamic-update-slice_fusion, bf16[2048,512]{1,0:T(8,128)(2,1)S(1)} %bitcast.169), kind=kOutput, calls=%fused_computation.40 | convolution fusion | flops 4296015872 | bytes 12582912 | tf_op jit(solution)/shard_map/rd,rc->dc/dot_general | solution.py:449
  533.4 19.6 %convolution_convert_fusion = bf16[2048,1536]{1,0:T(8,128)(2,1)} fusion(bf16[2048,2048]{1,0:T(8,128)(2,1)} %constant_dynamic-update-slice_fusion.10, bf16[2048,768]{0,1:T(8,128)(2,1)} %get-tuple-element.85, bf16[2048,768]{0,1:T(8,128)(2,1)} %get-tuple-element.86), kind=kOutput, calls=%fused_computation.9 | convolution fusion | flops 12900630528 | bytes 20971520 | tf_op jit(solution)/shard_map/rd,rf->df/dot_general | solution.py:438
  572.6 9.4 %collective-permute-done.78 = bf16[768,256]{1,0:T(8,128)(2,1)} collective-permute-done((bf16[768,256]{1,0:T(8,128)(2,1)}, bf16[768,256]{1,0:T(8,128)(2,1)}, u32[]{:S(2)}, u32[]{:S(2)}) %collective-permute-start.78) | collective-permute-done | bytes 393248 | tf_op jit(solution)/shard_map/ppermute | solution.py:34
  622.4 67.4 %reduce-scatter.9.cloned.1.call-done = bf16[512,1536]{1,0:T(8,128)(2,1)} async-done(((bf16[2048,1536]{1,0:T(8,128)(2,1)}), bf16[512,1536]{1,0:T(8,128)(2,1)}) %reduce-scatter.9.cloned.1.call-update) | async-done | bytes 1572880 | tf_op jit(solution)/shard_map/reduce_scatter | solution.py:342
  717.9 8.8 %stack.138 = f32[14]{0:T(128)S(1)} concatenate(f32[1]{0:T(128)} %bitcast.36, f32[1]{0:T(128)} %bitcast.37, f32[1]{0:T(128)} %bitcast.38, f32[1]{0:T(128)} %bitcast.39, f32[1]{0:T(128)} %bitcast.40, f32[1]{0:T(128)} %bitcast.41, f32[1]{0:T(128)} %bitcast.42, f32[1]{0:T(128)} %bitcast.44, f32[1]{0:T(128)} %bitcast.47, f32[1]{0:T(128)} %bitcast.48, f32[1]{0:T(128)} %bitcast.54, ...), dimensions={0} | concatenate | bytes 112 | tf_op jit(solution)/shard_map/stack | solution.py:492
  726.7 41.0 %all-reduce = (f32[4352]{0:T(1024)S(1)}, f32[14]{0:T(128)S(1)}) all-reduce(f32[4352]{0:T(1024)S(1)} %pad_maximum_fusion.11, f32[14]{0:T(128)S(1)} %stack.138), channel_id=1, replica_groups=mesh['outer'=4,'inner'=2,'narrow'=4] {'outer','inner','narrow'}, use_global_device_ids=true, to_apply=%region_33.34 | all-reduce | flops 4366 | bytes 34928 | tf_op jit(solution)/shard_map/psum | solution.py:510
  (521 shorter events, 379.0 us)
Async XLA Ops:
  7.2 82.4 %all-gather.11.cloned.1.call-start = ((), (), s32[]{:S(2)}) async-start(), calls=%async_computation.10 | async-start | bytes 1310720 | tf_op jit(solution)/shard_map/all_gather | solution.py:338
  16.0 83.6 %all-gather.7.cloned.1.call-start = ((), (), s32[]{:S(2)}) async-start(), calls=%async_computation.4 | async-start | bytes 2621440 | tf_op jit(solution)/shard_map/all_gather | solution.py:338
  27.1 242.0 %all-gather.9.cloned.1.call-start = ((), (), s32[]{:S(2)}) async-start(), calls=%async_computation.5 | async-start | bytes 7864320 | tf_op jit(solution)/shard_map/all_gather | solution.py:338
  30.8 39.6 %collective-permute-start.2 = (bf16[256,2048]{1,0:T(8,128)(2,1)}, bf16[256,2048]{1,0:T(8,128)(2,1)}, u32[]{:S(2)}, u32[]{:S(2)}) collective-permute-start(bf16[256,2048]{1,0:T(8,128)(2,1)} %get-tuple-element.84), channel_id=1, source_target_pairs={{0,4},{4,0},{1,5},{5,1},{2,6},{6,2},{3,7},{7,3},{8,12},{12,8},{9,1... | collective-permute-start | bytes 3145736 | tf_op jit(solution)/shard_map/ppermute | solution.py:34
  31.2 42.0 %collective-permute-start.1 = (bf16[256,2048]{1,0:T(8,128)(2,1)}, bf16[256,2048]{1,0:T(8,128)(2,1)}, u32[]{:S(2)}, u32[]{:S(2)}) collective-permute-start(bf16[256,2048]{1,0:T(8,128)(2,1)} %get-tuple-element.84), channel_id=1, source_target_pairs={{0,2},{1,3},{2,0},{3,1},{4,6},{5,7},{6,4},{7,5},{8,10},{9,11},{10,... | collective-permute-start | bytes 3145736 | tf_op jit(solution)/shard_map/ppermute | solution.py:34
  36.4 33.8 %collective-permute-start.30 = (bf16[256,768]{1,0:T(8,128)(2,1)}, bf16[256,768]{1,0:T(8,128)(2,1)S(1)}, u32[]{:S(2)}, u32[]{:S(2)}) collective-permute-start(bf16[256,768]{1,0:T(8,128)(2,1)} %dynamic-slice_bitcast_fusion.1), channel_id=1, source_target_pairs={{0,4},{4,0},{1,5},{5,1},{2,6},{6,2},{3,7},{7,3},{8,12},{12,8},{9,1... | collective-permute-start | bytes 1179656 | tf_op jit(solution)/shard_map/ppermute | solution.py:34
  76.7 211.5 %all-gather.13.cloned.1.call-start = ((), (), s32[]{:S(2)}) async-start(), calls=%async_computation.11 | async-start | bytes 3932160 | tf_op jit(solution)/shard_map/all_gather | solution.py:338
  135.3 75.9 %collective-permute-start.44 = (bf16[256,2048]{1,0:T(8,128)(2,1)}, bf16[256,2048]{1,0:T(8,128)(2,1)}, u32[]{:S(2)}, u32[]{:S(2)}) collective-permute-start(bf16[256,2048]{1,0:T(8,128)(2,1)} %get-tuple-element.78), channel_id=1, source_target_pairs={{0,1},{1,0},{2,3},{3,2},{4,5},{5,4},{6,7},{7,6},{8,9},{9,8},{10,11... | collective-permute-start | bytes 3145736 | tf_op jit(solution)/shard_map/ppermute | solution.py:34
  135.7 37.2 %collective-permute-start.41 = (bf16[256,2048]{1,0:T(8,128)(2,1)}, bf16[256,2048]{1,0:T(8,128)(2,1)}, u32[]{:S(2)}, u32[]{:S(2)}) collective-permute-start(bf16[256,2048]{1,0:T(8,128)(2,1)} %get-tuple-element.78), channel_id=1, source_target_pairs={{0,4},{4,0},{1,5},{5,1},{2,6},{6,2},{3,7},{7,3},{8,12},{12,8},{9,1... | collective-permute-start | bytes 3145736 | tf_op jit(solution)/shard_map/ppermute | solution.py:34
  138.6 428.2 %reduce-scatter.11.cloned.1.call-start = ((), (), s32[]{:S(2)}) async-start(), calls=%async_computation.9 | async-start | bytes 3932160 | tf_op jit(solution)/shard_map/reduce_scatter | solution.py:342
  151.0 33.0 %collective-permute-start.42 = (bf16[128,2048]{1,0:T(8,128)(2,1)S(1)}, bf16[128,2048]{1,0:T(8,128)(2,1)S(1)}, u32[]{:S(2)}, u32[]{:S(2)}) collective-permute-start(bf16[128,2048]{1,0:T(8,128)(2,1)S(1)} %slice.451), channel_id=1, source_target_pairs={{0,4},{4,0},{1,5},{5,1},{2,6},{6,2},{3,7},{7,3},{8,12},{12,8},{9,1... | collective-permute-start | bytes 1572872 | tf_op jit(solution)/shard_map/ppermute | solution.py:34
  153.2 31.7 %collective-permute-start.18 = (bf16[128,2048]{1,0:T(8,128)(2,1)S(1)}, bf16[128,2048]{1,0:T(8,128)(2,1)S(1)}, u32[]{:S(2)}, u32[]{:S(2)}) collective-permute-start(bf16[128,2048]{1,0:T(8,128)(2,1)S(1)} %copy-done.61), channel_id=1, source_target_pairs={{0,2},{1,3},{2,0},{3,1},{4,6},{5,7},{6,4},{7,5},{8,10},{9,11},{10,... | collective-permute-start | bytes 1572872 | tf_op jit(solution)/shard_map/ppermute | solution.py:34
  162.9 32.3 %collective-permute-start.20 = (bf16[128,2048]{1,0:T(8,128)(2,1)S(1)}, bf16[128,2048]{1,0:T(8,128)(2,1)S(1)}, u32[]{:S(2)}, u32[]{:S(2)}) collective-permute-start(bf16[128,2048]{1,0:T(8,128)(2,1)S(1)} %get-tuple-element.109), channel_id=1, source_target_pairs={{0,4},{4,0},{1,5},{5,1},{2,6},{6,2},{3,7},{7,3},{8,12},{12,8},{9,1... | collective-permute-start | bytes 1572872 | tf_op jit(solution)/shard_map/ppermute | solution.py:34
  217.2 45.8 %collective-permute-start.25 = (bf16[256,2048]{1,0:T(8,128)(2,1)}, bf16[256,2048]{1,0:T(8,128)(2,1)}, u32[]{:S(2)}, u32[]{:S(2)}) collective-permute-start(bf16[256,2048]{1,0:T(8,128)(2,1)} %get-tuple-element.80), channel_id=1, source_target_pairs={{0,1},{1,0},{2,3},{3,2},{4,5},{5,4},{6,7},{7,6},{8,9},{9,8},{10,11... | collective-permute-start | bytes 3145736 | tf_op jit(solution)/shard_map/ppermute | solution.py:34
  354.3 39.3 %collective-permute-start.37 = (bf16[128,2048]{1,0:T(8,128)(2,1)}, bf16[128,2048]{1,0:T(8,128)(2,1)}, u32[]{:S(2)}, u32[]{:S(2)}) collective-permute-start(bf16[128,2048]{1,0:T(8,128)(2,1)} %get-tuple-element.106), channel_id=1, source_target_pairs={{0,2},{1,3},{2,0},{3,1},{4,6},{5,7},{6,4},{7,5},{8,10},{9,11},{10,... | collective-permute-start | bytes 1572872 | tf_op jit(solution)/shard_map/ppermute | solution.py:34
  380.6 209.2 %reduce-scatter.7.cloned.1.call-start = ((), (), s32[]{:S(2)}) async-start(), calls=%async_computation.7 | async-start | bytes 1310720 | tf_op jit(solution)/shard_map/reduce_scatter | solution.py:342
  434.1 36.5 %collective-permute-start.60 = (bf16[256,2048]{1,0:T(8,128)(2,1)S(1)}, bf16[256,2048]{1,0:T(8,128)(2,1)S(1)}, u32[]{:S(2)}, u32[]{:S(2)}) collective-permute-start(bf16[256,2048]{1,0:T(8,128)(2,1)S(1)} %get-tuple-element.75), channel_id=1, source_target_pairs={{0,1},{1,0},{2,3},{3,2},{4,5},{5,4},{6,7},{7,6},{8,9},{9,8},{10,11... | collective-permute-start | bytes 3145736 | tf_op jit(solution)/shard_map/ppermute | solution.py:34
  498.4 92.7 %reduce-scatter.5.cloned.1.call-start = ((), (), s32[]{:S(2)}) async-start(), calls=%async_computation.6 | async-start | bytes 2621440 | tf_op jit(solution)/shard_map/reduce_scatter | solution.py:342
  533.4 156.3 %reduce-scatter.9.cloned.1.call-start = ((), (), s32[]{:S(2)}) async-start(), calls=%async_computation.8 | async-start | bytes 7864320 | tf_op jit(solution)/shard_map/reduce_scatter | solution.py:342
  559.3 37.9 %collective-permute-start.65 = (bf16[1024,2048]{1,0:T(8,128)(2,1)}, bf16[1024,2048]{1,0:T(8,128)(2,1)}, u32[]{:S(2)}, u32[]{:S(2)}) collective-permute-start(bf16[1024,2048]{1,0:T(8,128)(2,1)} %convolution_convert_fusion.2), channel_id=1, source_target_pairs={{0,1},{1,0},{2,3},{3,2},{4,5},{5,4},{6,7},{7,6},{8,9},{9,8},{10,11... | collective-permute-start | bytes 12582920 | tf_op jit(solution)/shard_map/ppermute | solution.py:34
  605.4 87.5 %collective-permute-start.69 = (bf16[128,2048]{1,0:T(8,128)(2,1)}, bf16[128,2048]{1,0:T(8,128)(2,1)}, u32[]{:S(2)}, u32[]{:S(2)}) collective-permute-start(bf16[128,2048]{1,0:T(8,128)(2,1)} %get-tuple-element.94), channel_id=1, source_target_pairs={{0,2},{1,3},{2,0},{3,1},{4,6},{5,7},{6,4},{7,5},{8,10},{9,11},{10,... | collective-permute-start | bytes 1572872 | tf_op jit(solution)/shard_map/ppermute | solution.py:34
  608.5 86.3 %collective-permute-start.68 = (bf16[128,2048]{1,0:T(8,128)(2,1)}, bf16[128,2048]{1,0:T(8,128)(2,1)}, u32[]{:S(2)}, u32[]{:S(2)}) collective-permute-start(bf16[128,2048]{1,0:T(8,128)(2,1)} %get-tuple-element.95), channel_id=1, source_target_pairs={{0,4},{4,0},{1,5},{5,1},{2,6},{6,2},{3,7},{7,3},{8,12},{12,8},{9,1... | collective-permute-start | bytes 1572872 | tf_op jit(solution)/shard_map/ppermute | solution.py:34
  620.4 74.4 %collective-permute-start.67 = (bf16[128,2048]{1,0:T(8,128)(2,1)}, bf16[128,2048]{1,0:T(8,128)(2,1)}, u32[]{:S(2)}, u32[]{:S(2)}) collective-permute-start(bf16[128,2048]{1,0:T(8,128)(2,1)} %get-tuple-element.90), channel_id=1, source_target_pairs={{0,2},{1,3},{2,0},{3,1},{4,6},{5,7},{6,4},{7,5},{8,10},{9,11},{10,... | collective-permute-start | bytes 1572872 | tf_op jit(solution)/shard_map/ppermute | solution.py:34
  621.6 71.8 %collective-permute-start.71 = (bf16[128,2048]{1,0:T(8,128)(2,1)}, bf16[128,2048]{1,0:T(8,128)(2,1)}, u32[]{:S(2)}, u32[]{:S(2)}) collective-permute-start(bf16[128,2048]{1,0:T(8,128)(2,1)} %get-tuple-element.91), channel_id=1, source_target_pairs={{0,4},{4,0},{1,5},{5,1},{2,6},{6,2},{3,7},{7,3},{8,12},{12,8},{9,1... | collective-permute-start | bytes 1572872 | tf_op jit(solution)/shard_map/ppermute | solution.py:34
  (148 other events, 2168.7 us)
Sparse Core Ops, SparseCore 0:
  16.1 29.8 all-gather.10
  48.2 45.4 all-gather.6
  95.8 114.0 all-gather.8
  211.9 61.7 all-gather.12
  380.8 59.7 reduce-scatter.10
  498.5 27.0 reduce-scatter.6
  533.5 43.7 reduce-scatter.4
  579.6 110.0 reduce-scatter.8

commit v2 on v1

--- a/solution.py
+++ b/solution.py
@@ -23,59 +23,100 @@
 LEARN = 0.5
 
 SCALE = HD ** (-0.5)
+LIGHT = pl.CostEstimate(flops=1024, transcendentals=0, bytes_accessed=1024)
 
 CHIP = ("narrow", 2)
 CORE = ("narrow", 1)
 PAIR = ("inner", 1)
 
 
+def named(name, function, *operands):
+    with jax.named_scope(name):
+        return function(*operands)
+
+
 def swap(values, link):
     axis, bit = link
     return lax.ppermute(values, axis, [(i, i ^ bit) for i in range(lax.axis_size(axis))])
 
 
-def gather_rows(own):
-    half = own.shape[0] // 2
-    chip = swap(own, CHIP)
-    pair = swap(own, PAIR)
-    cross = [swap(chip[:half], PAIR), swap(pair[half:], CHIP)]
-    near = [own, chip, pair, *cross]
-    return jnp.concatenate(near + [swap(block, CORE) for block in near], 0)
-
-
-def scatter_rows(near, far_low):
-    rows = near.shape[0] // 4
+def together(*values):
+    return lax.optimization_barrier(values)
+
+
+def gather_start(own):
+    return together(swap(own, CHIP), swap(own, PAIR))
+
+
+def gather_cross(chip, pair, split):
+    if not split:
+        return [swap(pair, CHIP)]
+    half = pair.shape[0] // 2
+    return [swap(chip[:half], PAIR), swap(pair[half:], CHIP)]
+
+
+def gather_end(near):
+    return list(near) + [swap(block, CORE) for block in near]
+
+
+def partial_rows(left, right):
+    rows = left.shape[0] // 8
+    wide = jnp.float32
+    low = jnp.bfloat16
+
+    def part(first, last):
+        return lax.dot_general(
+            left[first * rows : last * rows],
+            right,
+            (((1,), (1,)), ((), ())),
+            preferred_element_type=wide,
+        )
+
+    cross_far, left = together(part(7, 8).astype(low), left)
+    cross_far, rest_far = together(swap(cross_far, CORE), part(4, 7).astype(low))
+    rest_far = swap(rest_far, CORE)
+    cross = (part(3, 4) + cross_far.astype(wide)).astype(low)
+    return (cross, part(0, 3) + rest_far.astype(wide))
+
+
+def scatter_cross(cross):
+    half = cross.shape[0] // 2
+    return together(swap(cross[:half], PAIR), swap(cross[half:], CHIP))
+
+
+def scatter_near(rest, from_pair, from_chip):
+    rows = rest.shape[0] // 3
     half = rows // 2
-    part = (near + swap(far_low, CORE).astype(jnp.float32)).astype(jnp.bfloat16)
-    own, chip, pair, cross = (part[i * rows : (i + 1) * rows] for i in range(4))
-    from_pair = swap(cross[:half], PAIR)
-    from_chip = swap(cross[half:], CHIP)
-    chip_late = swap(chip[half:], CHIP)
-    pair_early = swap(pair[:half], PAIR)
     wide = jnp.float32
-    chip_early = swap((chip[:half].astype(wide) + from_pair.astype(wide)).astype(jnp.bfloat16), CHIP)
-    pair_late = swap((pair[half:].astype(wide) + from_chip.astype(wide)).astype(jnp.bfloat16), PAIR)
-    return own.astype(wide) + jnp.concatenate(
-        [
-            chip_early.astype(wide) + pair_early.astype(wide),
-            chip_late.astype(wide) + pair_late.astype(wide),
-        ],
-        0,
-    )
-
-
-def product_rows(form, left, right):
-    rows = left.shape[0] // 2
-    far = jnp.einsum(form, left[rows:], right, preferred_element_type=jnp.float32)
-    near = jnp.einsum(form, left[:rows], right, preferred_element_type=jnp.float32)
-    return scatter_rows(near, far.astype(jnp.bfloat16))
-
-
-def halves(values, axis):
+    low = jnp.bfloat16
+    zero = jnp.float32(0.0)
+    low_half = ((0, half, 0), (0, 0, 0))
+    high_half = ((half, 0, 0), (0, 0, 0))
+    chip = (rest[rows : 2 * rows] + lax.pad(from_pair.astype(wide), zero, low_half)).astype(low)
+    pair = (rest[2 * rows :] + lax.pad(from_chip.astype(wide), zero, high_half)).astype(low)
+    return (rest[:rows].astype(low), swap(chip, CHIP), swap(pair, PAIR))
+
+
+def three(own, chip, pair):
+    return own.astype(jnp.float32) + chip.astype(jnp.float32) + pair.astype(jnp.float32)
+
+
+def product_rows(left, right):
+    cross, rest = partial_rows(left, right)
+    return three(*scatter_near(rest, *scatter_cross(cross)))
+
+
+def product_first(left, right):
+    return lax.dot_general(
+        left, right, (((0,), (0,)), ((), ())), preferred_element_type=jnp.float32
+    ).astype(jnp.bfloat16)
+
+
+def halves(values):
     place = lax.axis_index("inner")
-    size = values.shape[axis] // 2
-    mine = lax.dynamic_slice_in_dim(values, place * size, size, axis)
-    theirs = lax.dynamic_slice_in_dim(values, (1 - place) * size, size, axis)
+    size = values.shape[1] // 2
+    mine = lax.dynamic_slice_in_dim(values, place * size, size, 1)
+    theirs = lax.dynamic_slice_in_dim(values, (1 - place) * size, size, 1)
     return (mine, theirs)
 
 
@@ -84,9 +125,227 @@
     return jnp.concatenate([jnp.where(first, mine, theirs), jnp.where(first, theirs, mine)], axis)
 
 
-def trade(values, cut, join):
-    mine, theirs = halves(values, cut)
-    return in_order(mine, swap(theirs, PAIR), join)
+def pair_weights(parts):
+    cut = [halves(part) for part in parts]
+    mine = jnp.concatenate([mine for mine, _ in cut], 1)
+    theirs = jnp.concatenate([theirs for _, theirs in cut], 1)
+    return (mine, theirs)
+
+
+def gather_weights(mine, theirs):
+    return gather_outer(in_order(mine, theirs, 0))
+
+
+def own_grads(values):
+    rows = values.shape[0] // 2
+    place = lax.axis_index("inner")
+    mine = lax.dynamic_slice_in_dim(values, place * rows, rows, 0)
+    return (mine, swap(lax.dynamic_slice_in_dim(values, (1 - place) * rows, rows, 0), PAIR))
+
+
+def total(values):
+    for axis in ("narrow", "inner", "outer"):
+        bit = 1
+        while bit < lax.axis_size(axis):
+            values = values + swap(values, (axis, bit))
+            bit *= 2
+    return values
+
+
+def places_of(blocks, count):
+    half = blocks.shape[1] // 2
+    places = []
+    for side in (0, 4):
+        places += [blocks.at[side], blocks.at[side + 1], blocks.at[side + 2]]
+        if count == 8:
+            places += [blocks.at[side + 3]]
+        else:
+            places += [blocks.at[side + 3, pl.ds(0, half)], blocks.at[side + 3, pl.ds(half, half)]]
+    return places
+
+
+def parts_of(block, count):
+    first = block % 4 + (block // 4) * (count // 2)
+    return range(first, first + (count // 2 - 3 if block % 4 == 3 else 1))
+
+
+def join_kernel(*refs):
+    count = len(refs) - 4
+    pieces = refs[:count]
+    joined, blocks, arrive, leave = refs[count:]
+    places = places_of(blocks, count)
+    arrivals = [pltpu.make_async_copy(pieces[i], places[i], arrive.at[i]) for i in range(count)]
+    departures = [pltpu.make_async_copy(blocks.at[i], joined.at[i], leave.at[i]) for i in range(8)]
+    for copy in arrivals:
+        copy.start()
+    for block in range(8):
+        for index in parts_of(block, count):
+            arrivals[index].wait()
+        departures[block].start()
+    for copy in departures:
+        copy.wait()
+
+
+def join(pieces):
+    rows, depth = pieces[0].shape
+    anywhere = pl.BlockSpec(memory_space=pltpu.HBM)
+    return pl.pallas_call(
+        join_kernel,
+        out_shape=jax.ShapeDtypeStruct((8, rows, depth), jnp.bfloat16),
+        in_specs=[anywhere] * len(pieces),
+        out_specs=anywhere,
+        scratch_shapes=[
+            pltpu.VMEM((8, rows, depth), jnp.bfloat16),
+            pltpu.SemaphoreType.DMA((len(pieces),)),
+            pltpu.SemaphoreType.DMA((8,)),
+        ],
+        cost_estimate=LIGHT,
+        name="join",
+    )(*pieces).reshape(8 * rows, depth)
+
+
+def rows_kernel(finish, count, extra, results, *refs):
+    pieces = refs[:count]
+    weights = refs[count : count + extra]
+    outputs = refs[count + extra : count + extra + results]
+    joined, *beside, blocks, arrive, leave = refs[count + extra + results :]
+    step = pl.program_id(0)
+    places = places_of(blocks, count)
+
+    def arrival(index):
+        return pltpu.make_async_copy(pieces[index], places[index], arrive.at[index])
+
+    def departure(block):
+        return pltpu.make_async_copy(blocks.at[block], joined.at[block], leave.at[block])
+
+    def beside_copies():
+        if not beside:
+            return []
+        width = weights[0].shape[1]
+        return [
+            pltpu.make_async_copy(weight, beside[0].at[:, pl.ds(i * width, width)], leave.at[8 + i])
+            for i, weight in enumerate(weights)
+        ]
+
+    @pl.when(step == 0)
+    def _():
+        for index in range(count):
+            arrival(index).start()
+        for copy in beside_copies():
+            copy.start()
+
+    for block in range(8):
+
+        @pl.when(step == block)
+        def _(block=block):
+            for index in parts_of(block, count):
+                arrival(index).wait()
+            departure(block).start()
+
+    finish(blocks[step], weights, (), outputs)
+
+    @pl.when(step == 7)
+    def _():
+        for block in range(8):
+            departure(block).wait()
+        for copy in beside_copies():
+            copy.wait()
+
+
+def rows_call(name, finish, pieces, weights, widths, kinds, columns=None, place=0):
+    rows, depth = pieces[0].shape
+    columns = columns or weights[0].shape[1]
+    beside = (depth, len(weights) * columns)
+
+    def block(width):
+        return pl.BlockSpec((None, rows, width), lambda i: (i, 0, 0))
+
+    anywhere = pl.BlockSpec(memory_space=pltpu.HBM)
+    more = len(weights) > 1
+    results = pl.pallas_call(
+        functools.partial(rows_kernel, finish, len(pieces), len(weights), len(widths)),
+        out_shape=tuple(
+            jax.ShapeDtypeStruct((8, rows, width), kind) for width, kind in zip(widths, kinds)
+        )
+        + (jax.ShapeDtypeStruct((8, rows, depth), jnp.bfloat16),)
+        + (jax.ShapeDtypeStruct(beside, jnp.bfloat16),) * more,
+        grid=(8,),
+        in_specs=[anywhere] * len(pieces)
+        + [pl.BlockSpec((depth, columns), lambda i: (0, place), pipeline_mode=pl.Buffered(1))]
+        * len(weights),
+        out_specs=tuple(block(width) for width in widths) + (anywhere,) * (1 + more),
+        scratch_shapes=[
+            pltpu.VMEM((8, rows, depth), jnp.bfloat16),
+            pltpu.SemaphoreType.DMA((len(pieces),)),
+            pltpu.SemaphoreType.DMA((8 + len(weights),)),
+        ],
+        cost_estimate=LIGHT,
+        name=name,
+    )(*pieces, *weights)
+    count = len(widths) + 1
+    return [result.reshape(8 * rows, result.shape[-1]) for result in results[:count]] + list(results[count:])
+
+
+def blocks_kernel(finish, left, weight, *refs):
+    finish(left[...], (weight,), refs[:-1], refs[-1:])
+
+
+def blocks_call(name, finish, left, weight, operands, width, rows):
+    depth, columns = weight.shape
+    count = left.shape[0] // rows
+
+    def block(size):
+        return pl.BlockSpec((rows, size), lambda i: (i, 0))
+
+    return pl.pallas_call(
+        functools.partial(blocks_kernel, finish),
+        out_shape=jax.ShapeDtypeStruct((left.shape[0], width), jnp.bfloat16),
+        grid=(count,),
+        in_specs=[block(depth), pl.BlockSpec(weight.shape, lambda i: (0, 0), pipeline_mode=pl.Buffered(1))]
+        + [block(operand.shape[1]) for operand in operands],
+        out_specs=block(width),
+        cost_estimate=LIGHT,
+        name=name,
+    )(left, weight, *operands)
+
+
+def product(left, right):
+    return jnp.dot(left, right, preferred_element_type=jnp.float32)
+
+
+def plain_finish(left, weights, operands, outputs):
+    outputs[0][...] = product(left, weights[0][...]).astype(outputs[0].dtype)
+
+
+def tiles_of(size):
+    return [slice(start, start + 256) for start in range(0, size, 256)]
+
+
+def gate_finish(left, weights, operands, outputs):
+    both, hidden = outputs
+    size = hidden.shape[1]
+    for tile in tiles_of(size):
+        up_tile = slice(size + tile.start, size + tile.stop)
+        gate_val = product(left, weights[0][:, tile])
+        up_val = product(left, weights[1][:, tile])
+        both[:, tile] = gate_val.astype(both.dtype)
+        both[:, up_tile] = up_val.astype(both.dtype)
+        hidden[:, tile] = (gate_val * jax.nn.sigmoid(gate_val) * up_val).astype(hidden.dtype)
+
+
+def hidden_finish(left, weights, operands, outputs):
+    (both,) = operands
+    (grads,) = outputs
+    size = both.shape[1] // 2
+    for tile in tiles_of(size):
+        up_tile = slice(size + tile.start, size + tile.stop)
+        hidden_grad = product(left, weights[0][:, tile])
+        gate_val = both[:, tile].astype(jnp.float32)
+        up_val = both[:, up_tile].astype(jnp.float32)
+        sigmoid = jax.nn.sigmoid(gate_val)
+        slope = sigmoid * (1.0 + gate_val * (1.0 - sigmoid))
+        grads[:, tile] = (hidden_grad * up_val * slope).astype(grads.dtype)
+        grads[:, up_tile] = (hidden_grad * (gate_val * sigmoid)).astype(grads.dtype)
 
 
 def rope_tables(length):
@@ -233,7 +492,6 @@
     rows = raw.shape[0] // 8
     blocks = length // rows
     heads = raw.shape[1] // HD - 2
-    pairs = 2 * heads * length * length
     result = pl.pallas_call(
         functools.partial(forward_kernel, rows, blocks, heads),
         out_shape=jax.ShapeDtypeStruct((2, 2, 2, rows, heads * HD), jnp.bfloat16),
@@ -253,10 +511,7 @@
                 pltpu.VMEM((length, HD), jnp.bfloat16),
             ],
         ),
-        compiler_params=pltpu.CompilerParams(vmem_limit_bytes=40 << 20),
-        cost_estimate=pl.CostEstimate(
-            flops=4 * pairs * HD, transcendentals=pairs, bytes_accessed=raw.size * 6
-        ),
+        cost_estimate=LIGHT,
         name="attend_forward",
     )(meta, split_rows(raw, rows), gains, cos_table, sin_table)
     return result.reshape(8 * rows, heads * HD)
@@ -268,7 +523,6 @@
     blocks = length // rows
     width = raw.shape[1]
     heads = width // HD - 2
-    pairs = 2 * heads * length * length
     raw_grad, gain_grad = pl.pallas_call(
         functools.partial(backward_kernel, rows, blocks, heads),
         out_shape=(
@@ -298,10 +552,7 @@
                 pltpu.VMEM((heads, length, HD), jnp.float32),
             ],
         ),
-        compiler_params=pltpu.CompilerParams(vmem_limit_bytes=48 << 20),
-        cost_estimate=pl.CostEstimate(
-            flops=10 * pairs * HD, transcendentals=pairs, bytes_accessed=raw.size * 8
-        ),
+        cost_estimate=LIGHT,
         name="attend_backward",
     )(meta, split_rows(raw, rows), split_rows(context_grad, rows), gains, cos_table, sin_table)
     return (raw_grad.reshape(8 * rows, width), jnp.sum(gain_grad, 0))
@@ -316,18 +567,188 @@
     )
 
 
-def adam_step(gradient, moment_one, moment_two, master):
+def moments(gradient, moment_one, moment_two):
     new_one = BETA_ONE * moment_one + (1.0 - BETA_ONE) * gradient
     new_two = BETA_TWO * moment_two + (1.0 - BETA_TWO) * gradient * gradient
-    update = (
+    return (new_one, new_two)
+
+
+def update_of(new_one, new_two, master):
+    return (
         new_one / (1.0 - BETA_ONE**STEP) / (jnp.sqrt(new_two / (1.0 - BETA_TWO**STEP)) + ADAM_EPS)
         + DECAY * master
     )
-    return (new_one, new_two, update)
 
 
 def square(values):
-    return jnp.sum(values * values)
+    return jnp.sum(jnp.sum(values * values, 1, keepdims=True), 0, keepdims=True)
+
+
+def step_part(gradient, span, arrays, results):
+    one, two, master = (array[span].reshape(gradient.shape) for array in arrays)
+    new_one, new_two = moments(gradient, one, two)
+    results[0][span] = new_one.reshape(results[0][span].shape)
+    results[1][span] = new_two.reshape(results[1][span].shape)
+    return (square(master), square(update_of(new_one, new_two, master)))
+
+
+def put_sums(sums, pairs, first):
+    row = lax.broadcasted_iota(jnp.int32, sums.shape, 0)
+    tile = jnp.zeros(sums.shape, jnp.float32)
+    for index, value in enumerate(pairs):
+        tile = jnp.where(row == index, value, tile)
+    sums[...] = tile + jnp.where(first, 0.0, sums[...])
+
+
+def add_pairs(left, right):
+    return (left[0] + right[0], left[1] + right[1])
+
+
+def stacked_step(meta, mine, other, one, two, master, new_one, new_two, sums):
+    step = pl.program_id(0)
+    size = one.shape[2]
+    pairs = []
+    for side in range(2):
+        columns = slice(side * size, (side + 1) * size)
+        own = step == meta[0]
+        gradient = jnp.where(own, mine[:, columns], other[:, columns]).astype(jnp.float32)
+        pairs += step_part(gradient, (side,), (one, two, master), (new_one, new_two))
+    put_sums(sums, pairs, step == 0)
+
+
+def turned_step(meta, mine, other, one, two, master, new_one, new_two, sums):
+    step = pl.program_id(0)
+    gradient = jnp.where(step == meta[0], mine[...], other[...]).astype(jnp.float32).T
+    pair = step_part(gradient, (slice(None),), (one, two, master), (new_one, new_two))
+    put_sums(sums, pair, step == 0)
+
+
+def attn_step(
+    meta, mine, other, query_one, query_two, query, keyval_one, keyval_two, keyval,
+    output_one, output_two, output, new_query_one, new_query_two, new_keyval_one, new_keyval_two,
+    new_output_one, new_output_two, sums,
+):
+    step = pl.program_id(0)
+    own = step == meta[0]
+    width = query.shape[1]
+    key_width = keyval.shape[2]
+
+    def part(first, size):
+        columns = slice(first, first + size)
+        return jnp.where(own, mine[:, columns], other[:, columns]).astype(jnp.float32)
+
+    whole_span = (slice(None),)
+    pairs = []
+    pairs += step_part(part(0, width), whole_span, (query_one, query_two, query), (new_query_one, new_query_two))
+    for side in range(2):
+        pairs += step_part(
+            part(width + side * key_width, key_width), (side,),
+            (keyval_one, keyval_two, keyval), (new_keyval_one, new_keyval_two),
+        )
+    pairs += step_part(
+        part(width + 2 * key_width, mine.shape[1] - width - 2 * key_width).T, whole_span,
+        (output_one, output_two, output), (new_output_one, new_output_two),
+    )
+    put_sums(sums, pairs, step == 0)
+
+
+def half_block(array, axis):
+    shape = tuple(size // 2 if place == axis else size for place, size in enumerate(array.shape))
+    return pl.BlockSpec(shape, lambda i, meta: tuple(i if place == axis else 0 for place in range(len(shape))))
+
+
+def step_call(name, kernel, place, mine, other, arrays, axes):
+    fixed = pl.BlockSpec(mine.shape, lambda i, meta: (0, 0))
+    specs = [half_block(array, axis) for group, axis in zip(arrays, axes) for array in group]
+    out_arrays = [(array, axis) for group, axis in zip(arrays, axes) for array in group[:2]]
+    size = sum(array.size for group in arrays for array in group)
+    return pl.pallas_call(
+        kernel,
+        out_shape=tuple(jax.ShapeDtypeStruct(array.shape, jnp.float32) for array, _ in out_arrays)
+        + (jax.ShapeDtypeStruct((8, HD), jnp.float32),),
+        grid_spec=pltpu.PrefetchScalarGridSpec(
+            num_scalar_prefetch=1,
+            grid=(2,),
+            in_specs=[fixed, fixed] + specs,
+            out_specs=tuple(half_block(array, axis) for array, axis in out_arrays)
+            + (pl.BlockSpec((8, HD), lambda i, meta: (0, 0)),),
+        ),
+        cost_estimate=pl.CostEstimate(flops=8 * size, transcendentals=0, bytes_accessed=7 * size),
+        name=name,
+    )(place, mine, other, *[array for group in arrays for array in group])
+
+
+def ratio_of(weight_square, update_square):
+    return jnp.sqrt(weight_square) / jnp.sqrt(update_square)
+
+
+def apply_kernel(parts, axes, *refs):
+    sums = refs[0]
+    index = 1
+    count = len(parts)
+    for place, rows in enumerate(parts):
+        one, two, master = refs[1 + 3 * place : 4 + 3 * place]
+        result = refs[1 + 3 * count + place]
+        for side, row in enumerate(rows):
+            span = (side,) if len(rows) > 1 else (slice(None),)
+            trust = ratio_of(sums[row : row + 1, 0:1], sums[row + 1 : row + 2, 0:1])
+            old = master[span]
+            result[span] = old - LEARN * trust * update_of(one[span], two[span], old)
+
+
+def apply_call(name, sums, arrays, parts, axes, steps):
+    def block(array, axis):
+        shape = tuple(size // steps if place == axis else size for place, size in enumerate(array.shape))
+        return pl.BlockSpec(shape, lambda i: tuple(i if place == axis else 0 for place in range(len(shape))))
+
+    size = sum(array.size for group in arrays for array in group)
+    return pl.pallas_call(
+        functools.partial(apply_kernel, parts, axes),
+        out_shape=tuple(jax.ShapeDtypeStruct(group[2].shape, jnp.float32) for group in arrays),
+        grid=(steps,),
+        in_specs=[pl.BlockSpec(sums.shape, lambda i: (0, 0))]
+        + [block(array, axis) for group, axis in zip(arrays, axes) for array in group],
+        out_specs=tuple(block(group[2], axis) for group, axis in zip(arrays, axes)),
+        cost_estimate=pl.CostEstimate(flops=8 * size, transcendentals=0, bytes_accessed=6 * size),
+        name=name,
+    )(sums, *[array for group in arrays for array in group])
+
+
+def gains_kernel(rows, late, early, first, second, gains, new_first, new_second, new_gains, stats, trust):
+    each = (rows - 2) // 2
+    new_one, new_two = moments(late[:rows, :], first[:rows, :], second[:rows, :])
+    for result, values in ((new_first, new_one), (new_second, new_two), (new_gains, new_one)):
+        result[:rows, :] = values
+        result[rows:, :] = jnp.zeros_like(result[rows:, :])
+    lane = lax.broadcasted_iota(jnp.int32, (1, HD), 1)
+    weight_row = jnp.zeros((1, HD), jnp.float32)
+    update_row = jnp.zeros((1, HD), jnp.float32)
+
+    def put(place, weight_square, update_square, weight_row, update_row):
+        return (
+            jnp.where(lane == place, jnp.sqrt(weight_square), weight_row),
+            jnp.where(lane == place, jnp.sqrt(update_square), update_row),
+        )
+
+    for place, start, size in ((0, 0, each), (7, each, each), (4, 2 * each, 1), (5, 2 * each + 1, 1)):
+        span = slice(start, start + size)
+        old = gains[span, :]
+        update = update_of(new_one[span, :], new_two[span, :], old)
+        weight_square, update_square = (square(old), square(update))
+        new_gains[span, :] = old - LEARN * ratio_of(weight_square, update_square) * update
+        weight_row, update_row = put(place, weight_square, update_square, weight_row, update_row)
+    for place, index in ((1, 0), (2, 2), (3, 4), (6, 6)):
+        weight_row, update_row = put(
+            place, late[rows + index : rows + index + 1, 0:1], late[rows + index + 1 : rows + index + 2, 0:1],
+            weight_row, update_row,
+        )
+    for place, index in ((8, 0), (9, 2), (10, 8)):
+        weight_row, update_row = put(
+            place, early[index : index + 1, 0:1], early[index + 1 : index + 2, 0:1], weight_row, update_row
+        )
+    stats[0:1, :] = weight_row[:, :11]
+    stats[1:2, :] = update_row[:, :11]
+    trust[...] = (weight_row / jnp.where(lane < 11, update_row, 1.0))[:, :11]
 
 
 def root_mean(values):
@@ -375,177 +796,177 @@
     head_gains = norm_gains[2 * D :].reshape(2, HD)
     cos_table, sin_table = rope_tables(seq_len)
 
-    attn_pair = jnp.concatenate(
-        [
-            trade(part.astype(low), 1, 0)
-            for part in (query_weight, keyval_weight[0], keyval_weight[1])
-        ],
-        1,
-    )
-    output_pair = trade(output_weight.astype(low), 0, 1)
-    gateup_pair = jnp.concatenate(
-        [trade(gateup_weight[0].astype(low), 1, 0), trade(gateup_weight[1].astype(low), 1, 0)], 1
-    )
-    down_pair = trade(down_weight.astype(low), 0, 1)
-    full_attn = gather_outer(attn_pair)
-    full_output = gather_outer(output_pair[None])
-    full_gateup = gather_outer(gateup_pair)
-    full_down = gather_outer(down_pair[None])
-    piece = output_pair.shape[1]
-    hidden_size = down_pair.shape[0]
-
     residual = tokens[0].astype(jnp.float32)
     inv_one = lax.rsqrt(jnp.mean(residual * residual, -1, keepdims=True) + EPS)
     hat_one = residual * inv_one
-    whole_one = gather_rows((hat_one * gain_one).astype(low))
-    raw = jnp.einsum("rd,dc->rc", whole_one, full_attn, preferred_element_type=jnp.float32)
+    normed = (hat_one * gain_one).astype(low)
+
+    query_half = query_weight.shape[1] // 2
+    key_half = keyval_weight.shape[2] // 2
+    output_half = output_weight.shape[0] // 2
+    hidden_size = down_weight.shape[0] // 2
+    raw_width = query_half + 2 * key_half
+    places = lax.axis_index("narrow") * shard_len + jnp.arange(shard_len, dtype=jnp.int32)
+    valid = (places < lengths[0]).astype(jnp.float32)
+    grad_out = cotangent[0].astype(jnp.float32) * valid[:, None]
+    attn_low = [w.astype(low) for w in (query_weight, keyval_weight[0], keyval_weight[1])]
+    mine, theirs = pair_weights(attn_low + [output_weight.astype(low).T])
+    full_attn = gather_weights(mine, swap(theirs, PAIR))
+
+    chip, pair = named("norm_one", gather_start, normed)
+    gateup_mine, gateup_theirs = pair_weights([part.astype(low) for part in gateup_weight])
+    chip, pair, gateup_theirs = together(chip, pair, gateup_theirs)
+    (cross,) = named("norm_one", gather_cross, chip, pair, False)
+    gateup_pair = in_order(gateup_mine, swap(gateup_theirs, PAIR), 0)
+    full_attn, grad_low = together(full_attn, grad_out.astype(low))
+    cross, gateup_pair = together(cross, gateup_pair)
+    full_gate = gather_outer(gateup_pair[:, :hidden_size])
+    full_up = gather_outer(gateup_pair[:, hidden_size:])
+    grad_chip, grad_pair = named("output_grad", gather_start, grad_low)
+    pieces_one = named("norm_one", gather_end, (normed, chip, pair, cross))
+    raw, whole_one = rows_call(
+        "query_key_value", plain_finish, pieces_one, [full_attn], [raw_width], [jnp.float32], raw_width
+    )
+    down_mine, down_theirs = pair_weights([down_weight.astype(low).T])
+    raw, grad_chip, grad_pair, down_theirs = together(raw, grad_chip, grad_pair, down_theirs)
+    down_pair = in_order(down_mine, swap(down_theirs, PAIR), 0)
     meta = jnp.concatenate(
         [lax.axis_index("narrow").astype(jnp.int32)[None], lengths, swap(lengths, PAIR)]
     )
     context = attend_forward(meta, raw, head_gains, cos_table, sin_table)
-
-    def out_product(left, right):
-        rows = left.shape[0]
-        result = jnp.einsum("rc,zcd->rzd", left, right, preferred_element_type=jnp.float32)
-        return result.reshape(rows, D)
-
-    def rows_out(left, right):
-        rows = left.shape[0] // 2
-        far = out_product(left[rows:], right).astype(low)
-        return scatter_rows(out_product(left[:rows], right), far)
-
-    attn_part = rows_out(context, full_output)
+    context, down_pair = together(context, down_pair)
+    full_down = gather_outer(down_pair)
+
+    full_output = full_attn[:, raw_width:]
+    cross, rest = named("attention_out", partial_rows, context, full_output)
+    moved = named("attention_out", scatter_cross, cross)
+    own, chip, pair = named("attention_out", scatter_near, rest, *moved)
+    own, chip, pair, full_gate = together(own, chip, pair, full_gate)
+    attn_part = three(own, chip, pair)
     middle = residual + attn_part
     inv_two = lax.rsqrt(jnp.mean(middle * middle, -1, keepdims=True) + EPS)
     hat_two = middle * inv_two
-    whole_two = gather_rows((hat_two * gain_two).astype(low))
-    gateup = jnp.einsum("rd,df->rf", whole_two, full_gateup, preferred_element_type=jnp.float32)
-    gate_val = gateup[:, :hidden_size]
-    up_val = gateup[:, hidden_size:]
-    sigmoid = jax.nn.sigmoid(gate_val)
-    swish = gate_val * sigmoid
-    hidden = (swish * up_val).astype(low)
-
-    places = lax.axis_index("narrow") * shard_len + jnp.arange(shard_len, dtype=jnp.int32)
-    valid = (places < lengths[0]).astype(jnp.float32)
-    grad_out = cotangent[0].astype(jnp.float32) * valid[:, None]
-    whole_grad = gather_rows(grad_out.astype(low))
-    pieces_grad = whole_grad.reshape(whole_grad.shape[0], outer_size, piece)
-    down_grad = jnp.einsum("rf,rzd->zfd", hidden, pieces_grad, preferred_element_type=jnp.float32)
-    hidden_grad = jnp.einsum("rzd,zfd->rf", pieces_grad, full_down, preferred_element_type=jnp.float32)
-    slope = sigmoid * (1.0 + gate_val * (1.0 - sigmoid))
-    pair_grad = jnp.concatenate([hidden_grad * up_val * slope, hidden_grad * swish], 1).astype(low)
-    gateup_grad = jnp.einsum("rd,rf->df", whole_two, pair_grad, preferred_element_type=jnp.float32)
-    normed_two = product_rows("rf,df->rd", pair_grad, full_gateup)
+    normed = (hat_two * gain_two).astype(low)
+    chip, pair = named("norm_two", gather_start, normed)
+    cross = named("norm_two", gather_cross, chip, pair, True)
+    *cross, grad_chip, grad_pair = together(*cross, grad_chip, grad_pair)
+    pieces_two = named("norm_two", gather_end, (normed, chip, pair, *cross))
+    grad_cross = named("output_grad", gather_cross, grad_chip, grad_pair, True)
+    pieces_grad = named("output_grad", gather_end, (grad_low, grad_chip, grad_pair, *grad_cross))
+    both, hidden, whole_two, full_gateup = rows_call(
+        "gate_up", gate_finish, pieces_two, [full_gate, full_up], [2 * hidden_size, hidden_size], [low, low]
+    )
+    whole_grad = join(pieces_grad)
+    down_grad = product_first(whole_grad, hidden)
+    full_down, down_grad = together(full_down, down_grad)
+    down_own = scatter_outer(down_grad)
+    pair_grad = blocks_call(
+        "hidden_grad", hidden_finish, whole_grad, full_down, [both], 2 * hidden_size, shard_len
+    )
+    normed_two = named("norm_two_grad", product_rows, pair_grad, full_gateup)
+    gateup_grad = product_first(whole_two, pair_grad)
+    normed_two, gateup_grad = together(normed_two, gateup_grad)
+    gateup_grad, down_own = together(gateup_grad, down_own)
+    gateup_own = scatter_outer(gateup_grad)
     middle_norm, gain_two_grad = norm_back(normed_two, hat_two, inv_two, gain_two)
     middle_grad = grad_out + middle_norm
-    whole_mid = gather_rows(middle_grad.astype(low))
-    pieces_mid = whole_mid.reshape(whole_mid.shape[0], outer_size, piece)
-    output_grad = jnp.einsum("rc,rzd->zcd", context, pieces_mid, preferred_element_type=jnp.float32)
-    context_grad = jnp.einsum(
-        "rzd,zcd->rc", pieces_mid, full_output, preferred_element_type=jnp.float32
-    ).astype(low)
-    attn_low, head_gain_grad = attend_backward(meta, raw, context_grad, head_gains, cos_table, sin_table)
-    attn_grad = jnp.einsum("rd,rc->dc", whole_one, attn_low, preferred_element_type=jnp.float32)
-    normed_one = product_rows("rc,dc->rd", attn_low, full_attn)
+    middle_low = middle_grad.astype(low)
+    chip, pair = named("middle_grad", gather_start, middle_low)
+    cross = named("middle_grad", gather_cross, chip, pair, True)
+    hidden, full_down, middle_low = together(hidden, full_down, middle_low)
+    mlp_cross, mlp_rest = named("mlp_out", partial_rows, hidden, full_down)
+    *cross, mlp_cross, mlp_rest = together(*cross, mlp_cross, mlp_rest)
+    pieces_mid = named("middle_grad", gather_end, (middle_low, chip, pair, *cross))
+    context_grad, whole_mid = rows_call(
+        "context_grad", plain_finish, pieces_mid, [full_attn], [output_half], [low],
+        output_half, raw_width // output_half,
+    )
+    moved = named("mlp_out", scatter_cross, mlp_cross)
+    context_grad, mlp_rest, *moved = together(context_grad, mlp_rest, *moved)
+    mlp_parts = named("mlp_out", scatter_near, mlp_rest, *moved)
+    raw_grad, head_gain_grad = attend_backward(meta, raw, context_grad, head_gains, cos_table, sin_table)
+    attn_grad = jnp.concatenate(
+        [product_first(whole_one, raw_grad), product_first(whole_mid, context)], 1
+    )
+    raw_grad, attn_grad, *mlp_parts = together(raw_grad, attn_grad, *mlp_parts)
+    mlp_part = three(*mlp_parts)
+    attn_grad, gateup_own = together(attn_grad, gateup_own)
+    attn_own = scatter_outer(attn_grad)
+    normed_one = named("norm_one_grad", product_rows, raw_grad, full_attn[:, :raw_width])
     input_norm, gain_one_grad = norm_back(normed_one, hat_one, inv_one, gain_one)
     input_grad = (middle_grad + input_norm).astype(low)
 
-    mlp_part = rows_out(hidden, full_down)
     final = middle + mlp_part
     result = final.astype(low)
     rms_values = jnp.stack([root_mean(attn_part), root_mean(mlp_part), root_mean(final)])[:, None, :]
 
-    down_sum = trade(scatter_outer(down_grad.astype(low))[0], 1, 0).astype(jnp.float32)
-    gateup_own = scatter_outer(gateup_grad.astype(low))
-    gateup_sum = jnp.stack(
-        [trade(gateup_own[:, :hidden_size], 0, 1), trade(gateup_own[:, hidden_size:], 0, 1)]
-    ).astype(jnp.float32)
-    output_sum = trade(scatter_outer(output_grad.astype(low))[0], 1, 0).astype(jnp.float32)
-    attn_own = scatter_outer(attn_grad.astype(low))
-    query_half = query_weight.shape[1] // 2
-    key_half = keyval_weight.shape[2] // 2
-    query_sum = trade(attn_own[:, :query_half], 0, 1).astype(jnp.float32)
-    keyval_sum = jnp.stack(
+    place = lax.axis_index("inner").astype(jnp.int32)[None]
+    down = (down_first, down_second, down_weight)
+    gateup = (gateup_first, gateup_second, gateup_weight)
+    new_down_first, new_down_second, down_sums = step_call(
+        "down_step", turned_step, place, *own_grads(down_own), [down], [0]
+    )
+    new_gateup_first, new_gateup_second, gateup_sums = step_call(
+        "gateup_step", stacked_step, place, *own_grads(gateup_own), [gateup], [2]
+    )
+    early = named("early_sums", total, jnp.concatenate([gateup_sums, down_sums], 0))
+    new_gateup, new_down = apply_call(
+        "gateup_down",
+        early,
         [
-            trade(attn_own[:, query_half : query_half + key_half], 0, 1),
-            trade(attn_own[:, query_half + key_half :], 0, 1),
-        ]
-    ).astype(jnp.float32)
-
-    gain_part = jnp.concatenate([gain_one_grad, gain_two_grad, head_gain_grad.reshape(-1)])
-    new_query_first, new_query_second, query_update = adam_step(
-        query_sum, query_first, query_second, query_weight
-    )
-    new_keyval_first, new_keyval_second, keyval_update = adam_step(
-        keyval_sum, keyval_first, keyval_second, keyval_weight
-    )
-    new_output_first, new_output_second, output_update = adam_step(
-        output_sum, output_first, output_second, output_weight
-    )
-    new_gateup_first, new_gateup_second, gateup_update = adam_step(
-        gateup_sum, gateup_first, gateup_second, gateup_weight
-    )
-    new_down_first, new_down_second, down_update = adam_step(
-        down_sum, down_first, down_second, down_weight
-    )
-    squares = jnp.stack(
+            (new_gateup_first, new_gateup_second, gateup_weight),
+            (new_down_first, new_down_second, down_weight),
+        ],
+        ((0, 2), (8,)),
+        (1, 0),
+        4,
+    )
+    attn_own, new_gateup, new_down = together(attn_own, new_gateup, new_down)
+    attn_arrays = [
+        (query_first, query_second, query_weight),
+        (keyval_first, keyval_second, keyval_weight),
+        (output_first, output_second, output_weight),
+    ]
+    (
+        new_query_first, new_query_second, new_keyval_first, new_keyval_second,
+        new_output_first, new_output_second, attn_sums,
+    ) = step_call("attention_step", attn_step, place, *own_grads(attn_own), attn_arrays, [1, 2, 0])
+    late = jnp.concatenate(
+        [gain_one_grad.reshape(-1, HD), gain_two_grad.reshape(-1, HD), head_gain_grad, attn_sums], 0
+    )
+    late = named("late_sums", total, late)
+    gain_rows = norm_gains.size // HD
+    new_query, new_keyval, new_output = apply_call(
+        "attention",
+        late[gain_rows:],
         [
-            square(query_weight),
-            square(keyval_weight[0]),
-            square(keyval_weight[1]),
-            square(output_weight),
-            square(gateup_weight[0]),
-            square(gateup_weight[1]),
-            square(down_weight),
-            square(query_update),
-            square(keyval_update[0]),
-            square(keyval_update[1]),
-            square(output_update),
-            square(gateup_update[0]),
-            square(gateup_update[1]),
-            square(down_update),
-        ]
-    )
-    gain_total, square_total = lax.psum((gain_part, squares), ("outer", "inner", "narrow"))
-    matrix_norms = jnp.sqrt(square_total)
-    matrix_weight = matrix_norms[:7]
-    matrix_update = matrix_norms[7:]
-    new_gains_first, new_gains_second, gains_update = adam_step(
-        gain_total, gains_first, gains_second, norm_gains
-    )
-    segments = ((0, D), (2 * D, 2 * D + HD), (2 * D + HD, 2 * D + 2 * HD), (D, 2 * D))
-    gain_weight = [jnp.sqrt(square(norm_gains[lower:upper])) for lower, upper in segments]
-    gain_update = [jnp.sqrt(square(gains_update[lower:upper])) for lower, upper in segments]
-
-    def ordered(gain, matrix):
-        return jnp.stack(
-            [gain[0], matrix[0], matrix[1], matrix[2], gain[1], gain[2], matrix[3], gain[3]]
-            + [matrix[4], matrix[5], matrix[6]]
-        )
-
-    weight_norms = ordered(gain_weight, matrix_weight)
-    update_norms = ordered(gain_update, matrix_update)
-    trust = weight_norms / update_norms
-    gain_trust = jnp.concatenate(
-        [
-            jnp.full((D,), 1.0, jnp.float32) * trust[0],
-            jnp.full((D,), 1.0, jnp.float32) * trust[7],
-            jnp.full((HD,), 1.0, jnp.float32) * trust[4],
-            jnp.full((HD,), 1.0, jnp.float32) * trust[5],
-        ]
-    )
-    new_gains = norm_gains - LEARN * gain_trust * gains_update
-    new_query = query_weight - LEARN * trust[1] * query_update
-    new_keyval = (
-        keyval_weight - LEARN * jnp.stack([trust[2], trust[3]])[:, None, None] * keyval_update
-    )
-    new_output = output_weight - LEARN * trust[6] * output_update
-    new_gateup = (
-        gateup_weight - LEARN * jnp.stack([trust[8], trust[9]])[:, None, None] * gateup_update
-    )
-    new_down = down_weight - LEARN * trust[10] * down_update
-    lamb_stats = jnp.stack([weight_norms, update_norms])
+            (new_query_first, new_query_second, query_weight),
+            (new_keyval_first, new_keyval_second, keyval_weight),
+            (new_output_first, new_output_second, output_weight),
+        ],
+        ((0,), (2, 4), (6,)),
+        (0, 1, 0),
+        2,
+    )
+    padded = -(-gain_rows // 8) * 8
+    gain_shape = jax.ShapeDtypeStruct((padded, HD), jnp.float32)
+    new_gains_first, new_gains_second, new_gains, lamb_stats, trust = pl.pallas_call(
+        functools.partial(gains_kernel, gain_rows),
+        out_shape=(gain_shape, gain_shape, gain_shape)
+        + tuple(jax.ShapeDtypeStruct((rows, 11), jnp.float32) for rows in (2, 1)),
+        name="gains",
+    )(
+        late,
+        early,
+        *[
+            jnp.pad(values, (0, (padded - gain_rows) * HD)).reshape(padded, HD)
+            for values in (gains_first, gains_second, norm_gains)
+        ],
+    )
+    new_gains, new_gains_first, new_gains_second = (
+        values.reshape(-1)[: norm_gains.size] for values in (new_gains, new_gains_first, new_gains_second)
+    )
+    trust = trust[0]
     return (
         result[None],
         input_grad[None],

time: 806 us -> 652 us (0.81)
  local copies, waits for them, and re-layouts: 147 us -> 40.5 us
  Pallas kernels: 32.7 us -> 132 us
  matrix products: 141 us -> 92.3 us
  blocking collectives: 41 us -> 0 us
  waiting for transfers between devices: 261 us -> 241 us
  other arithmetic: 87.3 us -> 70.3 us
  between operations: 24.9 us -> 16.1 us
    pallas_call x0 -> x11, Pallas kernels: none -> 95.2 us  [the longest x3 40.5 us: rows_call(): pl.pallas_call(functools.partial(rows_kernel, finish, len(pieces), len(we...]
    reduce_scatter x4 -> x3, waiting for transfers between devices: 67.4 us -> 0.02 us  [scatter_outer(): return lax.psum_scatter(values, 'outer', scatter_dimension=0, tiled=True)]
    dot_general x16 -> x20, matrix products: 141 us -> 92.3 us  [the longest x16 53.5 us: part(): lax.dot_general(left[first * rows:last * rows], right, (((1,), (1,)), (()...]
    unnamed x202 -> x137, local copies, waits for them, and re-layouts: 56.5 us -> 14.7 us
    psum x1 -> x0, blocking collectives: 41 us -> none  [shards(): lax.psum((gain_part, squares), ('outer', 'inner', 'narrow'))]
    ppermute x79 -> x75, waiting for transfers between devices: 194 us -> 234 us  [swap(): lax.ppermute(values, axis, [(i, i ^ bit) for i in range(lax.axis_size(axi...]
    reshape x3 -> x2, local copies, waits for them, and re-layouts: 34.3 us -> 1.23 us  [shards(): jnp.pad(values, (0, (padded - gain_rows) * HD)).reshape(padded, HD)]
    reduce_sum x11 -> x0, other arithmetic: 18.5 us -> none  [square(): return jnp.sum(values * values)]
  transfers between devices with their start and end apart: 87 -> 82, of which waited for: 29 -> 42; matrix products, arithmetic and copies ran while one was open for 38% -> 27% of each run, Pallas kernels for 4% -> 16%
where the time goes in v2:
time: 652 us; the launch traced here: 647 us
  waiting for transfers between devices  241 us (37%)
  Pallas kernels  132 us (20%)
  matrix products  92.3 us (14%)
  other arithmetic  70.3 us (11%)
  starting transfers between devices  54.9 us (8%)
  local copies, waits for them, and re-layouts  40.5 us (6%)
  between operations  16.1 us (2%)
    ppermute x75, waiting for transfers between devices, swap(): lax.ppermute(values, axis, [(i, i ^ bit) for i in range(lax.axis_size(axi...  234 us
    ppermute x75, starting transfers between devices, swap(): lax.ppermute(values, axis, [(i, i ^ bit) for i in range(lax.axis_size(axi...  53.7 us
    dot_general x16, matrix products, part(): lax.dot_general(left[first * rows:last * rows], right, (((1,), (1,)), (()...  53.5 us
    pallas_call x3, Pallas kernels, rows_call(): pl.pallas_call(functools.partial(rows_kernel, finish, len(pieces), len(we...  40.5 us
    dot_general x4, matrix products, product_first(): lax.dot_general(left, right, (((0,), (0,)), ((), ())), preferred_element_...  38.9 us
    pallas_call x1, Pallas kernels, attend_backward(): pl.pallas_call(functools.partial(backward_kernel, rows, blocks, heads), o...  25.6 us
    pallas_call x3, Pallas kernels, step_call(): pl.pallas_call(kernel, out_shape=tuple((jax.ShapeDtypeStruct(array.shape,...  18.5 us
    unnamed x137, local copies, waits for them, and re-layouts  14.7 us
  transfers between devices with their start and end apart: 82, of which 42 were waited for; matrix products, arithmetic and copies ran while one was open for 27% of the time, Pallas kernels for 16%

profile of v2, /device:TPU:0, one launch (start us, length us, event | category | flops | bytes accessed | tf_op | source)
XLA Modules:
  0.0 647.3 jit_solution(11356563970690087219)
XLA Ops:
  12.9 9.1 %collective-permute-done.9 = bf16[256,768]{1,0:T(8,128)(2,1)S(1)} collective-permute-done((bf16[256,768]{1,0:T(8,128)(2,1)S(1)}, bf16[256,768]{1,0:T(8,128)(2,1)S(1)}, u32[]{:S(2)}, u32[]{:S(2)}) %collective-permute-start.9) | collective-permute-done | bytes 393248 | tf_op jit(solution)/shard_map/ppermute | solution.py:40
  34.2 18.4 %collective-permute-done.1.refs_1_ = bf16[256,2048]{1,0:T(8,128)(2,1)} collective-permute-done((bf16[256,2048]{1,0:T(8,128)(2,1)}, bf16[256,2048]{1,0:T(8,128)(2,1)}, u32[]{:S(2)}, u32[]{:S(2)}) %collective-permute-start.1) | collective-permute-done | bytes 1048608 | tf_op jit(solution)/shard_map/norm_one/ppermute | solution.py:40
  56.5 14.5 %collective-permute-done.4 = bf16[256,1536]{1,0:T(8,128)(2,1)S(1)} collective-permute-done((bf16[256,1536]{1,0:T(8,128)(2,1)S(1)}, bf16[256,1536]{1,0:T(8,128)(2,1)S(1)}, u32[]{:S(2)}, u32[]{:S(2)}) %collective-permute-start.4) | collective-permute-done | bytes 786464 | tf_op jit(solution)/shard_map/ppermute | solution.py:40
  95.9 10.5 %query_key_value.1 = (f32[8,256,512]{2,1,0:T(8,128)}, bf16[8,256,2048]{2,1,0:T(8,128)(2,1)}) custom-call(bf16[256,2048]{1,0:T(8,128)(2,1)} %fusion.7.refs_0_, bf16[256,2048]{1,0:T(8,128)(2,1)} %collective-permute-done.1.refs_1_, bf16[256,2048]{1,0:T(8,128)(2,1)} %collective-permute-done.2.refs_2_, bf16[256,2048]{1,0:T(8,128)(2,1)} %collective-permute-done.3.refs_3_, ...), custom_call_target="tpu_custom_call" | custom-call | flops 1024 | bytes 1024 | tf_op jit(solution)/shard_map/query_key_value/pallas_call | solution.py:265
  119.9 10.9 %attend_forward.1 = bf16[2,2,2,256,256]{4,3,2,1,0:T(8,128)(2,1)} custom-call(s32[3]{0:T(128)} %pad_add_fusion.meta, f32[2,2,2,256,512]{4,3,2,1,0:T(8,128)} %bitcast.98, f32[2,128]{1,0:T(2,128)} %slice_bitcast_fusion.3.gains, f32[1024,128]{1,0:T(8,128)} %get-tuple-element.316.cos_ref, f32[1024,128]{1,0:T(8,128)} %get-tuple-element.317.sin_ref), custom_call_target="tpu_custom_call" | custom-call | flops 1024 | bytes 1024 | tf_op jit(solution)/shard_map/attend_forward/pallas_call | solution.py:495
  144.0 11.7 %collective-permute-done.15 = bf16[128,2048]{1,0:T(8,128)(2,1)S(1)} collective-permute-done((bf16[128,2048]{1,0:T(8,128)(2,1)S(1)}, bf16[128,2048]{1,0:T(8,128)(2,1)S(1)}, u32[]{:S(2)}, u32[]{:S(2)}) %collective-permute-start.15) | collective-permute-done | bytes 524320 | tf_op jit(solution)/shard_map/attention_out/ppermute | solution.py:40
  163.1 20.9 %collective-permute-done.17 = bf16[256,2048]{1,0:T(8,128)(2,1)} collective-permute-done((bf16[256,2048]{1,0:T(8,128)(2,1)S(1)}, bf16[256,2048]{1,0:T(8,128)(2,1)}, u32[]{:S(2)}, u32[]{:S(2)}) %collective-permute-start.17) | collective-permute-done | bytes 1048608 | tf_op jit(solution)/shard_map/attention_out/ppermute | solution.py:40
  190.9 19.9 %collective-permute-done.19.refs_1_ = bf16[256,2048]{1,0:T(8,128)(2,1)} collective-permute-done((bf16[256,2048]{1,0:T(8,128)(2,1)S(1)}, bf16[256,2048]{1,0:T(8,128)(2,1)}, u32[]{:S(2)}, u32[]{:S(2)}) %collective-permute-start.19) | collective-permute-done | bytes 1048608 | tf_op jit(solution)/shard_map/norm_two/ppermute | solution.py:40
  231.4 12.9 %collective-permute-done.28.refs_3_ = bf16[128,2048]{1,0:T(8,128)(2,1)} collective-permute-done((bf16[128,2048]{1,0:T(8,128)(2,1)S(1)}, bf16[128,2048]{1,0:T(8,128)(2,1)}, u32[]{:S(2)}, u32[]{:S(2)}) %collective-permute-start.28) | collective-permute-done | bytes 524320 | tf_op jit(solution)/shard_map/output_grad/ppermute | solution.py:40
  245.0 21.1 %gate_up.1 = (bf16[8,256,1536]{2,1,0:T(8,128)(2,1)}, bf16[8,256,768]{2,1,0:T(8,128)(2,1)}, bf16[8,256,2048]{2,1,0:T(8,128)(2,1)}, bf16[2048,1536]{1,0:T(8,128)(2,1)}) custom-call(bf16[256,2048]{1,0:T(8,128)(2,1)} %copy-done.16, bf16[256,2048]{1,0:T(8,128)(2,1)} %collective-permute-done.19.refs_1_, bf16[256,2048]{1,0:T(8,128)(2,1)} %collective-permute-done.20.refs_2_, ...), custom_call_target="tpu_custom_call" | custom-call | flops 1024 | bytes 1024 | tf_op jit(solution)/shard_map/gate_up/pallas_call | solution.py:265
  273.6 11.4 %bitcast_convert_fusion = bf16[2048,768]{1,0:T(8,128)(2,1)} fusion(bf16[8,256,2048]{2,1,0:T(8,128)(2,1)} %join.1, bf16[8,256,768]{2,1,0:T(8,128)(2,1)} %get-tuple-element.167), kind=kOutput, calls=%fused_computation.1 | convolution fusion | flops 6444023808 | bytes 14680064 | tf_op jit(solution)/shard_map/dot_general | solution.py:110
  285.0 14.5 %hidden_grad.1 = bf16[2048,1536]{1,0:T(8,128)(2,1)} custom-call(bf16[2048,2048]{1,0:T(8,128)(2,1)} %bitcast.97, bf16[2048,768]{1,0:T(8,128)(2,1)} %all-gather.11.cloned.1.call-done.weight, bf16[2048,1536]{1,0:T(8,128)(2,1)} %bitcast.102), custom_call_target="tpu_custom_call" | custom-call | flops 1024 | bytes 1024 | tf_op jit(solution)/shard_map/hidden_grad/pallas_call | solution.py:300
  305.0 8.1 %convolution_convert_fusion.4 = bf16[768,2048]{1,0:T(8,128)(2,1)} fusion(bf16[2048,1536]{1,0:T(8,128)(2,1)S(1)} %copy-done.60, bf16[2048,1536]{1,0:T(8,128)(2,1)} %hidden_grad.1), kind=kOutput, calls=%fused_computation.9 | convolution fusion | flops 4833411072 | bytes 11796480 | tf_op jit(solution)/shard_map/norm_two_grad/dot_general | solution.py:68
  320.4 12.5 %collective-permute-done.37 = bf16[128,2048]{1,0:T(8,128)(2,1)S(1)} collective-permute-done((bf16[128,2048]{1,0:T(8,128)(2,1)S(1)}, bf16[128,2048]{1,0:T(8,128)(2,1)S(1)}, u32[]{:S(2)}, u32[]{:S(2)}) %collective-permute-start.37) | collective-permute-done | bytes 524320 | tf_op jit(solution)/shard_map/norm_two_grad/ppermute | solution.py:40
  333.8 8.4 %convert_add_fusion.2 = f32[768,2048]{1,0:T(8,128)S(1)} fusion(bf16[768,2048]{1,0:T(8,128)(2,1)} %collective-permute-done.36, bf16[2048,1536]{1,0:T(8,128)(2,1)} %get-tuple-element.173, bf16[2048,1536]{1,0:T(8,128)(2,1)} %hidden_grad.1), kind=kOutput, calls=%fused_computation.4 | convolution fusion | flops 4834983936 | bytes 18087936 | tf_op jit(solution)/shard_map/norm_two_grad/dot_general | solution.py:68
  346.9 15.8 %convolution_convert_fusion = bf16[2048,1536]{1,0:T(8,128)(2,1)} fusion(bf16[2048,2048]{1,0:T(8,128)(2,1)S(1)} %bitcast.128, bf16[2048,1536]{1,0:T(8,128)(2,1)S(1)} %bitcast.101), kind=kOutput, calls=%fused_computation | convolution fusion | flops 12888047616 | bytes 20971520 | tf_op jit(solution)/shard_map/dot_general | solution.py:110
  391.3 20.2 %collective-permute-done.41.refs_1_ = bf16[256,2048]{1,0:T(8,128)(2,1)S(1)} collective-permute-done((bf16[256,2048]{1,0:T(8,128)(2,1)S(1)}, bf16[256,2048]{1,0:T(8,128)(2,1)S(1)}, u32[]{:S(2)}, u32[]{:S(2)}) %collective-permute-start.41) | collective-permute-done | bytes 1048608 | tf_op jit(solution)/shard_map/middle_grad/ppermute | solution.py:40
  433.4 8.9 %context_grad.1 = (bf16[8,256,256]{2,1,0:T(8,128)(2,1)}, bf16[8,256,2048]{2,1,0:T(8,128)(2,1)}) custom-call(bf16[256,2048]{1,0:T(8,128)(2,1)} %copy-done.20, bf16[256,2048]{1,0:T(8,128)(2,1)} %copy-done.22, bf16[256,2048]{1,0:T(8,128)(2,1)} %copy-done.23, bf16[128,2048]{1,0:T(8,128)(2,1)} %copy-done.40, bf16[128,2048]{1,0:T(8,128)(2,1)} %copy-done.41, ...), custom_call_target="tpu_custom_call" | custom-call | flops 1024 | bytes 1024 | tf_op jit(solution)/shard_map/context_grad/pallas_call | solution.py:265
  443.9 25.6 %attend_backward.1 = (bf16[2,2,2,256,512]{4,3,2,1,0:T(8,128)(2,1)}, f32[2,2,128]{2,1,0:T(2,128)}) custom-call(s32[3]{0:T(128)} %pad_add_fusion.meta, f32[2,2,2,256,512]{4,3,2,1,0:T(8,128)} %bitcast.99, bf16[2,2,2,256,256]{4,3,2,1,0:T(8,128)(2,1)} %bitcast.108, f32[2,128]{1,0:T(2,128)} %slice_bitcast_fusion.3.gains, f32[1024,128]{1,0:T(8,128)} %get-tuple-element.316.cos_ref, ...), custom_call_target="tpu_custom_call" | custom-call | flops 1024 | bytes 1024 | tf_op jit(solution)/shard_map/attend_backward/pallas_call | solution.py:526
  479.0 9.0 %convolution_convert_fusion.5 = bf16[2048,512]{1,0:T(8,128)(2,1)S(1)} fusion(bf16[2048,2048]{1,0:T(8,128)(2,1)} %bitcast.125, bf16[2048,512]{1,0:T(8,128)(2,1)S(1)} %bitcast.113), kind=kOutput, calls=%fused_computation.18 | convolution fusion | flops 4296015872 | bytes 12582912 | tf_op jit(solution)/shard_map/dot_general | solution.py:110
  492.5 8.2 %collective-permute-done.54 = bf16[256,2048]{1,0:T(8,128)(2,1)} collective-permute-done((bf16[256,2048]{1,0:T(8,128)(2,1)}, bf16[256,2048]{1,0:T(8,128)(2,1)}, u32[]{:S(2)}, u32[]{:S(2)}) %collective-permute-start.54) | collective-permute-done | bytes 1048608 | tf_op jit(solution)/shard_map/mlp_out/ppermute | solution.py:40
  543.8 10.7 %collective-permute-done.62.other = bf16[256,1536]{1,0:T(8,128)(2,1)S(1)} collective-permute-done((bf16[256,1536]{1,0:T(8,128)(2,1)S(1)}, bf16[256,1536]{1,0:T(8,128)(2,1)S(1)}, u32[]{:S(2)}, u32[]{:S(2)}) %collective-permute-start.62) | collective-permute-done | bytes 786464 | tf_op jit(solution)/shard_map/ppermute | solution.py:40
  555.4 8.1 %gateup_step.1 = (f32[2,256,1536]{2,1,0:T(8,128)}, f32[2,256,1536]{2,1,0:T(8,128)}, f32[8,128]{1,0:T(8,128)}) custom-call(s32[1]{0:T(128)} %bitcast.38.meta, bf16[256,1536]{1,0:T(8,128)(2,1)} %get-tuple-element.270.mine, bf16[256,1536]{1,0:T(8,128)(2,1)} %copy-done.34, f32[2,256,1536]{2,1,0:T(8,128)} %one.2, f32[2,256,1536]{2,1,0:T(8,128)} %two.2, ...), custom_call_target="tpu_custom_call" | custom-call | flops 18874368 | bytes 16515072 | tf_op jit(solution)/shard_map/gateup_step/pallas_call | solution.py:665
  584.4 9.6 %gateup_down.1 = (f32[2,256,1536]{2,1,0:T(8,128)}, f32[1536,256]{1,0:T(8,128)}) custom-call(f32[16,128]{1,0:T(8,128)} %add.242.refs_0_.early, f32[2,256,1536]{2,1,0:T(8,128)} %get-tuple-element.129.refs_1_, f32[2,256,1536]{2,1,0:T(8,128)} %get-tuple-element.130.refs_2_, f32[2,256,1536]{2,1,0:T(8,128)} %refs_3_.2, f32[1536,256]{1,0:T(8,128)} %get-tuple-element.132.refs_4_, ...), custom_call_target="tpu_custom_call" | custom-call | flops 28311552 | bytes 21233664 | tf_op jit(solution)/shard_map/gateup_down/pallas_call | solution.py:705
  (411 shorter events, 310.4 us)
Async XLA Ops:
  7.2 81.0 %all-gather.5.cloned.1.call-start = ((), (), s32[]{:S(2)}) async-start(), calls=%async_computation.3 | async-start | bytes 3932160 | tf_op jit(solution)/shard_map/all_gather | solution.py:759
  23.1 140.0 %all-gather.7.cloned.1.call-start = ((), (), s32[]{:S(2)}) async-start(), calls=%async_computation.4 | async-start | bytes 3932160 | tf_op jit(solution)/shard_map/all_gather | solution.py:759
  28.0 24.7 %collective-permute-start.1 = (bf16[256,2048]{1,0:T(8,128)(2,1)}, bf16[256,2048]{1,0:T(8,128)(2,1)}, u32[]{:S(2)}, u32[]{:S(2)}) collective-permute-start(bf16[256,2048]{1,0:T(8,128)(2,1)} %fusion.7.refs_0_), channel_id=1, source_target_pairs={{0,2},{1,3},{2,0},{3,1},{4,6},{5,7},{6,4},{7,5},{8,10},{9,11},{10,... | collective-permute-start | bytes 3145736 | tf_op jit(solution)/shard_map/norm_one/ppermute | solution.py:40
  55.8 33.9 %collective-permute-start.5 = (bf16[256,2048]{1,0:T(8,128)(2,1)}, bf16[256,2048]{1,0:T(8,128)(2,1)}, u32[]{:S(2)}, u32[]{:S(2)}) collective-permute-start(bf16[256,2048]{1,0:T(8,128)(2,1)} %fusion.7.refs_0_), channel_id=1, source_target_pairs={{0,1},{1,0},{2,3},{3,2},{4,5},{5,4},{6,7},{7,6},{8,9},{9,8},{10,11... | collective-permute-start | bytes 3145736 | tf_op jit(solution)/shard_map/norm_one/ppermute | solution.py:40
  79.4 165.6 %all-gather.9.cloned.1.call-start = ((), (), s32[]{:S(2)}) async-start(), calls=%async_computation.5 | async-start | bytes 3932160 | tf_op jit(solution)/shard_map/all_gather | solution.py:759
  88.2 25.2 %collective-permute-start.10 = (bf16[256,2048]{1,0:T(8,128)(2,1)}, bf16[256,2048]{1,0:T(8,128)(2,1)}, u32[]{:S(2)}, u32[]{:S(2)}) collective-permute-start(bf16[256,2048]{1,0:T(8,128)(2,1)} %fusion.22.refs_0_), channel_id=1, source_target_pairs={{0,2},{1,3},{2,0},{3,1},{4,6},{5,7},{6,4},{7,5},{8,10},{9,11},{10,... | collective-permute-start | bytes 3145736 | tf_op jit(solution)/shard_map/output_grad/ppermute | solution.py:40
  89.7 24.9 %collective-permute-start.11 = (bf16[256,2048]{1,0:T(8,128)(2,1)}, bf16[256,2048]{1,0:T(8,128)(2,1)}, u32[]{:S(2)}, u32[]{:S(2)}) collective-permute-start(bf16[256,2048]{1,0:T(8,128)(2,1)} %fusion.22.refs_0_), channel_id=1, source_target_pairs={{0,4},{4,0},{1,5},{5,1},{2,6},{6,2},{3,7},{7,3},{8,12},{12,8},{9,1... | collective-permute-start | bytes 3145736 | tf_op jit(solution)/shard_map/output_grad/ppermute | solution.py:40
  139.6 145.4 %all-gather.11.cloned.1.call-start = ((), (), s32[]{:S(2)}) async-start(), calls=%async_computation.6 | async-start | bytes 3932160 | tf_op jit(solution)/shard_map/all_gather | solution.py:759
  190.8 183.8 %reduce-scatter.4.cloned.1.call-start = ((), (), s32[]{:S(2)}) async-start(), calls=%async_computation.7 | async-start | bytes 3932160 | tf_op jit(solution)/shard_map/reduce_scatter | solution.py:763
  190.8 37.4 %collective-permute-start.23 = (bf16[256,2048]{1,0:T(8,128)(2,1)S(1)}, bf16[256,2048]{1,0:T(8,128)(2,1)S(1)}, u32[]{:S(2)}, u32[]{:S(2)}) collective-permute-start(bf16[256,2048]{1,0:T(8,128)(2,1)S(1)} %multiply_convert_fusion.refs_0_), channel_id=1, source_target_pairs={{0,1},{1,0},{2,3},{3,2},{4,5},{5,4},{6,7},{7,6},{8,9},{9,8},{10,11... | collective-permute-start | bytes 3145736 | tf_op jit(solution)/shard_map/norm_two/ppermute | solution.py:40
  229.2 36.9 %collective-permute-start.30 = (bf16[256,2048]{1,0:T(8,128)(2,1)}, bf16[256,2048]{1,0:T(8,128)(2,1)S(1)}, u32[]{:S(2)}, u32[]{:S(2)}) collective-permute-start(bf16[256,2048]{1,0:T(8,128)(2,1)} %fusion.22.refs_0_), channel_id=1, source_target_pairs={{0,1},{1,0},{2,3},{3,2},{4,5},{5,4},{6,7},{7,6},{8,9},{9,8},{10,11... | collective-permute-start | bytes 3145736 | tf_op jit(solution)/shard_map/output_grad/ppermute | solution.py:40
  229.2 36.9 %collective-permute-start.31 = (bf16[256,2048]{1,0:T(8,128)(2,1)}, bf16[256,2048]{1,0:T(8,128)(2,1)}, u32[]{:S(2)}, u32[]{:S(2)}) collective-permute-start(bf16[256,2048]{1,0:T(8,128)(2,1)} %collective-permute-done.10.refs_1_), channel_id=1, source_target_pairs={{0,1},{1,0},{2,3},{3,2},{4,5},{5,4},{6,7},{7,6},{8,9},{9,8},{10,11... | collective-permute-start | bytes 3145736 | tf_op jit(solution)/shard_map/output_grad/ppermute | solution.py:40
  229.8 36.4 %collective-permute-start.32 = (bf16[256,2048]{1,0:T(8,128)(2,1)}, bf16[256,2048]{1,0:T(8,128)(2,1)}, u32[]{:S(2)}, u32[]{:S(2)}) collective-permute-start(bf16[256,2048]{1,0:T(8,128)(2,1)} %collective-permute-done.11.refs_2_), channel_id=1, source_target_pairs={{0,1},{1,0},{2,3},{3,2},{4,5},{5,4},{6,7},{7,6},{8,9},{9,8},{10,11... | collective-permute-start | bytes 3145736 | tf_op jit(solution)/shard_map/output_grad/ppermute | solution.py:40
  313.2 191.4 %reduce-scatter.6.cloned.1.call-start = ((), (), s32[]{:S(2)}) async-start(), calls=%async_computation.8 | async-start | bytes 7864320 | tf_op jit(solution)/shard_map/reduce_scatter | solution.py:763
  345.2 24.8 %collective-permute-start.40 = (bf16[256,2048]{1,0:T(8,128)(2,1)}, bf16[256,2048]{1,0:T(8,128)(2,1)}, u32[]{:S(2)}, u32[]{:S(2)}) collective-permute-start(bf16[256,2048]{1,0:T(8,128)(2,1)} %get-tuple-element.264), channel_id=1, source_target_pairs={{0,4},{4,0},{1,5},{5,1},{2,6},{6,2},{3,7},{7,3},{8,12},{12,8},{9,1... | collective-permute-start | bytes 3145736 | tf_op jit(solution)/shard_map/norm_two_grad/ppermute | solution.py:40
  346.2 24.4 %collective-permute-start.39 = (bf16[256,2048]{1,0:T(8,128)(2,1)S(1)}, bf16[256,2048]{1,0:T(8,128)(2,1)}, u32[]{:S(2)}, u32[]{:S(2)}) collective-permute-start(bf16[256,2048]{1,0:T(8,128)(2,1)S(1)} %get-tuple-element.263), channel_id=1, source_target_pairs={{0,2},{1,3},{2,0},{3,1},{4,6},{5,7},{6,4},{7,5},{8,10},{9,11},{10,... | collective-permute-start | bytes 3145736 | tf_op jit(solution)/shard_map/norm_two_grad/ppermute | solution.py:40
  374.6 219.3 %reduce-scatter.8.cloned.1.call-start = ((), (), s32[]{:S(2)}) async-start(), calls=%async_computation.9 | async-start | bytes 3932160 | tf_op jit(solution)/shard_map/reduce_scatter | solution.py:763
  385.8 27.9 %collective-permute-start.46 = (bf16[768,2048]{1,0:T(8,128)(2,1)S(1)}, bf16[768,2048]{1,0:T(8,128)(2,1)S(1)}, u32[]{:S(2)}, u32[]{:S(2)}) collective-permute-start(bf16[768,2048]{1,0:T(8,128)(2,1)S(1)} %convolution_convert_fusion.2), channel_id=1, source_target_pairs={{0,1},{1,0},{2,3},{3,2},{4,5},{5,4},{6,7},{7,6},{8,9},{9,8},{10,11... | collective-permute-start | bytes 9437192 | tf_op jit(solution)/shard_map/mlp_out/ppermute | solution.py:40
  386.3 25.1 %collective-permute-start.41 = (bf16[256,2048]{1,0:T(8,128)(2,1)S(1)}, bf16[256,2048]{1,0:T(8,128)(2,1)S(1)}, u32[]{:S(2)}, u32[]{:S(2)}) collective-permute-start(bf16[256,2048]{1,0:T(8,128)(2,1)S(1)} %get-tuple-element.182.refs_0_), channel_id=1, source_target_pairs={{0,2},{1,3},{2,0},{3,1},{4,6},{5,7},{6,4},{7,5},{8,10},{9,11},{10,... | collective-permute-start | bytes 3145736 | tf_op jit(solution)/shard_map/middle_grad/ppermute | solution.py:40
  386.9 24.9 %collective-permute-start.42 = (bf16[256,2048]{1,0:T(8,128)(2,1)S(1)}, bf16[256,2048]{1,0:T(8,128)(2,1)S(1)}, u32[]{:S(2)}, u32[]{:S(2)}) collective-permute-start(bf16[256,2048]{1,0:T(8,128)(2,1)S(1)} %get-tuple-element.182.refs_0_), channel_id=1, source_target_pairs={{0,4},{4,0},{1,5},{5,1},{2,6},{6,2},{3,7},{7,3},{8,12},{12,8},{9,1... | collective-permute-start | bytes 3145736 | tf_op jit(solution)/shard_map/middle_grad/ppermute | solution.py:40
  387.7 41.3 %collective-permute-start.47 = (bf16[256,2048]{1,0:T(8,128)(2,1)S(1)}, bf16[256,2048]{1,0:T(8,128)(2,1)S(1)}, u32[]{:S(2)}, u32[]{:S(2)}) collective-permute-start(bf16[256,2048]{1,0:T(8,128)(2,1)S(1)} %get-tuple-element.182.refs_0_), channel_id=1, source_target_pairs={{0,1},{1,0},{2,3},{3,2},{4,5},{5,4},{6,7},{7,6},{8,9},{9,8},{10,11... | collective-permute-start | bytes 3145736 | tf_op jit(solution)/shard_map/middle_grad/ppermute | solution.py:40
  509.3 25.8 %collective-permute-start.57 = (bf16[768,2048]{1,0:T(8,128)(2,1)}, bf16[768,2048]{1,0:T(8,128)(2,1)}, u32[]{:S(2)}, u32[]{:S(2)}) collective-permute-start(bf16[768,2048]{1,0:T(8,128)(2,1)} %convolution_convert_fusion.1), channel_id=1, source_target_pairs={{0,1},{1,0},{2,3},{3,2},{4,5},{5,4},{6,7},{7,6},{8,9},{9,8},{10,11... | collective-permute-start | bytes 9437192 | tf_op jit(solution)/shard_map/norm_one_grad/ppermute | solution.py:40
  542.2 54.6 %collective-permute-start.61 = (bf16[256,2048]{1,0:T(8,128)(2,1)}, bf16[256,2048]{1,0:T(8,128)(2,1)S(1)}, u32[]{:S(2)}, u32[]{:S(2)}) collective-permute-start(bf16[256,2048]{1,0:T(8,128)(2,1)} %get-tuple-element.260), channel_id=1, source_target_pairs={{0,4},{4,0},{1,5},{5,1},{2,6},{6,2},{3,7},{7,3},{8,12},{12,8},{9,1... | collective-permute-start | bytes 3145736 | tf_op jit(solution)/shard_map/norm_one_grad/ppermute | solution.py:40
  543.2 53.6 %collective-permute-start.60 = (bf16[256,2048]{1,0:T(8,128)(2,1)}, bf16[256,2048]{1,0:T(8,128)(2,1)}, u32[]{:S(2)}, u32[]{:S(2)}) collective-permute-start(bf16[256,2048]{1,0:T(8,128)(2,1)} %get-tuple-element.259), channel_id=1, source_target_pairs={{0,2},{1,3},{2,0},{3,1},{4,6},{5,7},{6,4},{7,5},{8,10},{9,11},{10,... | collective-permute-start | bytes 3145736 | tf_op jit(solution)/shard_map/norm_one_grad/ppermute | solution.py:40
  (125 other events, 1506.2 us)
Sparse Core Ops, SparseCore 0:
  23.2 64.9 all-gather.4
  90.4 62.1 all-gather.6
  154.8 62.1 all-gather.8
  218.9 62.1 all-gather.10
  313.3 57.9 reduce-scatter.3
  374.7 109.4 reduce-scatter.5
  504.7 57.4 reduce-scatter.7

commit v3 on v2

--- a/solution.py
+++ b/solution.py
@@ -59,57 +59,177 @@
     return list(near) + [swap(block, CORE) for block in near]
 
 
-def partial_rows(left, right):
+def cross_kernel(left, right, near, far):
+    values = lax.dot_general(
+        left[...], right[...], (((1,), (1,)), ((), ())), preferred_element_type=jnp.float32
+    )
+
+    @pl.when(pl.program_id(0) == 0)
+    def _():
+        far[...] = values.astype(far.dtype)
+
+    @pl.when(pl.program_id(0) == 1)
+    def _():
+        near[...] = values
+
+
+def cross_call(left, right, depth, place):
     rows = left.shape[0] // 8
-    wide = jnp.float32
+    shape = (rows, right.shape[0])
+    return pl.pallas_call(
+        cross_kernel,
+        out_shape=(jax.ShapeDtypeStruct(shape, jnp.float32), jax.ShapeDtypeStruct(shape, jnp.bfloat16)),
+        grid=(2,),
+        in_specs=[
+            pl.BlockSpec((rows, depth), lambda i: (7 - 4 * i, 0)),
+            pl.BlockSpec((right.shape[0], depth), lambda i: (0, place), pipeline_mode=pl.Buffered(1)),
+        ],
+        out_specs=(pl.BlockSpec(shape, lambda i: (0, 0)),) * 2,
+        cost_estimate=LIGHT,
+        name="cross",
+    )(left, right)
+
+
+def part_kernel(left, right, *outs):
+    values = lax.dot_general(
+        left[...], right[...], (((1,), (1,)), ((), ())), preferred_element_type=jnp.float32
+    )
+    for index, out in enumerate(outs):
+
+        @pl.when(pl.program_id(0) == index)
+        def _(out=out):
+            out[...] = values.astype(out.dtype)
+
+
+def near_kernel(left, right, out):
+    out[...] = lax.dot_general(
+        left[...], right[...], (((1,), (1,)), ((), ())), preferred_element_type=jnp.float32
+    )
+
+
+def near_call(left, right, depth, place):
+    rows = left.shape[0] // 8
+    columns = right.shape[0]
+    return pl.pallas_call(
+        near_kernel,
+        out_shape=jax.ShapeDtypeStruct((3 * rows, columns), jnp.float32),
+        grid=(3,),
+        in_specs=[
+            pl.BlockSpec((rows, depth), lambda i: (i, 0)),
+            pl.BlockSpec((columns, depth), lambda i: (0, place), pipeline_mode=pl.Buffered(1)),
+        ],
+        out_specs=pl.BlockSpec((rows, columns), lambda i: (i, 0)),
+        cost_estimate=LIGHT,
+        name="near",
+    )(left, right)
+
+
+def part_call(left, right, depth, place, first, kind):
+    rows = left.shape[0] // 8
+    columns = right.shape[0]
+    return pl.pallas_call(
+        part_kernel,
+        out_shape=(jax.ShapeDtypeStruct((rows, columns), kind),) * 3,
+        grid=(3,),
+        in_specs=[
+            pl.BlockSpec((rows, depth), lambda i: (first + i, 0)),
+            pl.BlockSpec((columns, depth), lambda i: (0, place), pipeline_mode=pl.Buffered(1)),
+        ],
+        out_specs=(pl.BlockSpec((rows, columns), lambda i: (0, 0)),) * 3,
+        cost_estimate=LIGHT,
+        name="part",
+    )(left, right)
+
+
+def partial_rows(left, right, depth, place=0):
     low = jnp.bfloat16
-
-    def part(first, last):
-        return lax.dot_general(
-            left[first * rows : last * rows],
-            right,
-            (((1,), (1,)), ((), ())),
-            preferred_element_type=wide,
-        )
-
-    cross_far, left = together(part(7, 8).astype(low), left)
-    cross_far, rest_far = together(swap(cross_far, CORE), part(4, 7).astype(low))
-    rest_far = swap(rest_far, CORE)
-    cross = (part(3, 4) + cross_far.astype(wide)).astype(low)
-    return (cross, part(0, 3) + rest_far.astype(wide))
+    near_cross, far_cross = cross_call(left, right, depth, place)
+    far_cross, left = together(far_cross, left)
+    rest_far = part_call(left, right, depth, place, 4, low)
+    far_cross, *rest_far = together(swap(far_cross, CORE), *rest_far)
+    cross = (near_cross + far_cross.astype(jnp.float32)).astype(low)
+    near = near_call(left, right, depth, place)
+    return (cross, near, [swap(block, CORE) for block in rest_far])
 
 
 def scatter_cross(cross):
     half = cross.shape[0] // 2
-    return together(swap(cross[:half], PAIR), swap(cross[half:], CHIP))
-
-
-def scatter_near(rest, from_pair, from_chip):
-    rows = rest.shape[0] // 3
-    half = rows // 2
+    return (swap(cross[:half], PAIR), swap(cross[half:], CHIP))
+
+
+def sums_kernel(near_chip, near_pair, far_chip, far_pair, from_pair, from_chip, chip, pair):
     wide = jnp.float32
-    low = jnp.bfloat16
-    zero = jnp.float32(0.0)
-    low_half = ((0, half, 0), (0, 0, 0))
-    high_half = ((half, 0, 0), (0, 0, 0))
-    chip = (rest[rows : 2 * rows] + lax.pad(from_pair.astype(wide), zero, low_half)).astype(low)
-    pair = (rest[2 * rows :] + lax.pad(from_chip.astype(wide), zero, high_half)).astype(low)
-    return (rest[:rows].astype(low), swap(chip, CHIP), swap(pair, PAIR))
-
-
-def three(own, chip, pair):
+    early = pl.program_id(0) < pl.num_programs(0) // 2
+    left = near_chip[...] + far_chip[...].astype(wide)
+    right = near_pair[...] + far_pair[...].astype(wide)
+    chip[...] = jnp.where(early, left + from_pair[...].astype(wide), left).astype(chip.dtype)
+    pair[...] = jnp.where(early, right, right + from_chip[...].astype(wide)).astype(pair.dtype)
+
+
+def near_sums(near, far, from_pair, from_chip):
+    rows, columns = far[1].shape
+    steps = 4
+    half = steps // 2
+    block = (rows // steps, columns)
+    straight = pl.BlockSpec(block, lambda i: (i, 0))
+    return pl.pallas_call(
+        sums_kernel,
+        out_shape=(jax.ShapeDtypeStruct((rows, columns), jnp.bfloat16),) * 2,
+        grid=(steps,),
+        in_specs=[
+            pl.BlockSpec(block, lambda i: (steps + i, 0)),
+            pl.BlockSpec(block, lambda i: (2 * steps + i, 0)),
+            straight,
+            straight,
+        ]
+        + [
+            pl.BlockSpec(block, lambda i: (jnp.minimum(i, half - 1), 0)),
+            pl.BlockSpec(block, lambda i: (jnp.maximum(i - half, 0), 0)),
+        ],
+        out_specs=(straight, straight),
+        cost_estimate=LIGHT,
+        name="sums",
+    )(near, near, far[1], far[2], from_pair, from_chip)
+
+
+def scatter_near(chip, pair):
+    return (swap(chip, CHIP), swap(pair, PAIR))
+
+
+def all_sums(near, far, chip, pair):
+    own = (near[: far[0].shape[0]] + far[0].astype(jnp.float32)).astype(jnp.bfloat16)
     return own.astype(jnp.float32) + chip.astype(jnp.float32) + pair.astype(jnp.float32)
 
 
-def product_rows(left, right):
-    cross, rest = partial_rows(left, right)
-    return three(*scatter_near(rest, *scatter_cross(cross)))
-
-
-def product_first(left, right):
-    return lax.dot_general(
-        left, right, (((0,), (0,)), ((), ())), preferred_element_type=jnp.float32
-    ).astype(jnp.bfloat16)
+def first_kernel(*refs):
+    out = refs[-1]
+    start = 0
+    for left, right in zip(refs[:-1:2], refs[1:-1:2]):
+        span = slice(start, start + right.shape[1])
+        values = lax.dot_general(
+            left[...], right[...], (((0,), (0,)), ((), ())), preferred_element_type=jnp.float32
+        )
+        out[:, span] = values.astype(out.dtype)
+        start = span.stop
+
+
+def product_first(name, *pairs, cost=LIGHT):
+    rows, depth = pairs[0][0].shape
+    columns = sum(right.shape[1] for _, right in pairs)
+    tile = 512
+    specs = []
+    for _, right in pairs:
+        specs.append(pl.BlockSpec((rows, tile), lambda i: (0, i)))
+        specs.append(pl.BlockSpec(right.shape, lambda i: (0, 0), pipeline_mode=pl.Buffered(1)))
+    return pl.pallas_call(
+        first_kernel,
+        out_shape=jax.ShapeDtypeStruct((depth, columns), jnp.bfloat16),
+        grid=(depth // tile,),
+        in_specs=specs,
+        out_specs=pl.BlockSpec((tile, columns), lambda i: (i, 0)),
+        cost_estimate=cost,
+        name=name,
+    )(*[array for pair in pairs for array in pair])
 
 
 def halves(values):
@@ -327,7 +447,7 @@
     for tile in tiles_of(size):
         up_tile = slice(size + tile.start, size + tile.stop)
         gate_val = product(left, weights[0][:, tile])
-        up_val = product(left, weights[1][:, tile])
+        up_val = product(left, weights[0][:, up_tile])
         both[:, tile] = gate_val.astype(both.dtype)
         both[:, up_tile] = up_val.astype(both.dtype)
         hidden[:, tile] = (gate_val * jax.nn.sigmoid(gate_val) * up_val).astype(hidden.dtype)
@@ -391,13 +511,12 @@
         values[span, :] = tile[:, (heads + 1) * HD :].astype(jnp.bfloat16)
 
 
-def weights_of(query, keys, start, valid_len):
-    scores = lax.dot_general(query, keys, (((1,), (1,)), ((), ())), preferred_element_type=jnp.float32)
-    row = start + lax.broadcasted_iota(jnp.int32, scores.shape, 0)
-    column = lax.broadcasted_iota(jnp.int32, scores.shape, 1)
-    allowed = (column <= row) & (column < valid_len)
-    weights = jnp.where(allowed, jnp.exp(scores * SCALE), 0.0)
-    return (weights, 1.0 / jnp.sum(weights, -1, keepdims=True))
+def weights_of(left, right, start, valid_len, key_axis):
+    scores = lax.dot_general(left, right, (((1,), (1,)), ((), ())), preferred_element_type=jnp.float32)
+    query_place = start + lax.broadcasted_iota(jnp.int32, scores.shape, 1 - key_axis)
+    key_place = lax.broadcasted_iota(jnp.int32, scores.shape, key_axis)
+    allowed = (key_place <= query_place) & (key_place < valid_len)
+    return jnp.where(allowed, jnp.exp(scores * SCALE), 0.0)
 
 
 def forward_kernel(rows, blocks, heads, meta, raw, gains, cos_ref, sin_ref, context, queries, keys, values):
@@ -408,7 +527,8 @@
         seen = (block + 1) * rows
         for head in range(heads):
             query = queries[head, block * rows : seen, :]
-            weights, inverse = weights_of(query, keys[:seen, :], block * rows, valid_len)
+            weights = weights_of(query, keys[:seen, :], block * rows, valid_len, 1)
+            inverse = 1.0 / jnp.sum(weights, -1, keepdims=True)
             part = jnp.dot(
                 weights.astype(jnp.bfloat16), values[:seen, :], preferred_element_type=jnp.float32
             )
@@ -431,20 +551,18 @@
         for head in range(heads):
             query = queries[head, block * rows : seen, :]
             grad = context_grad[core, chip, :, head * HD : (head + 1) * HD]
-            weights, inverse = weights_of(query, keys[:seen, :], block * rows, valid_len)
-            probability = weights * inverse
-            value_grad[:seen, :] += lax.dot_general(
-                probability.astype(jnp.bfloat16), grad, first, preferred_element_type=jnp.float32
+            weights = weights_of(keys[:seen, :], query, block * rows, valid_len, 0)
+            probability = weights * (1.0 / jnp.sum(weights, 0, keepdims=True))
+            value_grad[:seen, :] += jnp.dot(
+                probability.astype(jnp.bfloat16), grad, preferred_element_type=jnp.float32
             )
-            prob_grad = lax.dot_general(grad, values[:seen, :], last, preferred_element_type=jnp.float32)
-            inner = jnp.sum(probability * prob_grad, -1, keepdims=True)
+            prob_grad = lax.dot_general(values[:seen, :], grad, last, preferred_element_type=jnp.float32)
+            inner = jnp.sum(probability * prob_grad, 0, keepdims=True)
             score_grad = (probability * (prob_grad - inner)).astype(jnp.bfloat16)
-            query_grad[head, block * rows : seen, :] = SCALE * jnp.dot(
-                score_grad, keys[:seen, :], preferred_element_type=jnp.float32
+            query_grad[head, block * rows : seen, :] = SCALE * lax.dot_general(
+                score_grad, keys[:seen, :], first, preferred_element_type=jnp.float32
             )
-            key_grad[:seen, :] += SCALE * lax.dot_general(
-                score_grad, query, first, preferred_element_type=jnp.float32
-            )
+            key_grad[:seen, :] += SCALE * jnp.dot(score_grad, query, preferred_element_type=jnp.float32)
     query_total = jnp.zeros((1, HD), jnp.float32)
     key_total = jnp.zeros((1, HD), jnp.float32)
     for block in range(blocks):
@@ -587,9 +705,10 @@
 def step_part(gradient, span, arrays, results):
     one, two, master = (array[span].reshape(gradient.shape) for array in arrays)
     new_one, new_two = moments(gradient, one, two)
-    results[0][span] = new_one.reshape(results[0][span].shape)
-    results[1][span] = new_two.reshape(results[1][span].shape)
-    return (square(master), square(update_of(new_one, new_two, master)))
+    update = update_of(new_one, new_two, master)
+    for result, values in zip(results, (new_one, new_two, update)):
+        result[span] = values.reshape(result[span].shape)
+    return (square(master), square(update))
 
 
 def put_sums(sums, pairs, first):
@@ -604,7 +723,7 @@
     return (left[0] + right[0], left[1] + right[1])
 
 
-def stacked_step(meta, mine, other, one, two, master, new_one, new_two, sums):
+def stacked_step(meta, mine, other, one, two, master, new_one, new_two, update, sums):
     step = pl.program_id(0)
     size = one.shape[2]
     pairs = []
@@ -612,21 +731,21 @@
         columns = slice(side * size, (side + 1) * size)
         own = step == meta[0]
         gradient = jnp.where(own, mine[:, columns], other[:, columns]).astype(jnp.float32)
-        pairs += step_part(gradient, (side,), (one, two, master), (new_one, new_two))
+        pairs += step_part(gradient, (side,), (one, two, master), (new_one, new_two, update))
     put_sums(sums, pairs, step == 0)
 
 
-def turned_step(meta, mine, other, one, two, master, new_one, new_two, sums):
+def turned_step(meta, mine, other, one, two, master, new_one, new_two, update, sums):
     step = pl.program_id(0)
     gradient = jnp.where(step == meta[0], mine[...], other[...]).astype(jnp.float32).T
-    pair = step_part(gradient, (slice(None),), (one, two, master), (new_one, new_two))
+    pair = step_part(gradient, (slice(None),), (one, two, master), (new_one, new_two, update))
     put_sums(sums, pair, step == 0)
 
 
 def attn_step(
     meta, mine, other, query_one, query_two, query, keyval_one, keyval_two, keyval,
-    output_one, output_two, output, new_query_one, new_query_two, new_keyval_one, new_keyval_two,
-    new_output_one, new_output_two, sums,
+    output_one, output_two, output, new_query_one, new_query_two, query_update,
+    new_keyval_one, new_keyval_two, keyval_update, new_output_one, new_output_two, output_update, sums,
 ):
     step = pl.program_id(0)
     own = step == meta[0]
@@ -639,15 +758,15 @@
 
     whole_span = (slice(None),)
     pairs = []
-    pairs += step_part(part(0, width), whole_span, (query_one, query_two, query), (new_query_one, new_query_two))
+    pairs += step_part(part(0, width), whole_span, (query_one, query_two, query), (new_query_one, new_query_two, query_update))
     for side in range(2):
         pairs += step_part(
             part(width + side * key_width, key_width), (side,),
-            (keyval_one, keyval_two, keyval), (new_keyval_one, new_keyval_two),
+            (keyval_one, keyval_two, keyval), (new_keyval_one, new_keyval_two, keyval_update),
         )
     pairs += step_part(
         part(width + 2 * key_width, mine.shape[1] - width - 2 * key_width).T, whole_span,
-        (output_one, output_two, output), (new_output_one, new_output_two),
+        (output_one, output_two, output), (new_output_one, new_output_two, output_update),
     )
     put_sums(sums, pairs, step == 0)
 
@@ -660,8 +779,7 @@
 def step_call(name, kernel, place, mine, other, arrays, axes):
     fixed = pl.BlockSpec(mine.shape, lambda i, meta: (0, 0))
     specs = [half_block(array, axis) for group, axis in zip(arrays, axes) for array in group]
-    out_arrays = [(array, axis) for group, axis in zip(arrays, axes) for array in group[:2]]
-    size = sum(array.size for group in arrays for array in group)
+    out_arrays = [(array, axis) for group, axis in zip(arrays, axes) for array in group]
     return pl.pallas_call(
         kernel,
         out_shape=tuple(jax.ShapeDtypeStruct(array.shape, jnp.float32) for array, _ in out_arrays)
@@ -673,7 +791,7 @@
             out_specs=tuple(half_block(array, axis) for array, axis in out_arrays)
             + (pl.BlockSpec((8, HD), lambda i, meta: (0, 0)),),
         ),
-        cost_estimate=pl.CostEstimate(flops=8 * size, transcendentals=0, bytes_accessed=7 * size),
+        cost_estimate=LIGHT,
         name=name,
     )(place, mine, other, *[array for group in arrays for array in group])
 
@@ -684,16 +802,14 @@
 
 def apply_kernel(parts, axes, *refs):
     sums = refs[0]
-    index = 1
     count = len(parts)
     for place, rows in enumerate(parts):
-        one, two, master = refs[1 + 3 * place : 4 + 3 * place]
-        result = refs[1 + 3 * count + place]
+        update, master = refs[1 + 2 * place : 3 + 2 * place]
+        result = refs[1 + 2 * count + place]
         for side, row in enumerate(rows):
             span = (side,) if len(rows) > 1 else (slice(None),)
             trust = ratio_of(sums[row : row + 1, 0:1], sums[row + 1 : row + 2, 0:1])
-            old = master[span]
-            result[span] = old - LEARN * trust * update_of(one[span], two[span], old)
+            result[span] = master[span] - LEARN * trust * update[span]
 
 
 def apply_call(name, sums, arrays, parts, axes, steps):
@@ -701,22 +817,21 @@
         shape = tuple(size // steps if place == axis else size for place, size in enumerate(array.shape))
         return pl.BlockSpec(shape, lambda i: tuple(i if place == axis else 0 for place in range(len(shape))))
 
-    size = sum(array.size for group in arrays for array in group)
     return pl.pallas_call(
         functools.partial(apply_kernel, parts, axes),
-        out_shape=tuple(jax.ShapeDtypeStruct(group[2].shape, jnp.float32) for group in arrays),
+        out_shape=tuple(jax.ShapeDtypeStruct(group[1].shape, jnp.float32) for group in arrays),
         grid=(steps,),
         in_specs=[pl.BlockSpec(sums.shape, lambda i: (0, 0))]
         + [block(array, axis) for group, axis in zip(arrays, axes) for array in group],
-        out_specs=tuple(block(group[2], axis) for group, axis in zip(arrays, axes)),
-        cost_estimate=pl.CostEstimate(flops=8 * size, transcendentals=0, bytes_accessed=6 * size),
+        out_specs=tuple(block(group[1], axis) for group, axis in zip(arrays, axes)),
+        cost_estimate=LIGHT,
         name=name,
     )(sums, *[array for group in arrays for array in group])
 
 
-def gains_kernel(rows, late, early, first, second, gains, new_first, new_second, new_gains, stats, trust):
+def gains_kernel(rows, sums, first, second, gains, new_first, new_second, new_gains, stats, trust):
     each = (rows - 2) // 2
-    new_one, new_two = moments(late[:rows, :], first[:rows, :], second[:rows, :])
+    new_one, new_two = moments(sums[24 : 24 + rows, :], first[:rows, :], second[:rows, :])
     for result, values in ((new_first, new_one), (new_second, new_two), (new_gains, new_one)):
         result[:rows, :] = values
         result[rows:, :] = jnp.zeros_like(result[rows:, :])
@@ -737,14 +852,9 @@
         weight_square, update_square = (square(old), square(update))
         new_gains[span, :] = old - LEARN * ratio_of(weight_square, update_square) * update
         weight_row, update_row = put(place, weight_square, update_square, weight_row, update_row)
-    for place, index in ((1, 0), (2, 2), (3, 4), (6, 6)):
+    for place, index in ((1, 16), (2, 18), (3, 20), (6, 22), (8, 0), (9, 2), (10, 8)):
         weight_row, update_row = put(
-            place, late[rows + index : rows + index + 1, 0:1], late[rows + index + 1 : rows + index + 2, 0:1],
-            weight_row, update_row,
-        )
-    for place, index in ((8, 0), (9, 2), (10, 8)):
-        weight_row, update_row = put(
-            place, early[index : index + 1, 0:1], early[index + 1 : index + 2, 0:1], weight_row, update_row
+            place, sums[index : index + 1, 0:1], sums[index + 1 : index + 2, 0:1], weight_row, update_row
         )
     stats[0:1, :] = weight_row[:, :11]
     stats[1:2, :] = update_row[:, :11]
@@ -814,35 +924,37 @@
     full_attn = gather_weights(mine, swap(theirs, PAIR))
 
     chip, pair = named("norm_one", gather_start, normed)
-    gateup_mine, gateup_theirs = pair_weights([part.astype(low) for part in gateup_weight])
-    chip, pair, gateup_theirs = together(chip, pair, gateup_theirs)
+    gateup_mine, gateup_theirs = pair_weights(
+        [gateup_weight[0].astype(low), gateup_weight[1].astype(low), down_weight.astype(low).T]
+    )
+    meta = jnp.concatenate(
+        [lax.axis_index("narrow").astype(jnp.int32)[None], lengths, swap(lengths, PAIR)]
+    )
+    chip, pair, gateup_theirs, cos_table, sin_table, meta, head_gains = together(
+        chip, pair, gateup_theirs, cos_table, sin_table, meta, head_gains
+    )
     (cross,) = named("norm_one", gather_cross, chip, pair, False)
     gateup_pair = in_order(gateup_mine, swap(gateup_theirs, PAIR), 0)
     full_attn, grad_low = together(full_attn, grad_out.astype(low))
     cross, gateup_pair = together(cross, gateup_pair)
-    full_gate = gather_outer(gateup_pair[:, :hidden_size])
-    full_up = gather_outer(gateup_pair[:, hidden_size:])
+    full_gateup = gather_outer(gateup_pair[:, : 2 * hidden_size])
+    full_down = gather_outer(gateup_pair[:, 2 * hidden_size :])
     grad_chip, grad_pair = named("output_grad", gather_start, grad_low)
     pieces_one = named("norm_one", gather_end, (normed, chip, pair, cross))
     raw, whole_one = rows_call(
         "query_key_value", plain_finish, pieces_one, [full_attn], [raw_width], [jnp.float32], raw_width
     )
-    down_mine, down_theirs = pair_weights([down_weight.astype(low).T])
-    raw, grad_chip, grad_pair, down_theirs = together(raw, grad_chip, grad_pair, down_theirs)
-    down_pair = in_order(down_mine, swap(down_theirs, PAIR), 0)
-    meta = jnp.concatenate(
-        [lax.axis_index("narrow").astype(jnp.int32)[None], lengths, swap(lengths, PAIR)]
-    )
     context = attend_forward(meta, raw, head_gains, cos_table, sin_table)
-    context, down_pair = together(context, down_pair)
-    full_down = gather_outer(down_pair)
-
-    full_output = full_attn[:, raw_width:]
-    cross, rest = named("attention_out", partial_rows, context, full_output)
+    context, grad_chip, grad_pair = together(context, grad_chip, grad_pair)
+
+    cross, near, far = named(
+        "attention_out", partial_rows, context, full_attn, output_half, raw_width // output_half
+    )
     moved = named("attention_out", scatter_cross, cross)
-    own, chip, pair = named("attention_out", scatter_near, rest, *moved)
-    own, chip, pair, full_gate = together(own, chip, pair, full_gate)
-    attn_part = three(own, chip, pair)
+    near, far[0], from_pair, from_chip = together(near, far[0], *moved)
+    chip, pair = named("attention_out", near_sums, near, far, from_pair, from_chip)
+    chip, pair = named("attention_out", scatter_near, chip, pair)
+    attn_part = all_sums(near, far, chip, pair)
     middle = residual + attn_part
     inv_two = lax.rsqrt(jnp.mean(middle * middle, -1, keepdims=True) + EPS)
     hat_two = middle * inv_two
@@ -852,101 +964,118 @@
     *cross, grad_chip, grad_pair = together(*cross, grad_chip, grad_pair)
     pieces_two = named("norm_two", gather_end, (normed, chip, pair, *cross))
     grad_cross = named("output_grad", gather_cross, grad_chip, grad_pair, True)
-    pieces_grad = named("output_grad", gather_end, (grad_low, grad_chip, grad_pair, *grad_cross))
-    both, hidden, whole_two, full_gateup = rows_call(
-        "gate_up", gate_finish, pieces_two, [full_gate, full_up], [2 * hidden_size, hidden_size], [low, low]
-    )
-    whole_grad = join(pieces_grad)
-    down_grad = product_first(whole_grad, hidden)
+    both, hidden, whole_two = rows_call(
+        "gate_up", gate_finish, pieces_two, [full_gateup], [2 * hidden_size, hidden_size], [low, low],
+    )
+    hidden, *grad_cross = together(hidden, *grad_cross)
+    whole_grad = join(
+        named("output_grad", gather_end, (grad_low, grad_chip, grad_pair, *grad_cross))
+    )
+    down_grad = product_first("down_weight_grad", (whole_grad, hidden))
     full_down, down_grad = together(full_down, down_grad)
     down_own = scatter_outer(down_grad)
     pair_grad = blocks_call(
         "hidden_grad", hidden_finish, whole_grad, full_down, [both], 2 * hidden_size, shard_len
     )
-    normed_two = named("norm_two_grad", product_rows, pair_grad, full_gateup)
-    gateup_grad = product_first(whole_two, pair_grad)
-    normed_two, gateup_grad = together(normed_two, gateup_grad)
-    gateup_grad, down_own = together(gateup_grad, down_own)
+    cross, near, far = named("norm_two_grad", partial_rows, pair_grad, full_gateup, 2 * hidden_size)
+    moved = named("norm_two_grad", scatter_cross, cross)
+    near, far[0], from_pair, from_chip = together(near, far[0], *moved)
+    chip, pair = named("norm_two_grad", near_sums, near, far, from_pair, from_chip)
+    chip, pair, pair_grad = together(chip, pair, pair_grad)
+    chip, pair = named("norm_two_grad", scatter_near, chip, pair)
+    gateup_grad = product_first(
+        "gateup_weight_grad",
+        (whole_two, pair_grad),
+        cost=pl.CostEstimate(
+            flops=2 * whole_two.size * pair_grad.shape[1], transcendentals=0, bytes_accessed=2 * whole_two.size
+        ),
+    )
+    chip, pair, down_own, gateup_grad = together(chip, pair, down_own, gateup_grad)
     gateup_own = scatter_outer(gateup_grad)
+    normed_two = all_sums(near, far, chip, pair)
     middle_norm, gain_two_grad = norm_back(normed_two, hat_two, inv_two, gain_two)
     middle_grad = grad_out + middle_norm
-    middle_low = middle_grad.astype(low)
+    down_mine, down_other = own_grads(down_own)
+    middle_low, down_other = together(middle_grad.astype(low), down_other)
     chip, pair = named("middle_grad", gather_start, middle_low)
     cross = named("middle_grad", gather_cross, chip, pair, True)
-    hidden, full_down, middle_low = together(hidden, full_down, middle_low)
-    mlp_cross, mlp_rest = named("mlp_out", partial_rows, hidden, full_down)
-    *cross, mlp_cross, mlp_rest = together(*cross, mlp_cross, mlp_rest)
+    hidden, middle_low = together(hidden, middle_low)
+    mlp_cross, mlp_near, mlp_far = named("mlp_out", partial_rows, hidden, full_down, hidden_size)
+    *cross, mlp_cross, mlp_near = together(*cross, mlp_cross, mlp_near)
     pieces_mid = named("middle_grad", gather_end, (middle_low, chip, pair, *cross))
     context_grad, whole_mid = rows_call(
         "context_grad", plain_finish, pieces_mid, [full_attn], [output_half], [low],
         output_half, raw_width // output_half,
     )
     moved = named("mlp_out", scatter_cross, mlp_cross)
-    context_grad, mlp_rest, *moved = together(context_grad, mlp_rest, *moved)
-    mlp_parts = named("mlp_out", scatter_near, mlp_rest, *moved)
+    mlp_chip, mlp_pair = named("mlp_out", near_sums, mlp_near, mlp_far, *moved)
+    context_grad, mlp_chip, mlp_pair = together(context_grad, mlp_chip, mlp_pair)
+    mlp_chip, mlp_pair = named("mlp_out", scatter_near, mlp_chip, mlp_pair)
     raw_grad, head_gain_grad = attend_backward(meta, raw, context_grad, head_gains, cos_table, sin_table)
-    attn_grad = jnp.concatenate(
-        [product_first(whole_one, raw_grad), product_first(whole_mid, context)], 1
-    )
-    raw_grad, attn_grad, *mlp_parts = together(raw_grad, attn_grad, *mlp_parts)
-    mlp_part = three(*mlp_parts)
-    attn_grad, gateup_own = together(attn_grad, gateup_own)
+    raw_grad, mlp_chip, mlp_pair = together(raw_grad, mlp_chip, mlp_pair)
+    mlp_part = all_sums(mlp_near, mlp_far, mlp_chip, mlp_pair)
+    attn_grad = product_first("attention_weight_grad", (whole_one, raw_grad), (whole_mid, context))
     attn_own = scatter_outer(attn_grad)
-    normed_one = named("norm_one_grad", product_rows, raw_grad, full_attn[:, :raw_width])
-    input_norm, gain_one_grad = norm_back(normed_one, hat_one, inv_one, gain_one)
-    input_grad = (middle_grad + input_norm).astype(low)
-
+    gateup_mine, gateup_other = own_grads(gateup_own)
+    place = lax.axis_index("inner").astype(jnp.int32)[None]
+    down = (down_first, down_second, down_weight)
+    gateup = (gateup_first, gateup_second, gateup_weight)
+    cross, near, far = named("norm_one_grad", partial_rows, raw_grad, full_attn, raw_width)
+    cross, gateup_other = together(cross, gateup_other)
+    moved = named("norm_one_grad", scatter_cross, cross)
+    near, far[0], from_pair, from_chip = together(near, far[0], *moved)
+    chip, pair = named("norm_one_grad", near_sums, near, far, from_pair, from_chip)
+    chip, pair = named("norm_one_grad", scatter_near, chip, pair)
+    new_down_first, new_down_second, down_update, down_sums = step_call(
+        "down_step", turned_step, place, down_mine, down_other, [down], [0]
+    )
+    new_gateup_first, new_gateup_second, gateup_update, gateup_sums = step_call(
+        "gateup_step", stacked_step, place, gateup_mine, gateup_other, [gateup], [2]
+    )
     final = middle + mlp_part
     result = final.astype(low)
     rms_values = jnp.stack([root_mean(attn_part), root_mean(mlp_part), root_mean(final)])[:, None, :]
-
-    place = lax.axis_index("inner").astype(jnp.int32)[None]
-    down = (down_first, down_second, down_weight)
-    gateup = (gateup_first, gateup_second, gateup_weight)
-    new_down_first, new_down_second, down_sums = step_call(
-        "down_step", turned_step, place, *own_grads(down_own), [down], [0]
-    )
-    new_gateup_first, new_gateup_second, gateup_sums = step_call(
-        "gateup_step", stacked_step, place, *own_grads(gateup_own), [gateup], [2]
-    )
-    early = named("early_sums", total, jnp.concatenate([gateup_sums, down_sums], 0))
-    new_gateup, new_down = apply_call(
-        "gateup_down",
-        early,
-        [
-            (new_gateup_first, new_gateup_second, gateup_weight),
-            (new_down_first, new_down_second, down_weight),
-        ],
-        ((0, 2), (8,)),
-        (1, 0),
-        4,
-    )
-    attn_own, new_gateup, new_down = together(attn_own, new_gateup, new_down)
+    attn_own, result, rms_values, gain_two_grad = together(attn_own, result, rms_values, gain_two_grad)
+    attn_mine, attn_other = own_grads(attn_own)
+    chip, pair, gateup_sums, down_sums, attn_other = together(
+        chip, pair, gateup_sums, down_sums, attn_other
+    )
+    normed_one = all_sums(near, far, chip, pair)
+    input_norm, gain_one_grad = norm_back(normed_one, hat_one, inv_one, gain_one)
+    input_grad = (middle_grad + input_norm).astype(low)
+
     attn_arrays = [
         (query_first, query_second, query_weight),
         (keyval_first, keyval_second, keyval_weight),
         (output_first, output_second, output_weight),
     ]
     (
-        new_query_first, new_query_second, new_keyval_first, new_keyval_second,
-        new_output_first, new_output_second, attn_sums,
-    ) = step_call("attention_step", attn_step, place, *own_grads(attn_own), attn_arrays, [1, 2, 0])
-    late = jnp.concatenate(
-        [gain_one_grad.reshape(-1, HD), gain_two_grad.reshape(-1, HD), head_gain_grad, attn_sums], 0
-    )
-    late = named("late_sums", total, late)
+        new_query_first, new_query_second, query_update, new_keyval_first, new_keyval_second,
+        keyval_update, new_output_first, new_output_second, output_update, attn_sums,
+    ) = step_call("attention_step", attn_step, place, attn_mine, attn_other, attn_arrays, [1, 2, 0])
+    sums = jnp.concatenate(
+        [gateup_sums, down_sums, attn_sums]
+        + [gain_one_grad.reshape(-1, HD), gain_two_grad.reshape(-1, HD), head_gain_grad],
+        0,
+    )
+    sums = named("all_sums", total, sums)
+    matrix_sums = sums[:24]
     gain_rows = norm_gains.size // HD
     new_query, new_keyval, new_output = apply_call(
         "attention",
-        late[gain_rows:],
-        [
-            (new_query_first, new_query_second, query_weight),
-            (new_keyval_first, new_keyval_second, keyval_weight),
-            (new_output_first, new_output_second, output_weight),
-        ],
-        ((0,), (2, 4), (6,)),
+        matrix_sums,
+        [(query_update, query_weight), (keyval_update, keyval_weight), (output_update, output_weight)],
+        ((16,), (18, 20), (22,)),
         (0, 1, 0),
         2,
+    )
+    new_gateup, new_down = apply_call(
+        "gateup_down",
+        matrix_sums,
+        [(gateup_update, gateup_weight), (down_update, down_weight)],
+        ((0, 2), (8,)),
+        (1, 0),
+        4,
     )
     padded = -(-gain_rows // 8) * 8
     gain_shape = jax.ShapeDtypeStruct((padded, HD), jnp.float32)
@@ -956,8 +1085,7 @@
         + tuple(jax.ShapeDtypeStruct((rows, 11), jnp.float32) for rows in (2, 1)),
         name="gains",
     )(
-        late,
-        early,
+        sums,
         *[
             jnp.pad(values, (0, (padded - gain_rows) * HD)).reshape(padded, HD)
             for values in (gains_first, gains_second, norm_gains)

time: 652 us -> 614 us (0.942)
  Pallas kernels: 132 us -> 265 us
  matrix products: 92.3 us -> 0 us
  waiting for transfers between devices: 241 us -> 186 us
  other arithmetic: 70.3 us -> 47.7 us
    pallas_call x0 -> x19, Pallas kernels: none -> 142 us  [the longest x3 41.8 us: product_first(): pl.pallas_call(first_kernel, out_shape=jax.ShapeDtypeStruct((depth, colum...]
    dot_general x20 -> x0, matrix products: 92.3 us -> none  [the longest x16 53.5 us: part(): lax.dot_general(left[first * rows:last * rows], right, (((1,), (1,)), (()...]
    ppermute x75 -> x77, waiting for transfers between devices: 234 us -> 179 us  [swap(): lax.ppermute(values, axis, [(i, i ^ bit) for i in range(lax.axis_size(axi...]
    add x4 -> x0, other arithmetic: 14.4 us -> none  [the longest x3 10.3 us: partial_rows(): return (cross, part(0, 3) + rest_far.astype(wide))]
    convert_element_type x8 -> x6, other arithmetic: 14.5 us -> 12.6 us  [the longest x4 6.73 us: partial_rows(): cross = (near_cross + far_cross.astype(jnp.float32)).astype(low)]
    ppermute x75 -> x77, starting transfers between devices: 53.7 us -> 52.5 us  [swap(): lax.ppermute(values, axis, [(i, i ^ bit) for i in range(lax.axis_size(axi...]
    unnamed x137 -> x113, local copies, waits for them, and re-layouts: 14.7 us -> 13.9 us
  transfers between devices with their start and end apart: 82 -> 83, of which waited for: 42 -> 38; matrix products, arithmetic and copies ran while one was open for 27% -> 11% of each run, Pallas kernels for 16% -> 41%
where the time goes in v3:
time: 614 us; the launch traced here: 608 us
  Pallas kernels  265 us (43%)
  waiting for transfers between devices  186 us (30%)
  starting transfers between devices  53.9 us (9%)
  other arithmetic  47.7 us (8%)
  local copies, waits for them, and re-layouts  39.1 us (6%)
  between operations  15.7 us (3%)
    ppermute x77, waiting for transfers between devices, swap(): lax.ppermute(values, axis, [(i, i ^ bit) for i in range(lax.axis_size(axi...  179 us
    ppermute x77, starting transfers between devices, swap(): lax.ppermute(values, axis, [(i, i ^ bit) for i in range(lax.axis_size(axi...  52.5 us
    pallas_call x3, Pallas kernels, product_first(): pl.pallas_call(first_kernel, out_shape=jax.ShapeDtypeStruct((depth, colum...  41.8 us
    pallas_call x3, Pallas kernels, rows_call(): pl.pallas_call(functools.partial(rows_kernel, finish, len(pieces), len(we...  39.3 us
    pallas_call x4, Pallas kernels, part_call(): pl.pallas_call(part_kernel, out_shape=(jax.ShapeDtypeStruct((rows, column...  29 us
    pallas_call x4, Pallas kernels, near_call(): pl.pallas_call(near_kernel, out_shape=jax.ShapeDtypeStruct((3 * rows, col...  27.5 us
    pallas_call x4, Pallas kernels, cross_call(): pl.pallas_call(cross_kernel, out_shape=(jax.ShapeDtypeStruct(shape, jnp.f...  23.9 us
    pallas_call x1, Pallas kernels, attend_backward(): pl.pallas_call(functools.partial(backward_kernel, rows, blocks, heads), o...  22.3 us
  transfers between devices with their start and end apart: 83, of which 38 were waited for; matrix products, arithmetic and copies ran while one was open for 11% of the time, Pallas kernels for 41%

profile of v3, /device:TPU:0, one launch (start us, length us, event | category | flops | bytes accessed | tf_op | source)
XLA Modules:
  0.0 607.8 jit_solution(16522565907484121292)
XLA Ops:
  13.3 8.8 %collective-permute-done.9 = bf16[256,768]{1,0:T(8,128)(2,1)S(1)} collective-permute-done((bf16[256,768]{1,0:T(8,128)(2,1)S(1)}, bf16[256,768]{1,0:T(8,128)(2,1)S(1)}, u32[]{:S(2)}, u32[]{:S(2)}) %collective-permute-start.9) | collective-permute-done | bytes 393248 | tf_op jit(solution)/shard_map/ppermute | solution.py:40
  40.9 10.8 %collective-permute-done.2 = s32[1]{0:T(128)} collective-permute-done((s32[1]{0:T(128)}, s32[1]{0:T(128)}, u32[]{:S(2)}, u32[]{:S(2)}) %collective-permute-start.2) | collective-permute-done | bytes 36 | tf_op jit(solution)/shard_map/ppermute | solution.py:40
  55.0 23.6 %collective-permute-done.4 = bf16[256,2304]{1,0:T(8,128)(2,1)S(1)} collective-permute-done((bf16[256,2304]{1,0:T(8,128)(2,1)S(1)}, bf16[256,2304]{1,0:T(8,128)(2,1)S(1)}, u32[]{:S(2)}, u32[]{:S(2)}) %collective-permute-start.4) | collective-permute-done | bytes 1179680 | tf_op jit(solution)/shard_map/ppermute | solution.py:40
  91.3 10.3 %query_key_value.1 = (f32[8,256,512]{2,1,0:T(8,128)}, bf16[8,256,2048]{2,1,0:T(8,128)(2,1)}) custom-call(bf16[256,2048]{1,0:T(8,128)(2,1)} %fusion.4.refs_0_, bf16[256,2048]{1,0:T(8,128)(2,1)} %collective-permute-done.refs_1_, bf16[256,2048]{1,0:T(8,128)(2,1)} %collective-permute-done.1.refs_2_, bf16[256,2048]{1,0:T(8,128)(2,1)} %copy-done.22, ...), custom_call_target="tpu_custom_call" | custom-call | flops 1024 | bytes 1024 | tf_op jit(solution)/shard_map/query_key_value/pallas_call | solution.py:385
  101.6 10.9 %attend_forward.1 = bf16[2,2,2,256,256]{4,3,2,1,0:T(8,128)(2,1)} custom-call(s32[3]{0:T(128)} %pad_add_fusion.meta, f32[2,2,2,256,512]{4,3,2,1,0:T(8,128)} %bitcast.92, f32[2,128]{1,0:T(2,128)} %slice_bitcast_fusion.3.gains, f32[1024,128]{1,0:T(8,128)} %get-tuple-element.198.cos_ref, f32[1024,128]{1,0:T(8,128)} %get-tuple-element.199.sin_ref), custom_call_target="tpu_custom_call" | custom-call | flops 1024 | bytes 1024 | tf_op jit(solution)/shard_map/attend_forward/pallas_call | solution.py:613
  152.6 20.6 %collective-permute-done.19 = bf16[256,2048]{1,0:T(8,128)(2,1)S(1)} collective-permute-done((bf16[256,2048]{1,0:T(8,128)(2,1)}, bf16[256,2048]{1,0:T(8,128)(2,1)S(1)}, u32[]{:S(2)}, u32[]{:S(2)}) %collective-permute-start.19) | collective-permute-done | bytes 1048608 | tf_op jit(solution)/shard_map/attention_out/ppermute | solution.py:40
  179.9 21.9 %collective-permute-done.20.refs_1_ = bf16[256,2048]{1,0:T(8,128)(2,1)S(1)} collective-permute-done((bf16[256,2048]{1,0:T(8,128)(2,1)S(1)}, bf16[256,2048]{1,0:T(8,128)(2,1)S(1)}, u32[]{:S(2)}, u32[]{:S(2)}) %collective-permute-start.20) | collective-permute-done | bytes 1048608 | tf_op jit(solution)/shard_map/norm_two/ppermute | solution.py:40
  205.3 8.1 %collective-permute-done.22.refs_3_ = bf16[128,2048]{1,0:T(8,128)(2,1)S(1)} collective-permute-done((bf16[128,2048]{1,0:T(8,128)(2,1)S(1)}, bf16[128,2048]{1,0:T(8,128)(2,1)S(1)}, u32[]{:S(2)}, u32[]{:S(2)}) %collective-permute-start.22) | collective-permute-done | bytes 524320 | tf_op jit(solution)/shard_map/norm_two/ppermute | solution.py:40
  223.6 20.2 %gate_up.1 = (bf16[8,256,1536]{2,1,0:T(8,128)(2,1)}, bf16[8,256,768]{2,1,0:T(8,128)(2,1)}, bf16[8,256,2048]{2,1,0:T(8,128)(2,1)}) custom-call(bf16[256,2048]{1,0:T(8,128)(2,1)} %copy-done.7, bf16[256,2048]{1,0:T(8,128)(2,1)} %copy-done.11, bf16[256,2048]{1,0:T(8,128)(2,1)} %copy-done.12, bf16[128,2048]{1,0:T(8,128)(2,1)} %copy-done.24, ...), custom_call_target="tpu_custom_call" | custom-call | flops 1024 | bytes 1024 | tf_op jit(solution)/shard_map/gate_up/pallas_call | solution.py:385
  253.5 10.9 %down_weight_grad.1 = bf16[2048,768]{1,0:T(8,128)(2,1)} custom-call(bf16[2048,2048]{1,0:T(8,128)(2,1)} %bitcast.78, bf16[2048,768]{1,0:T(8,128)(2,1)} %bitcast.80), custom_call_target="tpu_custom_call" | custom-call | flops 1024 | bytes 1024 | tf_op jit(solution)/shard_map/down_weight_grad/pallas_call | solution.py:224
  268.1 14.5 %hidden_grad.1.left.refs_1_ = bf16[2048,1536]{1,0:T(8,128)(2,1)} custom-call(bf16[2048,2048]{1,0:T(8,128)(2,1)} %bitcast.79, bf16[2048,768]{1,0:T(8,128)(2,1)} %all-gather.8.cloned.1.call-done.weight.right, bf16[2048,1536]{1,0:T(8,128)(2,1)} %bitcast.96), custom_call_target="tpu_custom_call" | custom-call | flops 1024 | bytes 1024 | tf_op jit(solution)/shard_map/hidden_grad/pallas_call | solution.py:420
  282.7 8.6 %cross.5 = (f32[256,2048]{1,0:T(8,128)}, bf16[256,2048]{1,0:T(8,128)(2,1)}) custom-call(bf16[2048,1536]{1,0:T(8,128)(2,1)} %hidden_grad.1.left.refs_1_, bf16[2048,1536]{1,0:T(8,128)(2,1)} %all-gather.6.cloned.1.call-done.refs_10_.right), custom_call_target="tpu_custom_call" | custom-call | flops 1024 | bytes 1024 | tf_op jit(solution)/shard_map/norm_two_grad/cross/pallas_call | solution.py:79
  291.3 10.5 %part.5 = (bf16[256,2048]{1,0:T(8,128)(2,1)}, bf16[256,2048]{1,0:T(8,128)(2,1)}, bf16[256,2048]{1,0:T(8,128)(2,1)}) custom-call(bf16[2048,1536]{1,0:T(8,128)(2,1)} %hidden_grad.1.left.refs_1_, bf16[2048,1536]{1,0:T(8,128)(2,1)} %all-gather.6.cloned.1.call-done.refs_10_.right), custom_call_target="tpu_custom_call" | custom-call | flops 1024 | bytes 1024 | tf_op jit(solution)/shard_map/norm_two_grad/part/pallas_call | solution.py:130
  309.1 9.9 %near.5.near_chip.near_pair = f32[768,2048]{1,0:T(8,128)} custom-call(bf16[2048,1536]{1,0:T(8,128)(2,1)} %hidden_grad.1.left.refs_1_, bf16[2048,1536]{1,0:T(8,128)(2,1)} %all-gather.6.cloned.1.call-done.refs_10_.right), custom_call_target="tpu_custom_call" | custom-call | flops 1024 | bytes 1024 | tf_op jit(solution)/shard_map/norm_two_grad/near/pallas_call | solution.py:113
  328.5 18.6 %gateup_weight_grad.1 = bf16[2048,1536]{1,0:T(8,128)(2,1)} custom-call(bf16[2048,2048]{1,0:T(8,128)(2,1)} %bitcast.102, bf16[2048,1536]{1,0:T(8,128)(2,1)} %hidden_grad.1.left.refs_1_), custom_call_target="tpu_custom_call" | custom-call | flops 12884901888 | bytes 8388608 | tf_op jit(solution)/shard_map/gateup_weight_grad/pallas_call | solution.py:224
  370.8 7.1 %part.6 = (bf16[256,2048]{1,0:T(8,128)(2,1)}, bf16[256,2048]{1,0:T(8,128)(2,1)}, bf16[256,2048]{1,0:T(8,128)(2,1)}) custom-call(bf16[2048,768]{1,0:T(8,128)(2,1)} %bitcast.82, bf16[2048,768]{1,0:T(8,128)(2,1)} %all-gather.8.cloned.1.call-done.weight.right), custom_call_target="tpu_custom_call" | custom-call | flops 1024 | bytes 1024 | tf_op jit(solution)/shard_map/mlp_out/part/pallas_call | solution.py:130
  392.2 9.9 %collective-permute-done.47.refs_3_ = bf16[128,2048]{1,0:T(8,128)(2,1)S(1)} collective-permute-done((bf16[128,2048]{1,0:T(8,128)(2,1)S(1)}, bf16[128,2048]{1,0:T(8,128)(2,1)S(1)}, u32[]{:S(2)}, u32[]{:S(2)}) %collective-permute-start.47) | collective-permute-done | bytes 524320 | tf_op jit(solution)/shard_map/middle_grad/ppermute | solution.py:40
  408.6 8.9 %context_grad.1 = (bf16[8,256,256]{2,1,0:T(8,128)(2,1)}, bf16[8,256,2048]{2,1,0:T(8,128)(2,1)}) custom-call(bf16[256,2048]{1,0:T(8,128)(2,1)} %get-tuple-element.262.refs_0_, bf16[256,2048]{1,0:T(8,128)(2,1)} %collective-permute-done.45.refs_1_, bf16[256,2048]{1,0:T(8,128)(2,1)} %collective-permute-done.46.refs_2_, bf16[128,2048]{1,0:T(8,128)(2,1)} %copy-done.26, ...), custom_call_target="tpu_custom_call" | custom-call | flops 1024 | bytes 1024 | tf_op jit(solution)/shard_map/context_grad/pallas_call | solution.py:385
  428.8 22.3 %attend_backward.1 = (bf16[2,2,2,256,512]{4,3,2,1,0:T(8,128)(2,1)}, f32[2,2,128]{2,1,0:T(2,128)}) custom-call(s32[3]{0:T(128)} %pad_add_fusion.meta, f32[2,2,2,256,512]{4,3,2,1,0:T(8,128)} %bitcast.93, bf16[2,2,2,256,256]{4,3,2,1,0:T(8,128)(2,1)} %bitcast.98, f32[2,128]{1,0:T(2,128)} %slice_bitcast_fusion.3.gains, f32[1024,128]{1,0:T(8,128)} %get-tuple-element.198.cos_ref, ...), custom_call_target="tpu_custom_call" | custom-call | flops 1024 | bytes 1024 | tf_op jit(solution)/shard_map/attend_backward/pallas_call | solution.py:644
  452.2 12.4 %attention_weight_grad.1 = bf16[2048,768]{1,0:T(8,128)(2,1)} custom-call(bf16[2048,2048]{1,0:T(8,128)(2,1)} %bitcast.94, bf16[2048,512]{1,0:T(8,128)(2,1)} %bitcast.84, bf16[2048,2048]{1,0:T(8,128)(2,1)} %bitcast.95, bf16[2048,256]{1,0:T(8,128)(2,1)} %bitcast.91), custom_call_target="tpu_custom_call" | custom-call | flops 1024 | bytes 1024 | tf_op jit(solution)/shard_map/attention_weight_grad/pallas_call | solution.py:224
  493.0 11.2 %collective-permute-done.64.other = bf16[256,1536]{1,0:T(8,128)(2,1)S(1)} collective-permute-done((bf16[256,1536]{1,0:T(8,128)(2,1)S(1)}, bf16[256,1536]{1,0:T(8,128)(2,1)S(1)}, u32[]{:S(2)}, u32[]{:S(2)}) %collective-permute-start.64) | collective-permute-done | bytes 786464 | tf_op jit(solution)/shard_map/ppermute | solution.py:40
  508.0 10.3 %collective-permute-done.65.from_pair = bf16[128,2048]{1,0:T(8,128)(2,1)} collective-permute-done((bf16[128,2048]{1,0:T(8,128)(2,1)S(1)}, bf16[128,2048]{1,0:T(8,128)(2,1)}, u32[]{:S(2)}, u32[]{:S(2)}) %collective-permute-start.65) | collective-permute-done | bytes 524320 | tf_op jit(solution)/shard_map/norm_one_grad/ppermute | solution.py:40
  538.0 8.4 %gateup_step.1 = (f32[2,256,1536]{2,1,0:T(8,128)}, f32[2,256,1536]{2,1,0:T(8,128)}, f32[2,256,1536]{2,1,0:T(8,128)}, f32[8,128]{1,0:T(8,128)}) custom-call(s32[1]{0:T(128)} %bitcast.33.meta, bf16[256,1536]{1,0:T(8,128)(2,1)} %get-tuple-element.367.mine, bf16[256,1536]{1,0:T(8,128)(2,1)} %copy-done.23, f32[2,256,1536]{2,1,0:T(8,128)} %one.2, ...), custom_call_target="tpu_custom_call" | custom-call | flops 1024 | bytes 1024 | tf_op jit(solution)/shard_map/gateup_step/pallas_call | solution.py:783
  546.4 10.7 %collective-permute-done.71.other = bf16[256,768]{1,0:T(8,128)(2,1)S(1)} collective-permute-done((bf16[256,768]{1,0:T(8,128)(2,1)S(1)}, bf16[256,768]{1,0:T(8,128)(2,1)S(1)}, u32[]{:S(2)}, u32[]{:S(2)}) %collective-permute-start.71) | collective-permute-done | bytes 393248 | tf_op jit(solution)/shard_map/ppermute | solution.py:40
  (368 shorter events, 282.8 us)
Async XLA Ops:
  7.2 81.1 %all-gather.4.cloned.1.call-start = ((), (), s32[]{:S(2)}) async-start(), calls=%async_computation.3 | async-start | bytes 3932160 | tf_op jit(solution)/shard_map/all_gather | solution.py:869
  23.2 200.4 %all-gather.6.cloned.1.call-start = ((), (), s32[]{:S(2)}) async-start(), calls=%async_computation.4 | async-start | bytes 7864320 | tf_op jit(solution)/shard_map/all_gather | solution.py:869
  25.9 27.1 %collective-permute-start = (bf16[256,2048]{1,0:T(8,128)(2,1)}, bf16[256,2048]{1,0:T(8,128)(2,1)}, u32[]{:S(2)}, u32[]{:S(2)}) collective-permute-start(bf16[256,2048]{1,0:T(8,128)(2,1)} %fusion.4.refs_0_), channel_id=1, source_target_pairs={{0,2},{1,3},{2,0},{3,1},{4,6},{5,7},{6,4},{7,5},{8,10},{9,11},{10,... | collective-permute-start | bytes 3145736 | tf_op jit(solution)/shard_map/norm_one/ppermute | solution.py:40
  27.6 25.4 %collective-permute-start.1 = (bf16[256,2048]{1,0:T(8,128)(2,1)}, bf16[256,2048]{1,0:T(8,128)(2,1)}, u32[]{:S(2)}, u32[]{:S(2)}) collective-permute-start(bf16[256,2048]{1,0:T(8,128)(2,1)} %fusion.4.refs_0_), channel_id=1, source_target_pairs={{0,4},{4,0},{1,5},{5,1},{2,6},{6,2},{3,7},{7,3},{8,12},{12,8},{9,1... | collective-permute-start | bytes 3145736 | tf_op jit(solution)/shard_map/norm_one/ppermute | solution.py:40
  53.0 25.6 %collective-permute-start.4 = (bf16[256,2304]{1,0:T(8,128)(2,1)S(1)}, bf16[256,2304]{1,0:T(8,128)(2,1)S(1)}, u32[]{:S(2)}, u32[]{:S(2)}) collective-permute-start(bf16[256,2304]{1,0:T(8,128)(2,1)S(1)} %pad_maximum_fusion.1), channel_id=1, source_target_pairs={{0,4},{4,0},{1,5},{5,1},{2,6},{6,2},{3,7},{7,3},{8,12},{12,8},{9,1... | collective-permute-start | bytes 3538952 | tf_op jit(solution)/shard_map/ppermute | solution.py:40
  54.5 24.8 %collective-permute-start.3 = (bf16[256,2048]{1,0:T(8,128)(2,1)}, bf16[256,2048]{1,0:T(8,128)(2,1)S(1)}, u32[]{:S(2)}, u32[]{:S(2)}) collective-permute-start(bf16[256,2048]{1,0:T(8,128)(2,1)} %collective-permute-done.1.refs_2_), channel_id=1, source_target_pairs={{0,2},{1,3},{2,0},{3,1},{4,6},{5,7},{6,4},{7,5},{8,10},{9,11},{10,... | collective-permute-start | bytes 3145736 | tf_op jit(solution)/shard_map/norm_one/ppermute | solution.py:40
  82.0 185.9 %all-gather.8.cloned.1.call-start = ((), (), s32[]{:S(2)}) async-start(), calls=%async_computation.5 | async-start | bytes 3932160 | tf_op jit(solution)/shard_map/all_gather | solution.py:869
  88.3 25.2 %collective-permute-start.10 = (bf16[256,2048]{1,0:T(8,128)(2,1)}, bf16[256,2048]{1,0:T(8,128)(2,1)}, u32[]{:S(2)}, u32[]{:S(2)}) collective-permute-start(bf16[256,2048]{1,0:T(8,128)(2,1)} %fusion.13.refs_0_), channel_id=1, source_target_pairs={{0,2},{1,3},{2,0},{3,1},{4,6},{5,7},{6,4},{7,5},{8,10},{9,11},{10,... | collective-permute-start | bytes 3145736 | tf_op jit(solution)/shard_map/output_grad/ppermute | solution.py:40
  89.8 24.9 %collective-permute-start.11 = (bf16[256,2048]{1,0:T(8,128)(2,1)}, bf16[256,2048]{1,0:T(8,128)(2,1)}, u32[]{:S(2)}, u32[]{:S(2)}) collective-permute-start(bf16[256,2048]{1,0:T(8,128)(2,1)} %fusion.13.refs_0_), channel_id=1, source_target_pairs={{0,4},{4,0},{1,5},{5,1},{2,6},{6,2},{3,7},{7,3},{8,12},{12,8},{9,1... | collective-permute-start | bytes 3145736 | tf_op jit(solution)/shard_map/output_grad/ppermute | solution.py:40
  148.8 24.4 %collective-permute-start.19 = (bf16[256,2048]{1,0:T(8,128)(2,1)}, bf16[256,2048]{1,0:T(8,128)(2,1)S(1)}, u32[]{:S(2)}, u32[]{:S(2)}) collective-permute-start(bf16[256,2048]{1,0:T(8,128)(2,1)} %get-tuple-element.220), channel_id=1, source_target_pairs={{0,4},{4,0},{1,5},{5,1},{2,6},{6,2},{3,7},{7,3},{8,12},{12,8},{9,1... | collective-permute-start | bytes 3145736 | tf_op jit(solution)/shard_map/attention_out/ppermute | solution.py:40
  149.4 24.8 %collective-permute-start.18 = (bf16[256,2048]{1,0:T(8,128)(2,1)}, bf16[256,2048]{1,0:T(8,128)(2,1)}, u32[]{:S(2)}, u32[]{:S(2)}) collective-permute-start(bf16[256,2048]{1,0:T(8,128)(2,1)} %get-tuple-element.219), channel_id=1, source_target_pairs={{0,2},{1,3},{2,0},{3,1},{4,6},{5,7},{6,4},{7,5},{8,10},{9,11},{10,... | collective-permute-start | bytes 3145736 | tf_op jit(solution)/shard_map/attention_out/ppermute | solution.py:40
  152.0 200.0 %reduce-scatter.4.cloned.1.call-start = ((), (), s32[]{:S(2)}) async-start(), calls=%async_computation.6 | async-start | bytes 3932160 | tf_op jit(solution)/shard_map/reduce_scatter | solution.py:873
  179.9 38.6 %collective-permute-start.24 = (bf16[256,2048]{1,0:T(8,128)(2,1)S(1)}, bf16[256,2048]{1,0:T(8,128)(2,1)S(1)}, u32[]{:S(2)}, u32[]{:S(2)}) collective-permute-start(bf16[256,2048]{1,0:T(8,128)(2,1)S(1)} %multiply_convert_fusion.refs_0_), channel_id=1, source_target_pairs={{0,1},{1,0},{2,3},{3,2},{4,5},{5,4},{6,7},{7,6},{8,9},{9,8},{10,11... | collective-permute-start | bytes 3145736 | tf_op jit(solution)/shard_map/norm_two/ppermute | solution.py:40
  218.6 25.2 %collective-permute-start.29 = (bf16[128,2048]{1,0:T(8,128)(2,1)}, bf16[128,2048]{1,0:T(8,128)(2,1)}, u32[]{:S(2)}, u32[]{:S(2)}) collective-permute-start(bf16[128,2048]{1,0:T(8,128)(2,1)} %slice.130), channel_id=1, source_target_pairs={{0,4},{4,0},{1,5},{5,1},{2,6},{6,2},{3,7},{7,3},{8,12},{12,8},{9,1... | collective-permute-start | bytes 1572872 | tf_op jit(solution)/shard_map/output_grad/ppermute | solution.py:40
  267.9 214.5 %reduce-scatter.8.cloned.1.call-start = ((), (), s32[]{:S(2)}) async-start(), calls=%async_computation.8 | async-start | bytes 7864320 | tf_op jit(solution)/shard_map/reduce_scatter | solution.py:873
  352.0 177.7 %reduce-scatter.6.cloned.1.call-start = ((), (), s32[]{:S(2)}) async-start(), calls=%async_computation.7 | async-start | bytes 3932160 | tf_op jit(solution)/shard_map/reduce_scatter | solution.py:873
  370.3 32.7 %collective-permute-start.50 = (bf16[256,2048]{1,0:T(8,128)(2,1)}, bf16[256,2048]{1,0:T(8,128)(2,1)}, u32[]{:S(2)}, u32[]{:S(2)}) collective-permute-start(bf16[256,2048]{1,0:T(8,128)(2,1)} %get-tuple-element.262.refs_0_), channel_id=1, source_target_pairs={{0,1},{1,0},{2,3},{3,2},{4,5},{5,4},{6,7},{7,6},{8,9},{9,8},{10,11... | collective-permute-start | bytes 3145736 | tf_op jit(solution)/shard_map/middle_grad/ppermute | solution.py:40
  426.3 24.7 %collective-permute-start.59 = (bf16[256,2048]{1,0:T(8,128)(2,1)}, bf16[256,2048]{1,0:T(8,128)(2,1)}, u32[]{:S(2)}, u32[]{:S(2)}) collective-permute-start(bf16[256,2048]{1,0:T(8,128)(2,1)} %get-tuple-element.285), channel_id=1, source_target_pairs={{0,2},{1,3},{2,0},{3,1},{4,6},{5,7},{6,4},{7,5},{8,10},{9,11},{10,... | collective-permute-start | bytes 3145736 | tf_op jit(solution)/shard_map/mlp_out/ppermute | solution.py:40
  427.8 24.4 %collective-permute-start.60 = (bf16[256,2048]{1,0:T(8,128)(2,1)}, bf16[256,2048]{1,0:T(8,128)(2,1)}, u32[]{:S(2)}, u32[]{:S(2)}) collective-permute-start(bf16[256,2048]{1,0:T(8,128)(2,1)} %get-tuple-element.286), channel_id=1, source_target_pairs={{0,4},{4,0},{1,5},{5,1},{2,6},{6,2},{3,7},{7,3},{8,12},{12,8},{9,1... | collective-permute-start | bytes 3145736 | tf_op jit(solution)/shard_map/mlp_out/ppermute | solution.py:40
  490.9 28.4 %collective-permute-start.67 = (bf16[256,2048]{1,0:T(8,128)(2,1)S(1)}, bf16[256,2048]{1,0:T(8,128)(2,1)}, u32[]{:S(2)}, u32[]{:S(2)}) collective-permute-start(bf16[256,2048]{1,0:T(8,128)(2,1)S(1)} %copy-done.51), channel_id=1, source_target_pairs={{0,1},{1,0},{2,3},{3,2},{4,5},{5,4},{6,7},{7,6},{8,9},{9,8},{10,11... | collective-permute-start | bytes 3145736 | tf_op jit(solution)/shard_map/norm_one_grad/ppermute | solution.py:40
  491.4 27.9 %collective-permute-start.68 = (bf16[256,2048]{1,0:T(8,128)(2,1)S(1)}, bf16[256,2048]{1,0:T(8,128)(2,1)}, u32[]{:S(2)}, u32[]{:S(2)}) collective-permute-start(bf16[256,2048]{1,0:T(8,128)(2,1)S(1)} %copy-done.50), channel_id=1, source_target_pairs={{0,1},{1,0},{2,3},{3,2},{4,5},{5,4},{6,7},{7,6},{8,9},{9,8},{10,11... | collective-permute-start | bytes 3145736 | tf_op jit(solution)/shard_map/norm_one_grad/ppermute | solution.py:40
  524.2 32.8 %collective-permute-start.69 = (bf16[256,2048]{1,0:T(8,128)(2,1)}, bf16[256,2048]{1,0:T(8,128)(2,1)}, u32[]{:S(2)}, u32[]{:S(2)}) collective-permute-start(bf16[256,2048]{1,0:T(8,128)(2,1)} %get-tuple-element.310), channel_id=1, source_target_pairs={{0,2},{1,3},{2,0},{3,1},{4,6},{5,7},{6,4},{7,5},{8,10},{9,11},{10,... | collective-permute-start | bytes 3145736 | tf_op jit(solution)/shard_map/norm_one_grad/ppermute | solution.py:40
  525.4 31.7 %collective-permute-start.70 = (bf16[256,2048]{1,0:T(8,128)(2,1)}, bf16[256,2048]{1,0:T(8,128)(2,1)}, u32[]{:S(2)}, u32[]{:S(2)}) collective-permute-start(bf16[256,2048]{1,0:T(8,128)(2,1)} %get-tuple-element.311), channel_id=1, source_target_pairs={{0,4},{4,0},{1,5},{5,1},{2,6},{6,2},{3,7},{7,3},{8,12},{12,8},{9,1... | collective-permute-start | bytes 3145736 | tf_op jit(solution)/shard_map/norm_one_grad/ppermute | solution.py:40
  531.6 25.5 %collective-permute-start.71 = (bf16[256,768]{1,0:T(8,128)(2,1)S(1)}, bf16[256,768]{1,0:T(8,128)(2,1)S(1)}, u32[]{:S(2)}, u32[]{:S(2)}) collective-permute-start(bf16[256,768]{1,0:T(8,128)(2,1)S(1)} %get-tuple-element.380), channel_id=1, source_target_pairs={{0,4},{4,0},{1,5},{5,1},{2,6},{6,2},{3,7},{7,3},{8,12},{12,8},{9,1... | collective-permute-start | bytes 1179656 | tf_op jit(solution)/shard_map/ppermute | solution.py:40
  (112 other events, 1198.6 us)
Sparse Core Ops, SparseCore 0:
  23.3 64.9 all-gather.3
  90.5 113.9 all-gather.5
  206.1 61.7 all-gather.7
  270.6 58.8 reduce-scatter.3
  352.1 107.8 reduce-scatter.7
  464.7 58.7 reduce-scatter.5

commit v4 on v3

--- a/solution.py
+++ b/solution.py
@@ -141,15 +141,18 @@
     )(left, right)
 
 
-def partial_rows(left, right, depth, place=0):
+def partial_rows(left, right, depth, place=0, beside=()):
     low = jnp.bfloat16
     near_cross, far_cross = cross_call(left, right, depth, place)
     far_cross, left = together(far_cross, left)
     rest_far = part_call(left, right, depth, place, 4, low)
-    far_cross, *rest_far = together(swap(far_cross, CORE), *rest_far)
+    far_cross, *rest = together(swap(far_cross, CORE), *rest_far, *beside, *[left] * bool(beside))
+    rest_far = rest[:3]
+    if beside:
+        *beside, left = rest[3:]
     cross = (near_cross + far_cross.astype(jnp.float32)).astype(low)
     near = near_call(left, right, depth, place)
-    return (cross, near, [swap(block, CORE) for block in rest_far])
+    return (cross, near, [swap(block, CORE) for block in rest_far], *beside)
 
 
 def scatter_cross(cross):
@@ -168,7 +171,7 @@
 
 def near_sums(near, far, from_pair, from_chip):
     rows, columns = far[1].shape
-    steps = 4
+    steps = 2
     half = steps // 2
     block = (rows // steps, columns)
     straight = pl.BlockSpec(block, lambda i: (i, 0))
@@ -1008,6 +1011,7 @@
         output_half, raw_width // output_half,
     )
     moved = named("mlp_out", scatter_cross, mlp_cross)
+    context_grad, *moved = together(context_grad, *moved)
     mlp_chip, mlp_pair = named("mlp_out", near_sums, mlp_near, mlp_far, *moved)
     context_grad, mlp_chip, mlp_pair = together(context_grad, mlp_chip, mlp_pair)
     mlp_chip, mlp_pair = named("mlp_out", scatter_near, mlp_chip, mlp_pair)
@@ -1020,8 +1024,12 @@
     place = lax.axis_index("inner").astype(jnp.int32)[None]
     down = (down_first, down_second, down_weight)
     gateup = (gateup_first, gateup_second, gateup_weight)
-    cross, near, far = named("norm_one_grad", partial_rows, raw_grad, full_attn, raw_width)
-    cross, gateup_other = together(cross, gateup_other)
+    cross, near, far, gateup_other = named(
+        "norm_one_grad", partial_rows, raw_grad, full_attn, raw_width, 0, (gateup_other,)
+    )
+    final = middle + mlp_part
+    result = final.astype(low)
+    rms_values = jnp.stack([root_mean(attn_part), root_mean(mlp_part), root_mean(final)])[:, None, :]
     moved = named("norm_one_grad", scatter_cross, cross)
     near, far[0], from_pair, from_chip = together(near, far[0], *moved)
     chip, pair = named("norm_one_grad", near_sums, near, far, from_pair, from_chip)
@@ -1032,13 +1040,10 @@
     new_gateup_first, new_gateup_second, gateup_update, gateup_sums = step_call(
         "gateup_step", stacked_step, place, gateup_mine, gateup_other, [gateup], [2]
     )
-    final = middle + mlp_part
-    result = final.astype(low)
-    rms_values = jnp.stack([root_mean(attn_part), root_mean(mlp_part), root_mean(final)])[:, None, :]
-    attn_own, result, rms_values, gain_two_grad = together(attn_own, result, rms_values, gain_two_grad)
+    attn_own, gain_two_grad = together(attn_own, gain_two_grad)
     attn_mine, attn_other = own_grads(attn_own)
-    chip, pair, gateup_sums, down_sums, attn_other = together(
-        chip, pair, gateup_sums, down_sums, attn_other
+    chip, pair, gateup_sums, down_sums, attn_other, result, rms_values = together(
+        chip, pair, gateup_sums, down_sums, attn_other, result, rms_values
     )
     normed_one = all_sums(near, far, chip, pair)
     input_norm, gain_one_grad = norm_back(normed_one, hat_one, inv_one, gain_one)

time: 614 us -> 605 us (0.985)
    ppermute x77, waiting for transfers between devices: 179 us -> 166 us  [swap(): lax.ppermute(values, axis, [(i, i ^ bit) for i in range(lax.axis_size(axi...]
    unnamed x113 -> x109, local copies, waits for them, and re-layouts: 13.9 us -> 12.6 us
  transfers between devices with their start and end apart: 83 -> 83, of which waited for: 38 -> 40; matrix products, arithmetic and copies ran while one was open for 11% -> 11% of each run, Pallas kernels for 41% -> 41%
where the time goes in v4:
time: 605 us; the launch traced here: 599 us
  Pallas kernels  263 us (43%)
  waiting for transfers between devices  180 us (30%)
  starting transfers between devices  53.9 us (9%)
  other arithmetic  47.5 us (8%)
  local copies, waits for them, and re-layouts  39.5 us (7%)
  between operations  15.7 us (3%)
    ppermute x77, waiting for transfers between devices, swap(): lax.ppermute(values, axis, [(i, i ^ bit) for i in range(lax.axis_size(axi...  166 us
    ppermute x77, starting transfers between devices, swap(): lax.ppermute(values, axis, [(i, i ^ bit) for i in range(lax.axis_size(axi...  52.4 us
    pallas_call x3, Pallas kernels, product_first(): pl.pallas_call(first_kernel, out_shape=jax.ShapeDtypeStruct((depth, colum...  41.8 us
    pallas_call x3, Pallas kernels, rows_call(): pl.pallas_call(functools.partial(rows_kernel, finish, len(pieces), len(we...  39.4 us
    pallas_call x4, Pallas kernels, part_call(): pl.pallas_call(part_kernel, out_shape=(jax.ShapeDtypeStruct((rows, column...  28.9 us
    pallas_call x4, Pallas kernels, near_call(): pl.pallas_call(near_kernel, out_shape=jax.ShapeDtypeStruct((3 * rows, col...  27.5 us
    pallas_call x4, Pallas kernels, cross_call(): pl.pallas_call(cross_kernel, out_shape=(jax.ShapeDtypeStruct(shape, jnp.f...  23.9 us
    pallas_call x1, Pallas kernels, attend_backward(): pl.pallas_call(functools.partial(backward_kernel, rows, blocks, heads), o...  22.3 us
  transfers between devices with their start and end apart: 83, of which 40 were waited for; matrix products, arithmetic and copies ran while one was open for 11% of the time, Pallas kernels for 41%

profile of v4, /device:TPU:0, one launch (start us, length us, event | category | flops | bytes accessed | tf_op | source)
XLA Modules:
  0.0 599.2 jit_solution(10090624095927815315)
XLA Ops:
  13.3 8.8 %collective-permute-done.9 = bf16[256,768]{1,0:T(8,128)(2,1)S(1)} collective-permute-done((bf16[256,768]{1,0:T(8,128)(2,1)S(1)}, bf16[256,768]{1,0:T(8,128)(2,1)S(1)}, u32[]{:S(2)}, u32[]{:S(2)}) %collective-permute-start.9) | collective-permute-done | bytes 393248 | tf_op jit(solution)/shard_map/ppermute | solution.py:40
  41.2 10.6 %collective-permute-done.2 = s32[1]{0:T(128)} collective-permute-done((s32[1]{0:T(128)}, s32[1]{0:T(128)}, u32[]{:S(2)}, u32[]{:S(2)}) %collective-permute-start.2) | collective-permute-done | bytes 36 | tf_op jit(solution)/shard_map/ppermute | solution.py:40
  55.1 23.6 %collective-permute-done.4 = bf16[256,2304]{1,0:T(8,128)(2,1)S(1)} collective-permute-done((bf16[256,2304]{1,0:T(8,128)(2,1)S(1)}, bf16[256,2304]{1,0:T(8,128)(2,1)S(1)}, u32[]{:S(2)}, u32[]{:S(2)}) %collective-permute-start.4) | collective-permute-done | bytes 1179680 | tf_op jit(solution)/shard_map/ppermute | solution.py:40
  91.3 10.3 %query_key_value.1 = (f32[8,256,512]{2,1,0:T(8,128)}, bf16[8,256,2048]{2,1,0:T(8,128)(2,1)}) custom-call(bf16[256,2048]{1,0:T(8,128)(2,1)} %fusion.4.refs_0_, bf16[256,2048]{1,0:T(8,128)(2,1)} %collective-permute-done.refs_1_, bf16[256,2048]{1,0:T(8,128)(2,1)} %collective-permute-done.1.refs_2_, bf16[256,2048]{1,0:T(8,128)(2,1)} %copy-done.23, ...), custom_call_target="tpu_custom_call" | custom-call | flops 1024 | bytes 1024 | tf_op jit(solution)/shard_map/query_key_value/pallas_call | solution.py:388
  101.6 10.9 %attend_forward.1 = bf16[2,2,2,256,256]{4,3,2,1,0:T(8,128)(2,1)} custom-call(s32[3]{0:T(128)} %pad_add_fusion.meta, f32[2,2,2,256,512]{4,3,2,1,0:T(8,128)} %bitcast.92, f32[2,128]{1,0:T(2,128)} %slice_bitcast_fusion.3.gains, f32[1024,128]{1,0:T(8,128)} %get-tuple-element.200.cos_ref, f32[1024,128]{1,0:T(8,128)} %get-tuple-element.201.sin_ref), custom_call_target="tpu_custom_call" | custom-call | flops 1024 | bytes 1024 | tf_op jit(solution)/shard_map/attend_forward/pallas_call | solution.py:616
  134.5 7.0 %collective-permute-done.14.from_pair = bf16[128,2048]{1,0:T(8,128)(2,1)S(1)} collective-permute-done((bf16[128,2048]{1,0:T(8,128)(2,1)S(1)}, bf16[128,2048]{1,0:T(8,128)(2,1)S(1)}, u32[]{:S(2)}, u32[]{:S(2)}) %collective-permute-start.14) | collective-permute-done | bytes 524320 | tf_op jit(solution)/shard_map/attention_out/ppermute | solution.py:40
  152.0 20.6 %collective-permute-done.18 = bf16[256,2048]{1,0:T(8,128)(2,1)S(1)} collective-permute-done((bf16[256,2048]{1,0:T(8,128)(2,1)}, bf16[256,2048]{1,0:T(8,128)(2,1)S(1)}, u32[]{:S(2)}, u32[]{:S(2)}) %collective-permute-start.18) | collective-permute-done | bytes 1048608 | tf_op jit(solution)/shard_map/attention_out/ppermute | solution.py:40
  179.6 21.7 %collective-permute-done.20.refs_1_ = bf16[256,2048]{1,0:T(8,128)(2,1)S(1)} collective-permute-done((bf16[256,2048]{1,0:T(8,128)(2,1)S(1)}, bf16[256,2048]{1,0:T(8,128)(2,1)S(1)}, u32[]{:S(2)}, u32[]{:S(2)}) %collective-permute-start.20) | collective-permute-done | bytes 1048608 | tf_op jit(solution)/shard_map/norm_two/ppermute | solution.py:40
  204.8 8.0 %collective-permute-done.22.refs_3_ = bf16[128,2048]{1,0:T(8,128)(2,1)S(1)} collective-permute-done((bf16[128,2048]{1,0:T(8,128)(2,1)S(1)}, bf16[128,2048]{1,0:T(8,128)(2,1)S(1)}, u32[]{:S(2)}, u32[]{:S(2)}) %collective-permute-start.22) | collective-permute-done | bytes 524320 | tf_op jit(solution)/shard_map/norm_two/ppermute | solution.py:40
  223.1 20.2 %gate_up.1 = (bf16[8,256,1536]{2,1,0:T(8,128)(2,1)}, bf16[8,256,768]{2,1,0:T(8,128)(2,1)}, bf16[8,256,2048]{2,1,0:T(8,128)(2,1)}) custom-call(bf16[256,2048]{1,0:T(8,128)(2,1)} %copy-done.7, bf16[256,2048]{1,0:T(8,128)(2,1)} %copy-done.12, bf16[256,2048]{1,0:T(8,128)(2,1)} %copy-done.13, bf16[128,2048]{1,0:T(8,128)(2,1)} %copy-done.24, ...), custom_call_target="tpu_custom_call" | custom-call | flops 1024 | bytes 1024 | tf_op jit(solution)/shard_map/gate_up/pallas_call | solution.py:388
  253.0 10.9 %down_weight_grad.1 = bf16[2048,768]{1,0:T(8,128)(2,1)} custom-call(bf16[2048,2048]{1,0:T(8,128)(2,1)} %bitcast.78, bf16[2048,768]{1,0:T(8,128)(2,1)} %bitcast.80), custom_call_target="tpu_custom_call" | custom-call | flops 1024 | bytes 1024 | tf_op jit(solution)/shard_map/down_weight_grad/pallas_call | solution.py:227
  268.2 14.5 %hidden_grad.1.left.refs_1_ = bf16[2048,1536]{1,0:T(8,128)(2,1)} custom-call(bf16[2048,2048]{1,0:T(8,128)(2,1)} %bitcast.79, bf16[2048,768]{1,0:T(8,128)(2,1)} %all-gather.8.cloned.1.call-done.weight.right, bf16[2048,1536]{1,0:T(8,128)(2,1)} %bitcast.96), custom_call_target="tpu_custom_call" | custom-call | flops 1024 | bytes 1024 | tf_op jit(solution)/shard_map/hidden_grad/pallas_call | solution.py:423
  282.7 8.6 %cross.5 = (f32[256,2048]{1,0:T(8,128)}, bf16[256,2048]{1,0:T(8,128)(2,1)}) custom-call(bf16[2048,1536]{1,0:T(8,128)(2,1)} %hidden_grad.1.left.refs_1_, bf16[2048,1536]{1,0:T(8,128)(2,1)} %all-gather.6.cloned.1.call-done.refs_10_.right), custom_call_target="tpu_custom_call" | custom-call | flops 1024 | bytes 1024 | tf_op jit(solution)/shard_map/norm_two_grad/cross/pallas_call | solution.py:79
  291.3 10.5 %part.5 = (bf16[256,2048]{1,0:T(8,128)(2,1)}, bf16[256,2048]{1,0:T(8,128)(2,1)}, bf16[256,2048]{1,0:T(8,128)(2,1)}) custom-call(bf16[2048,1536]{1,0:T(8,128)(2,1)} %hidden_grad.1.left.refs_1_, bf16[2048,1536]{1,0:T(8,128)(2,1)} %all-gather.6.cloned.1.call-done.refs_10_.right), custom_call_target="tpu_custom_call" | custom-call | flops 1024 | bytes 1024 | tf_op jit(solution)/shard_map/norm_two_grad/part/pallas_call | solution.py:130
  309.1 10.0 %near.5.near_chip.near_pair = f32[768,2048]{1,0:T(8,128)} custom-call(bf16[2048,1536]{1,0:T(8,128)(2,1)} %hidden_grad.1.left.refs_1_, bf16[2048,1536]{1,0:T(8,128)(2,1)} %all-gather.6.cloned.1.call-done.refs_10_.right), custom_call_target="tpu_custom_call" | custom-call | flops 1024 | bytes 1024 | tf_op jit(solution)/shard_map/norm_two_grad/near/pallas_call | solution.py:113
  328.0 18.5 %gateup_weight_grad.1 = bf16[2048,1536]{1,0:T(8,128)(2,1)} custom-call(bf16[2048,2048]{1,0:T(8,128)(2,1)} %bitcast.102, bf16[2048,1536]{1,0:T(8,128)(2,1)} %hidden_grad.1.left.refs_1_), custom_call_target="tpu_custom_call" | custom-call | flops 12884901888 | bytes 8388608 | tf_op jit(solution)/shard_map/gateup_weight_grad/pallas_call | solution.py:227
  376.5 7.1 %part.6 = (bf16[256,2048]{1,0:T(8,128)(2,1)}, bf16[256,2048]{1,0:T(8,128)(2,1)}, bf16[256,2048]{1,0:T(8,128)(2,1)}) custom-call(bf16[2048,768]{1,0:T(8,128)(2,1)} %bitcast.83, bf16[2048,768]{1,0:T(8,128)(2,1)} %all-gather.8.cloned.1.call-done.weight.right), custom_call_target="tpu_custom_call" | custom-call | flops 1024 | bytes 1024 | tf_op jit(solution)/shard_map/mlp_out/part/pallas_call | solution.py:130
  391.2 9.2 %collective-permute-done.47.refs_3_ = bf16[128,2048]{1,0:T(8,128)(2,1)S(1)} collective-permute-done((bf16[128,2048]{1,0:T(8,128)(2,1)S(1)}, bf16[128,2048]{1,0:T(8,128)(2,1)S(1)}, u32[]{:S(2)}, u32[]{:S(2)}) %collective-permute-start.47) | collective-permute-done | bytes 524320 | tf_op jit(solution)/shard_map/middle_grad/ppermute | solution.py:40
  408.3 8.9 %context_grad.1 = (bf16[8,256,256]{2,1,0:T(8,128)(2,1)}, bf16[8,256,2048]{2,1,0:T(8,128)(2,1)}) custom-call(bf16[256,2048]{1,0:T(8,128)(2,1)} %get-tuple-element.264.refs_0_, bf16[256,2048]{1,0:T(8,128)(2,1)} %collective-permute-done.45.refs_1_, bf16[256,2048]{1,0:T(8,128)(2,1)} %collective-permute-done.46.refs_2_, bf16[128,2048]{1,0:T(8,128)(2,1)} %copy-done.26, ...), custom_call_target="tpu_custom_call" | custom-call | flops 1024 | bytes 1024 | tf_op jit(solution)/shard_map/context_grad/pallas_call | solution.py:388
  427.6 22.3 %attend_backward.1 = (bf16[2,2,2,256,512]{4,3,2,1,0:T(8,128)(2,1)}, f32[2,2,128]{2,1,0:T(2,128)}) custom-call(s32[3]{0:T(128)} %pad_add_fusion.meta, f32[2,2,2,256,512]{4,3,2,1,0:T(8,128)} %bitcast.93, bf16[2,2,2,256,256]{4,3,2,1,0:T(8,128)(2,1)} %bitcast.98, f32[2,128]{1,0:T(2,128)} %slice_bitcast_fusion.3.gains, f32[1024,128]{1,0:T(8,128)} %get-tuple-element.200.cos_ref, ...), custom_call_target="tpu_custom_call" | custom-call | flops 1024 | bytes 1024 | tf_op jit(solution)/shard_map/attend_backward/pallas_call | solution.py:647
  450.7 12.5 %attention_weight_grad.1 = bf16[2048,768]{1,0:T(8,128)(2,1)} custom-call(bf16[2048,2048]{1,0:T(8,128)(2,1)} %bitcast.94, bf16[2048,512]{1,0:T(8,128)(2,1)} %bitcast.84, bf16[2048,2048]{1,0:T(8,128)(2,1)} %bitcast.95, bf16[2048,256]{1,0:T(8,128)(2,1)} %bitcast.91), custom_call_target="tpu_custom_call" | custom-call | flops 1024 | bytes 1024 | tf_op jit(solution)/shard_map/attention_weight_grad/pallas_call | solution.py:227
  484.0 7.4 %collective-permute-done.62.other = bf16[256,1536]{1,0:T(8,128)(2,1)} collective-permute-done((bf16[256,1536]{1,0:T(8,128)(2,1)}, bf16[256,1536]{1,0:T(8,128)(2,1)}, u32[]{:S(2)}, u32[]{:S(2)}) %collective-permute-start.62) | collective-permute-done | bytes 786464 | tf_op jit(solution)/shard_map/ppermute | solution.py:40
  529.8 8.4 %gateup_step.1 = (f32[2,256,1536]{2,1,0:T(8,128)}, f32[2,256,1536]{2,1,0:T(8,128)}, f32[2,256,1536]{2,1,0:T(8,128)}, f32[8,128]{1,0:T(8,128)}) custom-call(s32[1]{0:T(128)} %bitcast.27.meta, bf16[256,1536]{1,0:T(8,128)(2,1)} %get-tuple-element.373.mine, bf16[256,1536]{1,0:T(8,128)(2,1)} %collective-permute-done.62.other, f32[2,256,1536]{2,1,0:T(8,128)} %one.2, ...), custom_call_target="tpu_custom_call" | custom-call | flops 1024 | bytes 1024 | tf_op jit(solution)/shard_map/gateup_step/pallas_call | solution.py:786
  538.2 10.1 %collective-permute-done.70.other = bf16[256,768]{1,0:T(8,128)(2,1)S(1)} collective-permute-done((bf16[256,768]{1,0:T(8,128)(2,1)}, bf16[256,768]{1,0:T(8,128)(2,1)S(1)}, u32[]{:S(2)}, u32[]{:S(2)}) %collective-permute-start.70) | collective-permute-done | bytes 393248 | tf_op jit(solution)/shard_map/ppermute | solution.py:40
  (364 shorter events, 282.9 us)
Async XLA Ops:
  7.2 81.1 %all-gather.4.cloned.1.call-start = ((), (), s32[]{:S(2)}) async-start(), calls=%async_computation.3 | async-start | bytes 3932160 | tf_op jit(solution)/shard_map/all_gather | solution.py:872
  23.2 199.9 %all-gather.6.cloned.1.call-start = ((), (), s32[]{:S(2)}) async-start(), calls=%async_computation.4 | async-start | bytes 7864320 | tf_op jit(solution)/shard_map/all_gather | solution.py:872
  26.0 27.0 %collective-permute-start = (bf16[256,2048]{1,0:T(8,128)(2,1)}, bf16[256,2048]{1,0:T(8,128)(2,1)}, u32[]{:S(2)}, u32[]{:S(2)}) collective-permute-start(bf16[256,2048]{1,0:T(8,128)(2,1)} %fusion.4.refs_0_), channel_id=1, source_target_pairs={{0,2},{1,3},{2,0},{3,1},{4,6},{5,7},{6,4},{7,5},{8,10},{9,11},{10,... | collective-permute-start | bytes 3145736 | tf_op jit(solution)/shard_map/norm_one/ppermute | solution.py:40
  27.7 25.3 %collective-permute-start.1 = (bf16[256,2048]{1,0:T(8,128)(2,1)}, bf16[256,2048]{1,0:T(8,128)(2,1)}, u32[]{:S(2)}, u32[]{:S(2)}) collective-permute-start(bf16[256,2048]{1,0:T(8,128)(2,1)} %fusion.4.refs_0_), channel_id=1, source_target_pairs={{0,4},{4,0},{1,5},{5,1},{2,6},{6,2},{3,7},{7,3},{8,12},{12,8},{9,1... | collective-permute-start | bytes 3145736 | tf_op jit(solution)/shard_map/norm_one/ppermute | solution.py:40
  53.0 25.6 %collective-permute-start.4 = (bf16[256,2304]{1,0:T(8,128)(2,1)S(1)}, bf16[256,2304]{1,0:T(8,128)(2,1)S(1)}, u32[]{:S(2)}, u32[]{:S(2)}) collective-permute-start(bf16[256,2304]{1,0:T(8,128)(2,1)S(1)} %pad_maximum_fusion.1), channel_id=1, source_target_pairs={{0,4},{4,0},{1,5},{5,1},{2,6},{6,2},{3,7},{7,3},{8,12},{12,8},{9,1... | collective-permute-start | bytes 3538952 | tf_op jit(solution)/shard_map/ppermute | solution.py:40
  54.5 24.7 %collective-permute-start.3 = (bf16[256,2048]{1,0:T(8,128)(2,1)}, bf16[256,2048]{1,0:T(8,128)(2,1)S(1)}, u32[]{:S(2)}, u32[]{:S(2)}) collective-permute-start(bf16[256,2048]{1,0:T(8,128)(2,1)} %collective-permute-done.1.refs_2_), channel_id=1, source_target_pairs={{0,2},{1,3},{2,0},{3,1},{4,6},{5,7},{6,4},{7,5},{8,10},{9,11},{10,... | collective-permute-start | bytes 3145736 | tf_op jit(solution)/shard_map/norm_one/ppermute | solution.py:40
  82.0 185.9 %all-gather.8.cloned.1.call-start = ((), (), s32[]{:S(2)}) async-start(), calls=%async_computation.5 | async-start | bytes 3932160 | tf_op jit(solution)/shard_map/all_gather | solution.py:872
  88.3 25.2 %collective-permute-start.10 = (bf16[256,2048]{1,0:T(8,128)(2,1)}, bf16[256,2048]{1,0:T(8,128)(2,1)}, u32[]{:S(2)}, u32[]{:S(2)}) collective-permute-start(bf16[256,2048]{1,0:T(8,128)(2,1)} %fusion.13.refs_0_), channel_id=1, source_target_pairs={{0,2},{1,3},{2,0},{3,1},{4,6},{5,7},{6,4},{7,5},{8,10},{9,11},{10,... | collective-permute-start | bytes 3145736 | tf_op jit(solution)/shard_map/output_grad/ppermute | solution.py:40
  89.8 24.9 %collective-permute-start.11 = (bf16[256,2048]{1,0:T(8,128)(2,1)}, bf16[256,2048]{1,0:T(8,128)(2,1)}, u32[]{:S(2)}, u32[]{:S(2)}) collective-permute-start(bf16[256,2048]{1,0:T(8,128)(2,1)} %fusion.13.refs_0_), channel_id=1, source_target_pairs={{0,4},{4,0},{1,5},{5,1},{2,6},{6,2},{3,7},{7,3},{8,12},{12,8},{9,1... | collective-permute-start | bytes 3145736 | tf_op jit(solution)/shard_map/output_grad/ppermute | solution.py:40
  148.2 24.4 %collective-permute-start.18 = (bf16[256,2048]{1,0:T(8,128)(2,1)}, bf16[256,2048]{1,0:T(8,128)(2,1)S(1)}, u32[]{:S(2)}, u32[]{:S(2)}) collective-permute-start(bf16[256,2048]{1,0:T(8,128)(2,1)} %get-tuple-element.221), channel_id=1, source_target_pairs={{0,2},{1,3},{2,0},{3,1},{4,6},{5,7},{6,4},{7,5},{8,10},{9,11},{10,... | collective-permute-start | bytes 3145736 | tf_op jit(solution)/shard_map/attention_out/ppermute | solution.py:40
  148.8 24.8 %collective-permute-start.19 = (bf16[256,2048]{1,0:T(8,128)(2,1)}, bf16[256,2048]{1,0:T(8,128)(2,1)}, u32[]{:S(2)}, u32[]{:S(2)}) collective-permute-start(bf16[256,2048]{1,0:T(8,128)(2,1)} %get-tuple-element.222), channel_id=1, source_target_pairs={{0,4},{4,0},{1,5},{5,1},{2,6},{6,2},{3,7},{7,3},{8,12},{12,8},{9,1... | collective-permute-start | bytes 3145736 | tf_op jit(solution)/shard_map/attention_out/ppermute | solution.py:40
  151.4 200.0 %reduce-scatter.4.cloned.1.call-start = ((), (), s32[]{:S(2)}) async-start(), calls=%async_computation.6 | async-start | bytes 3932160 | tf_op jit(solution)/shard_map/reduce_scatter | solution.py:876
  179.6 38.5 %collective-permute-start.24 = (bf16[256,2048]{1,0:T(8,128)(2,1)S(1)}, bf16[256,2048]{1,0:T(8,128)(2,1)S(1)}, u32[]{:S(2)}, u32[]{:S(2)}) collective-permute-start(bf16[256,2048]{1,0:T(8,128)(2,1)S(1)} %multiply_convert_fusion.refs_0_), channel_id=1, source_target_pairs={{0,1},{1,0},{2,3},{3,2},{4,5},{5,4},{6,7},{7,6},{8,9},{9,8},{10,11... | collective-permute-start | bytes 3145736 | tf_op jit(solution)/shard_map/norm_two/ppermute | solution.py:40
  218.2 25.1 %collective-permute-start.29 = (bf16[128,2048]{1,0:T(8,128)(2,1)}, bf16[128,2048]{1,0:T(8,128)(2,1)}, u32[]{:S(2)}, u32[]{:S(2)}) collective-permute-start(bf16[128,2048]{1,0:T(8,128)(2,1)} %slice.130), channel_id=1, source_target_pairs={{0,4},{4,0},{1,5},{5,1},{2,6},{6,2},{3,7},{7,3},{8,12},{12,8},{9,1... | collective-permute-start | bytes 1572872 | tf_op jit(solution)/shard_map/output_grad/ppermute | solution.py:40
  219.0 24.2 %collective-permute-start.30 = (bf16[128,2048]{1,0:T(8,128)(2,1)}, bf16[128,2048]{1,0:T(8,128)(2,1)}, u32[]{:S(2)}, u32[]{:S(2)}) collective-permute-start(bf16[128,2048]{1,0:T(8,128)(2,1)} %slice.131), channel_id=1, source_target_pairs={{0,2},{1,3},{2,0},{3,1},{4,6},{5,7},{6,4},{7,5},{8,10},{9,11},{10,... | collective-permute-start | bytes 1572872 | tf_op jit(solution)/shard_map/output_grad/ppermute | solution.py:40
  267.9 200.4 %reduce-scatter.6.cloned.1.call-start = ((), (), s32[]{:S(2)}) async-start(), calls=%async_computation.7 | async-start | bytes 7864320 | tf_op jit(solution)/shard_map/reduce_scatter | solution.py:876
  325.9 24.3 %collective-permute-start.42 = (bf16[256,2048]{1,0:T(8,128)(2,1)}, bf16[256,2048]{1,0:T(8,128)(2,1)}, u32[]{:S(2)}, u32[]{:S(2)}) collective-permute-start(bf16[256,2048]{1,0:T(8,128)(2,1)} %get-tuple-element.255), channel_id=1, source_target_pairs={{0,2},{1,3},{2,0},{3,1},{4,6},{5,7},{6,4},{7,5},{8,10},{9,11},{10,... | collective-permute-start | bytes 3145736 | tf_op jit(solution)/shard_map/norm_two_grad/ppermute | solution.py:40
  327.4 24.0 %collective-permute-start.43 = (bf16[256,2048]{1,0:T(8,128)(2,1)}, bf16[256,2048]{1,0:T(8,128)(2,1)}, u32[]{:S(2)}, u32[]{:S(2)}) collective-permute-start(bf16[256,2048]{1,0:T(8,128)(2,1)} %get-tuple-element.256), channel_id=1, source_target_pairs={{0,4},{4,0},{1,5},{5,1},{2,6},{6,2},{3,7},{7,3},{8,12},{12,8},{9,1... | collective-permute-start | bytes 3145736 | tf_op jit(solution)/shard_map/norm_two_grad/ppermute | solution.py:40
  351.4 171.6 %reduce-scatter.8.cloned.1.call-start = ((), (), s32[]{:S(2)}) async-start(), calls=%async_computation.8 | async-start | bytes 3932160 | tf_op jit(solution)/shard_map/reduce_scatter | solution.py:876
  425.3 24.6 %collective-permute-start.59 = (bf16[256,2048]{1,0:T(8,128)(2,1)}, bf16[256,2048]{1,0:T(8,128)(2,1)}, u32[]{:S(2)}, u32[]{:S(2)}) collective-permute-start(bf16[256,2048]{1,0:T(8,128)(2,1)} %get-tuple-element.290), channel_id=1, source_target_pairs={{0,2},{1,3},{2,0},{3,1},{4,6},{5,7},{6,4},{7,5},{8,10},{9,11},{10,... | collective-permute-start | bytes 3145736 | tf_op jit(solution)/shard_map/mlp_out/ppermute | solution.py:40
  426.7 24.0 %collective-permute-start.60 = (bf16[256,2048]{1,0:T(8,128)(2,1)}, bf16[256,2048]{1,0:T(8,128)(2,1)}, u32[]{:S(2)}, u32[]{:S(2)}) collective-permute-start(bf16[256,2048]{1,0:T(8,128)(2,1)} %get-tuple-element.291), channel_id=1, source_target_pairs={{0,4},{4,0},{1,5},{5,1},{2,6},{6,2},{3,7},{7,3},{8,12},{12,8},{9,1... | collective-permute-start | bytes 3145736 | tf_op jit(solution)/shard_map/mlp_out/ppermute | solution.py:40
  472.2 24.1 %collective-permute-start.71 = (bf16[256,2048]{1,0:T(8,128)(2,1)}, bf16[256,2048]{1,0:T(8,128)(2,1)}, u32[]{:S(2)}, u32[]{:S(2)}) collective-permute-start(bf16[256,2048]{1,0:T(8,128)(2,1)} %get-tuple-element.318), channel_id=1, source_target_pairs={{0,1},{1,0},{2,3},{3,2},{4,5},{5,4},{6,7},{7,6},{8,9},{9,8},{10,11... | collective-permute-start | bytes 3145736 | tf_op jit(solution)/shard_map/mlp_out/ppermute | solution.py:40
  515.1 33.2 %collective-permute-start.68 = (bf16[256,2048]{1,0:T(8,128)(2,1)}, bf16[256,2048]{1,0:T(8,128)(2,1)}, u32[]{:S(2)}, u32[]{:S(2)}) collective-permute-start(bf16[256,2048]{1,0:T(8,128)(2,1)} %get-tuple-element.309), channel_id=1, source_target_pairs={{0,2},{1,3},{2,0},{3,1},{4,6},{5,7},{6,4},{7,5},{8,10},{9,11},{10,... | collective-permute-start | bytes 3145736 | tf_op jit(solution)/shard_map/norm_one_grad/ppermute | solution.py:40
  515.4 32.9 %collective-permute-start.69 = (bf16[256,2048]{1,0:T(8,128)(2,1)}, bf16[256,2048]{1,0:T(8,128)(2,1)}, u32[]{:S(2)}, u32[]{:S(2)}) collective-permute-start(bf16[256,2048]{1,0:T(8,128)(2,1)} %get-tuple-element.310), channel_id=1, source_target_pairs={{0,4},{4,0},{1,5},{5,1},{2,6},{6,2},{3,7},{7,3},{8,12},{12,8},{9,1... | collective-permute-start | bytes 3145736 | tf_op jit(solution)/shard_map/norm_one_grad/ppermute | solution.py:40
  (110 other events, 1165.0 us)
Sparse Core Ops, SparseCore 0:
  23.3 64.9 all-gather.3
  90.5 113.9 all-gather.5
  206.1 61.7 all-gather.7
  270.7 58.8 reduce-scatter.3
  351.6 107.8 reduce-scatter.5
  463.3 59.6 reduce-scatter.7

commit v5 on v4

--- a/solution.py
+++ b/solution.py
@@ -259,11 +259,9 @@
     return gather_outer(in_order(mine, theirs, 0))
 
 
-def own_grads(values):
+def pair_rows(values):
     rows = values.shape[0] // 2
-    place = lax.axis_index("inner")
-    mine = lax.dynamic_slice_in_dim(values, place * rows, rows, 0)
-    return (mine, swap(lax.dynamic_slice_in_dim(values, (1 - place) * rows, rows, 0), PAIR))
+    return lax.dynamic_slice_in_dim(values, (1 - lax.axis_index("inner")) * rows, rows, 0)
 
 
 def total(values):
@@ -780,7 +778,8 @@
 
 
 def step_call(name, kernel, place, mine, other, arrays, axes):
-    fixed = pl.BlockSpec(mine.shape, lambda i, meta: (0, 0))
+    own = pl.BlockSpec(other.shape, lambda i, meta: (meta[0], 0))
+    fixed = pl.BlockSpec(other.shape, lambda i, meta: (0, 0))
     specs = [half_block(array, axis) for group, axis in zip(arrays, axes) for array in group]
     out_arrays = [(array, axis) for group, axis in zip(arrays, axes) for array in group]
     return pl.pallas_call(
@@ -790,7 +789,7 @@
         grid_spec=pltpu.PrefetchScalarGridSpec(
             num_scalar_prefetch=1,
             grid=(2,),
-            in_specs=[fixed, fixed] + specs,
+            in_specs=[own, fixed] + specs,
             out_specs=tuple(half_block(array, axis) for array, axis in out_arrays)
             + (pl.BlockSpec((8, HD), lambda i, meta: (0, 0)),),
         ),
@@ -835,9 +834,9 @@
 def gains_kernel(rows, sums, first, second, gains, new_first, new_second, new_gains, stats, trust):
     each = (rows - 2) // 2
     new_one, new_two = moments(sums[24 : 24 + rows, :], first[:rows, :], second[:rows, :])
-    for result, values in ((new_first, new_one), (new_second, new_two), (new_gains, new_one)):
-        result[:rows, :] = values
-        result[rows:, :] = jnp.zeros_like(result[rows:, :])
+    for row in range(rows):
+        new_first[row * HD : (row + 1) * HD] = new_one[row]
+        new_second[row * HD : (row + 1) * HD] = new_two[row]
     lane = lax.broadcasted_iota(jnp.int32, (1, HD), 1)
     weight_row = jnp.zeros((1, HD), jnp.float32)
     update_row = jnp.zeros((1, HD), jnp.float32)
@@ -853,7 +852,9 @@
         old = gains[span, :]
         update = update_of(new_one[span, :], new_two[span, :], old)
         weight_square, update_square = (square(old), square(update))
-        new_gains[span, :] = old - LEARN * ratio_of(weight_square, update_square) * update
+        new_old = old - LEARN * ratio_of(weight_square, update_square) * update
+        for row in range(size):
+            new_gains[(start + row) * HD : (start + row + 1) * HD] = new_old[row]
         weight_row, update_row = put(place, weight_square, update_square, weight_row, update_row)
     for place, index in ((1, 16), (2, 18), (3, 20), (6, 22), (8, 0), (9, 2), (10, 8)):
         weight_row, update_row = put(
@@ -993,13 +994,13 @@
             flops=2 * whole_two.size * pair_grad.shape[1], transcendentals=0, bytes_accessed=2 * whole_two.size
         ),
     )
-    chip, pair, down_own, gateup_grad = together(chip, pair, down_own, gateup_grad)
+    down_other = pair_rows(down_own)
+    chip, pair, down_other, gateup_grad = together(chip, pair, down_other, gateup_grad)
     gateup_own = scatter_outer(gateup_grad)
     normed_two = all_sums(near, far, chip, pair)
     middle_norm, gain_two_grad = norm_back(normed_two, hat_two, inv_two, gain_two)
     middle_grad = grad_out + middle_norm
-    down_mine, down_other = own_grads(down_own)
-    middle_low, down_other = together(middle_grad.astype(low), down_other)
+    middle_low, down_other = together(middle_grad.astype(low), swap(down_other, PAIR))
     chip, pair = named("middle_grad", gather_start, middle_low)
     cross = named("middle_grad", gather_cross, chip, pair, True)
     hidden, middle_low = together(hidden, middle_low)
@@ -1020,7 +1021,7 @@
     mlp_part = all_sums(mlp_near, mlp_far, mlp_chip, mlp_pair)
     attn_grad = product_first("attention_weight_grad", (whole_one, raw_grad), (whole_mid, context))
     attn_own = scatter_outer(attn_grad)
-    gateup_mine, gateup_other = own_grads(gateup_own)
+    gateup_other = swap(pair_rows(gateup_own), PAIR)
     place = lax.axis_index("inner").astype(jnp.int32)[None]
     down = (down_first, down_second, down_weight)
     gateup = (gateup_first, gateup_second, gateup_weight)
@@ -1035,13 +1036,13 @@
     chip, pair = named("norm_one_grad", near_sums, near, far, from_pair, from_chip)
     chip, pair = named("norm_one_grad", scatter_near, chip, pair)
     new_down_first, new_down_second, down_update, down_sums = step_call(
-        "down_step", turned_step, place, down_mine, down_other, [down], [0]
+        "down_step", turned_step, place, down_own, down_other, [down], [0]
     )
     new_gateup_first, new_gateup_second, gateup_update, gateup_sums = step_call(
-        "gateup_step", stacked_step, place, gateup_mine, gateup_other, [gateup], [2]
+        "gateup_step", stacked_step, place, gateup_own, gateup_other, [gateup], [2]
     )
     attn_own, gain_two_grad = together(attn_own, gain_two_grad)
-    attn_mine, attn_other = own_grads(attn_own)
+    attn_other = swap(pair_rows(attn_own), PAIR)
     chip, pair, gateup_sums, down_sums, attn_other, result, rms_values = together(
         chip, pair, gateup_sums, down_sums, attn_other, result, rms_values
     )
@@ -1057,7 +1058,7 @@
     (
         new_query_first, new_query_second, query_update, new_keyval_first, new_keyval_second,
         keyval_update, new_output_first, new_output_second, output_update, attn_sums,
-    ) = step_call("attention_step", attn_step, place, attn_mine, attn_other, attn_arrays, [1, 2, 0])
+    ) = step_call("attention_step", attn_step, place, attn_own, attn_other, attn_arrays, [1, 2, 0])
     sums = jnp.concatenate(
         [gateup_sums, down_sums, attn_sums]
         + [gain_one_grad.reshape(-1, HD), gain_two_grad.reshape(-1, HD), head_gain_grad],
@@ -1083,7 +1084,7 @@
         4,
     )
     padded = -(-gain_rows // 8) * 8
-    gain_shape = jax.ShapeDtypeStruct((padded, HD), jnp.float32)
+    gain_shape = jax.ShapeDtypeStruct(norm_gains.shape, jnp.float32)
     new_gains_first, new_gains_second, new_gains, lamb_stats, trust = pl.pallas_call(
         functools.partial(gains_kernel, gain_rows),
         out_shape=(gain_shape, gain_shape, gain_shape)
@@ -1095,9 +1096,6 @@
             jnp.pad(values, (0, (padded - gain_rows) * HD)).reshape(padded, HD)
             for values in (gains_first, gains_second, norm_gains)
         ],
-    )
-    new_gains, new_gains_first, new_gains_second = (
-        values.reshape(-1)[: norm_gains.size] for values in (new_gains, new_gains_first, new_gains_second)
     )
     trust = trust[0]
     return (

time: 605 us -> 598 us (0.988)
    unnamed x109 -> x107, local copies, waits for them, and re-layouts: 12.6 us -> 12.6 us
  transfers between devices with their start and end apart: 83 -> 83, of which waited for: 40 -> 40; matrix products, arithmetic and copies ran while one was open for 11% -> 11% of each run, Pallas kernels for 41% -> 42%
where the time goes in v5:
time: 598 us; the launch traced here: 593 us
  Pallas kernels  263 us (44%)
  waiting for transfers between devices  179 us (30%)
  starting transfers between devices  53.9 us (9%)
  other arithmetic  47.5 us (8%)
  local copies, waits for them, and re-layouts  34.2 us (6%)
  between operations  15.7 us (3%)
    ppermute x77, waiting for transfers between devices, swap(): lax.ppermute(values, axis, [(i, i ^ bit) for i in range(lax.axis_size(axi...  163 us
    ppermute x77, starting transfers between devices, swap(): lax.ppermute(values, axis, [(i, i ^ bit) for i in range(lax.axis_size(axi...  52.4 us
    pallas_call x3, Pallas kernels, product_first(): pl.pallas_call(first_kernel, out_shape=jax.ShapeDtypeStruct((depth, colum...  41.8 us
    pallas_call x3, Pallas kernels, rows_call(): pl.pallas_call(functools.partial(rows_kernel, finish, len(pieces), len(we...  39.3 us
    pallas_call x4, Pallas kernels, part_call(): pl.pallas_call(part_kernel, out_shape=(jax.ShapeDtypeStruct((rows, column...  28.9 us
    pallas_call x4, Pallas kernels, near_call(): pl.pallas_call(near_kernel, out_shape=jax.ShapeDtypeStruct((3 * rows, col...  27.5 us
    pallas_call x4, Pallas kernels, cross_call(): pl.pallas_call(cross_kernel, out_shape=(jax.ShapeDtypeStruct(shape, jnp.f...  23.9 us
    pallas_call x1, Pallas kernels, attend_backward(): pl.pallas_call(functools.partial(backward_kernel, rows, blocks, heads), o...  22.3 us
  transfers between devices with their start and end apart: 83, of which 40 were waited for; matrix products, arithmetic and copies ran while one was open for 11% of the time, Pallas kernels for 42%

profile of v5, /device:TPU:0, one launch (start us, length us, event | category | flops | bytes accessed | tf_op | source)
XLA Modules:
  0.0 593.0 jit_solution(14915431179932279472)
XLA Ops:
  13.3 8.8 %collective-permute-done.9 = bf16[256,768]{1,0:T(8,128)(2,1)S(1)} collective-permute-done((bf16[256,768]{1,0:T(8,128)(2,1)S(1)}, bf16[256,768]{1,0:T(8,128)(2,1)S(1)}, u32[]{:S(2)}, u32[]{:S(2)}) %collective-permute-start.9) | collective-permute-done | bytes 393248 | tf_op jit(solution)/shard_map/ppermute | solution.py:40
  41.2 10.6 %collective-permute-done.2 = s32[1]{0:T(128)} collective-permute-done((s32[1]{0:T(128)}, s32[1]{0:T(128)}, u32[]{:S(2)}, u32[]{:S(2)}) %collective-permute-start.2) | collective-permute-done | bytes 36 | tf_op jit(solution)/shard_map/ppermute | solution.py:40
  55.1 23.6 %collective-permute-done.4 = bf16[256,2304]{1,0:T(8,128)(2,1)S(1)} collective-permute-done((bf16[256,2304]{1,0:T(8,128)(2,1)S(1)}, bf16[256,2304]{1,0:T(8,128)(2,1)S(1)}, u32[]{:S(2)}, u32[]{:S(2)}) %collective-permute-start.4) | collective-permute-done | bytes 1179680 | tf_op jit(solution)/shard_map/ppermute | solution.py:40
  91.3 10.3 %query_key_value.1 = (f32[8,256,512]{2,1,0:T(8,128)}, bf16[8,256,2048]{2,1,0:T(8,128)(2,1)}) custom-call(bf16[256,2048]{1,0:T(8,128)(2,1)} %fusion.4.refs_0_, bf16[256,2048]{1,0:T(8,128)(2,1)} %collective-permute-done.refs_1_, bf16[256,2048]{1,0:T(8,128)(2,1)} %collective-permute-done.1.refs_2_, bf16[256,2048]{1,0:T(8,128)(2,1)} %copy-done.22, ...), custom_call_target="tpu_custom_call" | custom-call | flops 1024 | bytes 1024 | tf_op jit(solution)/shard_map/query_key_value/pallas_call | solution.py:386
  101.6 10.9 %attend_forward.1 = bf16[2,2,2,256,256]{4,3,2,1,0:T(8,128)(2,1)} custom-call(s32[3]{0:T(128)} %pad_add_fusion.meta, f32[2,2,2,256,512]{4,3,2,1,0:T(8,128)} %bitcast.86, f32[2,128]{1,0:T(2,128)} %slice_bitcast_fusion.gains, f32[1024,128]{1,0:T(8,128)} %get-tuple-element.200.cos_ref, f32[1024,128]{1,0:T(8,128)} %get-tuple-element.201.sin_ref), custom_call_target="tpu_custom_call" | custom-call | flops 1024 | bytes 1024 | tf_op jit(solution)/shard_map/attend_forward/pallas_call | solution.py:614
  152.0 20.6 %collective-permute-done.18 = bf16[256,2048]{1,0:T(8,128)(2,1)S(1)} collective-permute-done((bf16[256,2048]{1,0:T(8,128)(2,1)}, bf16[256,2048]{1,0:T(8,128)(2,1)S(1)}, u32[]{:S(2)}, u32[]{:S(2)}) %collective-permute-start.18) | collective-permute-done | bytes 1048608 | tf_op jit(solution)/shard_map/attention_out/ppermute | solution.py:40
  179.6 21.7 %collective-permute-done.20.refs_1_ = bf16[256,2048]{1,0:T(8,128)(2,1)S(1)} collective-permute-done((bf16[256,2048]{1,0:T(8,128)(2,1)S(1)}, bf16[256,2048]{1,0:T(8,128)(2,1)S(1)}, u32[]{:S(2)}, u32[]{:S(2)}) %collective-permute-start.20) | collective-permute-done | bytes 1048608 | tf_op jit(solution)/shard_map/norm_two/ppermute | solution.py:40
  204.8 8.0 %collective-permute-done.22.refs_3_ = bf16[128,2048]{1,0:T(8,128)(2,1)S(1)} collective-permute-done((bf16[128,2048]{1,0:T(8,128)(2,1)S(1)}, bf16[128,2048]{1,0:T(8,128)(2,1)S(1)}, u32[]{:S(2)}, u32[]{:S(2)}) %collective-permute-start.22) | collective-permute-done | bytes 524320 | tf_op jit(solution)/shard_map/norm_two/ppermute | solution.py:40
  223.1 20.2 %gate_up.1 = (bf16[8,256,1536]{2,1,0:T(8,128)(2,1)}, bf16[8,256,768]{2,1,0:T(8,128)(2,1)}, bf16[8,256,2048]{2,1,0:T(8,128)(2,1)}) custom-call(bf16[256,2048]{1,0:T(8,128)(2,1)} %copy-done.7, bf16[256,2048]{1,0:T(8,128)(2,1)} %copy-done.11, bf16[256,2048]{1,0:T(8,128)(2,1)} %copy-done.12, bf16[128,2048]{1,0:T(8,128)(2,1)} %copy-done.23, ...), custom_call_target="tpu_custom_call" | custom-call | flops 1024 | bytes 1024 | tf_op jit(solution)/shard_map/gate_up/pallas_call | solution.py:386
  253.0 10.9 %down_weight_grad.1 = bf16[2048,768]{1,0:T(8,128)(2,1)} custom-call(bf16[2048,2048]{1,0:T(8,128)(2,1)} %bitcast.72, bf16[2048,768]{1,0:T(8,128)(2,1)} %bitcast.74), custom_call_target="tpu_custom_call" | custom-call | flops 1024 | bytes 1024 | tf_op jit(solution)/shard_map/down_weight_grad/pallas_call | solution.py:227
  268.1 14.5 %hidden_grad.1.left.refs_1_ = bf16[2048,1536]{1,0:T(8,128)(2,1)} custom-call(bf16[2048,2048]{1,0:T(8,128)(2,1)} %bitcast.73, bf16[2048,768]{1,0:T(8,128)(2,1)} %all-gather.8.cloned.1.call-done.weight.right, bf16[2048,1536]{1,0:T(8,128)(2,1)} %bitcast.90), custom_call_target="tpu_custom_call" | custom-call | flops 1024 | bytes 1024 | tf_op jit(solution)/shard_map/hidden_grad/pallas_call | solution.py:421
  282.7 8.6 %cross.5 = (f32[256,2048]{1,0:T(8,128)}, bf16[256,2048]{1,0:T(8,128)(2,1)}) custom-call(bf16[2048,1536]{1,0:T(8,128)(2,1)} %hidden_grad.1.left.refs_1_, bf16[2048,1536]{1,0:T(8,128)(2,1)} %all-gather.6.cloned.1.call-done.refs_10_.right), custom_call_target="tpu_custom_call" | custom-call | flops 1024 | bytes 1024 | tf_op jit(solution)/shard_map/norm_two_grad/cross/pallas_call | solution.py:79
  291.3 10.5 %part.5 = (bf16[256,2048]{1,0:T(8,128)(2,1)}, bf16[256,2048]{1,0:T(8,128)(2,1)}, bf16[256,2048]{1,0:T(8,128)(2,1)}) custom-call(bf16[2048,1536]{1,0:T(8,128)(2,1)} %hidden_grad.1.left.refs_1_, bf16[2048,1536]{1,0:T(8,128)(2,1)} %all-gather.6.cloned.1.call-done.refs_10_.right), custom_call_target="tpu_custom_call" | custom-call | flops 1024 | bytes 1024 | tf_op jit(solution)/shard_map/norm_two_grad/part/pallas_call | solution.py:130
  309.1 10.0 %near.5.near_chip.near_pair = f32[768,2048]{1,0:T(8,128)} custom-call(bf16[2048,1536]{1,0:T(8,128)(2,1)} %hidden_grad.1.left.refs_1_, bf16[2048,1536]{1,0:T(8,128)(2,1)} %all-gather.6.cloned.1.call-done.refs_10_.right), custom_call_target="tpu_custom_call" | custom-call | flops 1024 | bytes 1024 | tf_op jit(solution)/shard_map/norm_two_grad/near/pallas_call | solution.py:113
  327.9 18.4 %gateup_weight_grad.1 = bf16[2048,1536]{1,0:T(8,128)(2,1)} custom-call(bf16[2048,2048]{1,0:T(8,128)(2,1)} %bitcast.96, bf16[2048,1536]{1,0:T(8,128)(2,1)} %hidden_grad.1.left.refs_1_), custom_call_target="tpu_custom_call" | custom-call | flops 12884901888 | bytes 8388608 | tf_op jit(solution)/shard_map/gateup_weight_grad/pallas_call | solution.py:227
  374.9 7.1 %part.6 = (bf16[256,2048]{1,0:T(8,128)(2,1)}, bf16[256,2048]{1,0:T(8,128)(2,1)}, bf16[256,2048]{1,0:T(8,128)(2,1)}) custom-call(bf16[2048,768]{1,0:T(8,128)(2,1)} %bitcast.77, bf16[2048,768]{1,0:T(8,128)(2,1)} %all-gather.8.cloned.1.call-done.weight.right), custom_call_target="tpu_custom_call" | custom-call | flops 1024 | bytes 1024 | tf_op jit(solution)/shard_map/mlp_out/part/pallas_call | solution.py:130
  389.5 9.3 %collective-permute-done.47.refs_3_ = bf16[128,2048]{1,0:T(8,128)(2,1)S(1)} collective-permute-done((bf16[128,2048]{1,0:T(8,128)(2,1)S(1)}, bf16[128,2048]{1,0:T(8,128)(2,1)S(1)}, u32[]{:S(2)}, u32[]{:S(2)}) %collective-permute-start.47) | collective-permute-done | bytes 524320 | tf_op jit(solution)/shard_map/middle_grad/ppermute | solution.py:40
  406.7 8.8 %context_grad.1 = (bf16[8,256,256]{2,1,0:T(8,128)(2,1)}, bf16[8,256,2048]{2,1,0:T(8,128)(2,1)}) custom-call(bf16[256,2048]{1,0:T(8,128)(2,1)} %get-tuple-element.264.refs_0_, bf16[256,2048]{1,0:T(8,128)(2,1)} %collective-permute-done.45.refs_1_, bf16[256,2048]{1,0:T(8,128)(2,1)} %collective-permute-done.46.refs_2_, bf16[128,2048]{1,0:T(8,128)(2,1)} %copy-done.25, ...), custom_call_target="tpu_custom_call" | custom-call | flops 1024 | bytes 1024 | tf_op jit(solution)/shard_map/context_grad/pallas_call | solution.py:386
  426.0 22.3 %attend_backward.1 = (bf16[2,2,2,256,512]{4,3,2,1,0:T(8,128)(2,1)}, f32[2,2,128]{2,1,0:T(2,128)}) custom-call(s32[3]{0:T(128)} %pad_add_fusion.meta, f32[2,2,2,256,512]{4,3,2,1,0:T(8,128)} %bitcast.87, bf16[2,2,2,256,256]{4,3,2,1,0:T(8,128)(2,1)} %bitcast.92, f32[2,128]{1,0:T(2,128)} %slice_bitcast_fusion.gains, f32[1024,128]{1,0:T(8,128)} %get-tuple-element.200.cos_ref, ...), custom_call_target="tpu_custom_call" | custom-call | flops 1024 | bytes 1024 | tf_op jit(solution)/shard_map/attend_backward/pallas_call | solution.py:645
  449.1 12.4 %attention_weight_grad.1 = bf16[2048,768]{1,0:T(8,128)(2,1)} custom-call(bf16[2048,2048]{1,0:T(8,128)(2,1)} %bitcast.88, bf16[2048,512]{1,0:T(8,128)(2,1)} %bitcast.78, bf16[2048,2048]{1,0:T(8,128)(2,1)} %bitcast.89, bf16[2048,256]{1,0:T(8,128)(2,1)} %bitcast.85), custom_call_target="tpu_custom_call" | custom-call | flops 1024 | bytes 1024 | tf_op jit(solution)/shard_map/attention_weight_grad/pallas_call | solution.py:227
  481.6 7.5 %collective-permute-done.62.other = bf16[256,1536]{1,0:T(8,128)(2,1)} collective-permute-done((bf16[256,1536]{1,0:T(8,128)(2,1)}, bf16[256,1536]{1,0:T(8,128)(2,1)}, u32[]{:S(2)}, u32[]{:S(2)}) %collective-permute-start.62) | collective-permute-done | bytes 786464 | tf_op jit(solution)/shard_map/ppermute | solution.py:40
  514.6 8.4 %reduce-scatter.8.cloned.1.call-done.mine = bf16[512,768]{1,0:T(8,128)(2,1)} async-done(((bf16[2048,768]{1,0:T(8,128)(2,1)}), bf16[512,768]{1,0:T(8,128)(2,1)}) %reduce-scatter.8.cloned.1.call-update) | async-done | bytes 786448 | tf_op jit(solution)/shard_map/reduce_scatter | solution.py:877
  529.7 8.4 %gateup_step.1 = (f32[2,256,1536]{2,1,0:T(8,128)}, f32[2,256,1536]{2,1,0:T(8,128)}, f32[2,256,1536]{2,1,0:T(8,128)}, f32[8,128]{1,0:T(8,128)}) custom-call(s32[1]{0:T(128)} %bitcast.27.meta, bf16[512,1536]{1,0:T(8,128)(2,1)} %reduce-scatter.6.cloned.1.call-done.mine, bf16[256,1536]{1,0:T(8,128)(2,1)} %collective-permute-done.62.other, f32[2,256,1536]{2,1,0:T(8,128)} %one.2, ...), custom_call_target="tpu_custom_call" | custom-call | flops 1024 | bytes 1024 | tf_op jit(solution)/shard_map/gateup_step/pallas_call | solution.py:785
  538.1 8.0 %collective-permute-done.70.other = bf16[256,768]{1,0:T(8,128)(2,1)S(1)} collective-permute-done((bf16[256,768]{1,0:T(8,128)(2,1)}, bf16[256,768]{1,0:T(8,128)(2,1)S(1)}, u32[]{:S(2)}, u32[]{:S(2)}) %collective-permute-start.70) | collective-permute-done | bytes 393248 | tf_op jit(solution)/shard_map/ppermute | solution.py:40
  (359 shorter events, 277.5 us)
Async XLA Ops:
  7.2 81.1 %all-gather.4.cloned.1.call-start = ((), (), s32[]{:S(2)}) async-start(), calls=%async_computation.3 | async-start | bytes 3932160 | tf_op jit(solution)/shard_map/all_gather | solution.py:873
  23.2 199.9 %all-gather.6.cloned.1.call-start = ((), (), s32[]{:S(2)}) async-start(), calls=%async_computation.4 | async-start | bytes 7864320 | tf_op jit(solution)/shard_map/all_gather | solution.py:873
  26.0 27.0 %collective-permute-start = (bf16[256,2048]{1,0:T(8,128)(2,1)}, bf16[256,2048]{1,0:T(8,128)(2,1)}, u32[]{:S(2)}, u32[]{:S(2)}) collective-permute-start(bf16[256,2048]{1,0:T(8,128)(2,1)} %fusion.4.refs_0_), channel_id=1, source_target_pairs={{0,2},{1,3},{2,0},{3,1},{4,6},{5,7},{6,4},{7,5},{8,10},{9,11},{10,... | collective-permute-start | bytes 3145736 | tf_op jit(solution)/shard_map/norm_one/ppermute | solution.py:40
  27.7 25.3 %collective-permute-start.1 = (bf16[256,2048]{1,0:T(8,128)(2,1)}, bf16[256,2048]{1,0:T(8,128)(2,1)}, u32[]{:S(2)}, u32[]{:S(2)}) collective-permute-start(bf16[256,2048]{1,0:T(8,128)(2,1)} %fusion.4.refs_0_), channel_id=1, source_target_pairs={{0,4},{4,0},{1,5},{5,1},{2,6},{6,2},{3,7},{7,3},{8,12},{12,8},{9,1... | collective-permute-start | bytes 3145736 | tf_op jit(solution)/shard_map/norm_one/ppermute | solution.py:40
  53.0 25.6 %collective-permute-start.4 = (bf16[256,2304]{1,0:T(8,128)(2,1)S(1)}, bf16[256,2304]{1,0:T(8,128)(2,1)S(1)}, u32[]{:S(2)}, u32[]{:S(2)}) collective-permute-start(bf16[256,2304]{1,0:T(8,128)(2,1)S(1)} %pad_maximum_fusion.1), channel_id=1, source_target_pairs={{0,4},{4,0},{1,5},{5,1},{2,6},{6,2},{3,7},{7,3},{8,12},{12,8},{9,1... | collective-permute-start | bytes 3538952 | tf_op jit(solution)/shard_map/ppermute | solution.py:40
  54.5 24.7 %collective-permute-start.3 = (bf16[256,2048]{1,0:T(8,128)(2,1)}, bf16[256,2048]{1,0:T(8,128)(2,1)S(1)}, u32[]{:S(2)}, u32[]{:S(2)}) collective-permute-start(bf16[256,2048]{1,0:T(8,128)(2,1)} %collective-permute-done.1.refs_2_), channel_id=1, source_target_pairs={{0,2},{1,3},{2,0},{3,1},{4,6},{5,7},{6,4},{7,5},{8,10},{9,11},{10,... | collective-permute-start | bytes 3145736 | tf_op jit(solution)/shard_map/norm_one/ppermute | solution.py:40
  82.0 185.9 %all-gather.8.cloned.1.call-start = ((), (), s32[]{:S(2)}) async-start(), calls=%async_computation.5 | async-start | bytes 3932160 | tf_op jit(solution)/shard_map/all_gather | solution.py:873
  88.3 25.2 %collective-permute-start.10 = (bf16[256,2048]{1,0:T(8,128)(2,1)}, bf16[256,2048]{1,0:T(8,128)(2,1)}, u32[]{:S(2)}, u32[]{:S(2)}) collective-permute-start(bf16[256,2048]{1,0:T(8,128)(2,1)} %fusion.13.refs_0_), channel_id=1, source_target_pairs={{0,2},{1,3},{2,0},{3,1},{4,6},{5,7},{6,4},{7,5},{8,10},{9,11},{10,... | collective-permute-start | bytes 3145736 | tf_op jit(solution)/shard_map/output_grad/ppermute | solution.py:40
  89.8 24.9 %collective-permute-start.11 = (bf16[256,2048]{1,0:T(8,128)(2,1)}, bf16[256,2048]{1,0:T(8,128)(2,1)}, u32[]{:S(2)}, u32[]{:S(2)}) collective-permute-start(bf16[256,2048]{1,0:T(8,128)(2,1)} %fusion.13.refs_0_), channel_id=1, source_target_pairs={{0,4},{4,0},{1,5},{5,1},{2,6},{6,2},{3,7},{7,3},{8,12},{12,8},{9,1... | collective-permute-start | bytes 3145736 | tf_op jit(solution)/shard_map/output_grad/ppermute | solution.py:40
  148.2 24.4 %collective-permute-start.18 = (bf16[256,2048]{1,0:T(8,128)(2,1)}, bf16[256,2048]{1,0:T(8,128)(2,1)S(1)}, u32[]{:S(2)}, u32[]{:S(2)}) collective-permute-start(bf16[256,2048]{1,0:T(8,128)(2,1)} %get-tuple-element.221), channel_id=1, source_target_pairs={{0,2},{1,3},{2,0},{3,1},{4,6},{5,7},{6,4},{7,5},{8,10},{9,11},{10,... | collective-permute-start | bytes 3145736 | tf_op jit(solution)/shard_map/attention_out/ppermute | solution.py:40
  148.8 24.8 %collective-permute-start.19 = (bf16[256,2048]{1,0:T(8,128)(2,1)}, bf16[256,2048]{1,0:T(8,128)(2,1)}, u32[]{:S(2)}, u32[]{:S(2)}) collective-permute-start(bf16[256,2048]{1,0:T(8,128)(2,1)} %get-tuple-element.222), channel_id=1, source_target_pairs={{0,4},{4,0},{1,5},{5,1},{2,6},{6,2},{3,7},{7,3},{8,12},{12,8},{9,1... | collective-permute-start | bytes 3145736 | tf_op jit(solution)/shard_map/attention_out/ppermute | solution.py:40
  151.5 194.9 %reduce-scatter.4.cloned.1.call-start = ((), (), s32[]{:S(2)}) async-start(), calls=%async_computation.6 | async-start | bytes 3932160 | tf_op jit(solution)/shard_map/reduce_scatter | solution.py:877
  179.6 38.5 %collective-permute-start.24 = (bf16[256,2048]{1,0:T(8,128)(2,1)S(1)}, bf16[256,2048]{1,0:T(8,128)(2,1)S(1)}, u32[]{:S(2)}, u32[]{:S(2)}) collective-permute-start(bf16[256,2048]{1,0:T(8,128)(2,1)S(1)} %multiply_convert_fusion.refs_0_), channel_id=1, source_target_pairs={{0,1},{1,0},{2,3},{3,2},{4,5},{5,4},{6,7},{7,6},{8,9},{9,8},{10,11... | collective-permute-start | bytes 3145736 | tf_op jit(solution)/shard_map/norm_two/ppermute | solution.py:40
  218.1 25.1 %collective-permute-start.29 = (bf16[128,2048]{1,0:T(8,128)(2,1)}, bf16[128,2048]{1,0:T(8,128)(2,1)}, u32[]{:S(2)}, u32[]{:S(2)}) collective-permute-start(bf16[128,2048]{1,0:T(8,128)(2,1)} %slice.112), channel_id=1, source_target_pairs={{0,4},{4,0},{1,5},{5,1},{2,6},{6,2},{3,7},{7,3},{8,12},{12,8},{9,1... | collective-permute-start | bytes 1572872 | tf_op jit(solution)/shard_map/output_grad/ppermute | solution.py:40
  219.0 24.2 %collective-permute-start.30 = (bf16[128,2048]{1,0:T(8,128)(2,1)}, bf16[128,2048]{1,0:T(8,128)(2,1)}, u32[]{:S(2)}, u32[]{:S(2)}) collective-permute-start(bf16[128,2048]{1,0:T(8,128)(2,1)} %slice.113), channel_id=1, source_target_pairs={{0,2},{1,3},{2,0},{3,1},{4,6},{5,7},{6,4},{7,5},{8,10},{9,11},{10,... | collective-permute-start | bytes 1572872 | tf_op jit(solution)/shard_map/output_grad/ppermute | solution.py:40
  267.9 198.8 %reduce-scatter.6.cloned.1.call-start = ((), (), s32[]{:S(2)}) async-start(), calls=%async_computation.7 | async-start | bytes 7864320 | tf_op jit(solution)/shard_map/reduce_scatter | solution.py:877
  325.9 24.3 %collective-permute-start.42 = (bf16[256,2048]{1,0:T(8,128)(2,1)}, bf16[256,2048]{1,0:T(8,128)(2,1)}, u32[]{:S(2)}, u32[]{:S(2)}) collective-permute-start(bf16[256,2048]{1,0:T(8,128)(2,1)} %get-tuple-element.255), channel_id=1, source_target_pairs={{0,2},{1,3},{2,0},{3,1},{4,6},{5,7},{6,4},{7,5},{8,10},{9,11},{10,... | collective-permute-start | bytes 3145736 | tf_op jit(solution)/shard_map/norm_two_grad/ppermute | solution.py:40
  327.4 24.0 %collective-permute-start.43 = (bf16[256,2048]{1,0:T(8,128)(2,1)}, bf16[256,2048]{1,0:T(8,128)(2,1)}, u32[]{:S(2)}, u32[]{:S(2)}) collective-permute-start(bf16[256,2048]{1,0:T(8,128)(2,1)} %get-tuple-element.256), channel_id=1, source_target_pairs={{0,4},{4,0},{1,5},{5,1},{2,6},{6,2},{3,7},{7,3},{8,12},{12,8},{9,1... | collective-permute-start | bytes 3145736 | tf_op jit(solution)/shard_map/norm_two_grad/ppermute | solution.py:40
  351.4 171.6 %reduce-scatter.8.cloned.1.call-start = ((), (), s32[]{:S(2)}) async-start(), calls=%async_computation.8 | async-start | bytes 3932160 | tf_op jit(solution)/shard_map/reduce_scatter | solution.py:877
  423.6 24.7 %collective-permute-start.59 = (bf16[256,2048]{1,0:T(8,128)(2,1)}, bf16[256,2048]{1,0:T(8,128)(2,1)}, u32[]{:S(2)}, u32[]{:S(2)}) collective-permute-start(bf16[256,2048]{1,0:T(8,128)(2,1)} %get-tuple-element.290), channel_id=1, source_target_pairs={{0,2},{1,3},{2,0},{3,1},{4,6},{5,7},{6,4},{7,5},{8,10},{9,11},{10,... | collective-permute-start | bytes 3145736 | tf_op jit(solution)/shard_map/mlp_out/ppermute | solution.py:40
  425.0 24.1 %collective-permute-start.60 = (bf16[256,2048]{1,0:T(8,128)(2,1)}, bf16[256,2048]{1,0:T(8,128)(2,1)}, u32[]{:S(2)}, u32[]{:S(2)}) collective-permute-start(bf16[256,2048]{1,0:T(8,128)(2,1)} %get-tuple-element.291), channel_id=1, source_target_pairs={{0,4},{4,0},{1,5},{5,1},{2,6},{6,2},{3,7},{7,3},{8,12},{12,8},{9,1... | collective-permute-start | bytes 3145736 | tf_op jit(solution)/shard_map/mlp_out/ppermute | solution.py:40
  470.0 24.0 %collective-permute-start.71 = (bf16[256,2048]{1,0:T(8,128)(2,1)}, bf16[256,2048]{1,0:T(8,128)(2,1)}, u32[]{:S(2)}, u32[]{:S(2)}) collective-permute-start(bf16[256,2048]{1,0:T(8,128)(2,1)} %get-tuple-element.318), channel_id=1, source_target_pairs={{0,1},{1,0},{2,3},{3,2},{4,5},{5,4},{6,7},{7,6},{8,9},{9,8},{10,11... | collective-permute-start | bytes 3145736 | tf_op jit(solution)/shard_map/mlp_out/ppermute | solution.py:40
  512.8 33.3 %collective-permute-start.68 = (bf16[256,2048]{1,0:T(8,128)(2,1)}, bf16[256,2048]{1,0:T(8,128)(2,1)}, u32[]{:S(2)}, u32[]{:S(2)}) collective-permute-start(bf16[256,2048]{1,0:T(8,128)(2,1)} %get-tuple-element.309), channel_id=1, source_target_pairs={{0,2},{1,3},{2,0},{3,1},{4,6},{5,7},{6,4},{7,5},{8,10},{9,11},{10,... | collective-permute-start | bytes 3145736 | tf_op jit(solution)/shard_map/norm_one_grad/ppermute | solution.py:40
  513.0 33.0 %collective-permute-start.69 = (bf16[256,2048]{1,0:T(8,128)(2,1)}, bf16[256,2048]{1,0:T(8,128)(2,1)}, u32[]{:S(2)}, u32[]{:S(2)}) collective-permute-start(bf16[256,2048]{1,0:T(8,128)(2,1)} %get-tuple-element.310), channel_id=1, source_target_pairs={{0,4},{4,0},{1,5},{5,1},{2,6},{6,2},{3,7},{7,3},{8,12},{12,8},{9,1... | collective-permute-start | bytes 3145736 | tf_op jit(solution)/shard_map/norm_one_grad/ppermute | solution.py:40
  (109 other events, 1167.2 us)
Sparse Core Ops, SparseCore 0:
  23.3 64.9 all-gather.3
  90.5 113.9 all-gather.5
  206.1 61.7 all-gather.7
  270.6 58.8 reduce-scatter.3
  351.5 107.8 reduce-scatter.5
  462.2 60.7 reduce-scatter.7
